TPU v7x, 32 devices: a whole 2x2x4 slice. The times are simulated.
32 devices in a mesh: group: 4 (over y, core), expert: 8 (over z, x).
Axes of the slice: x: 2, y: 2, z: 4, core: 2. Of those that a mesh axis runs over, the one named last changes fastest.
Arguments:
- tokens: bfloat16 [1024, 2048], P(('group', 'expert')), may hold values from -6 to 6
- out_grad: bfloat16 [1024, 2048], P(('group', 'expert')), may hold values from -6 to 6
- expert_ids: int32 [1024, 4], P(('group', 'expert')), may hold values from 0 to 63, as said below
- gate_w: bfloat16 [1024, 4], P(('group', 'expert')), may hold values from 0.049804688 to 0.59765625
- query_ids: int32 [32, 32], P(('group', 'expert')), may hold values from 0 to 7, never falling along the last dimension, each value on 1 to 8 neighbouring positions
- w_gate: bfloat16 [64, 2048, 512], P(('group', 'expert')), may hold values from -0.125 to 0.125
- w_up: bfloat16 [64, 2048, 512], P(('group', 'expert')), may hold values from -0.125 to 0.125
- w_down: bfloat16 [64, 512, 2048], P(('group', 'expert')), may hold values from -0.25 to 0.25
- proj_out: bfloat16 [64, 2048, 64], P(('group', 'expert')), may hold values from -0.125 to 0.125
- proj_in: bfloat16 [64, 512, 64], P(('group', 'expert')), may hold values from -0.25 to 0.25
- train_grads: bfloat16 [64, 4096, 512], P(('group', 'expert')), may hold values from -0.09375 to 0.09375
Outputs:
- token_grads: bfloat16 [1024, 2048], P(('group', 'expert'))
- scores: float32 [256, 512], P(('group', 'expert'))
Inputs may be any that keep to these rules, and one draw needn't show every extreme that they name: `expert_ids`: each token names 4 different experts, two in each of 2 different groups, a group being 16 consecutive experts. Among the 32 tokens of one block every group is named by exactly 16 tokens and every expert by at most 4 tokens; in every block some expert is named by exactly 4. `query_ids`: along one block's tokens the query number never falls; each of the 8 queries of a block has 1 to 8 tokens, and one has exactly 8.
All inputs are finite; a program needn't handle non-finite values.
Results may differ from a plain program's by a relative error of at most 0.0064.
Values may be sent and summed in bfloat16 or wider, within the bound.
No kernel may reach another device: no remote copies, remote signals or barrier semaphores. Data moves between devices by JAX's collectives and lax.ppermute only.
A program may use at most 128 MiB of HBM per device.

v0:
```python
import jax
import jax.numpy as jnp
from jax import lax
from jax.sharding import PartitionSpec as P

QRY_DEV = 8


def pair_terms(rows_x, rows_g, rows_w, gate_mat, up_mat, down_mat, left_proj, right_proj, stored):
    contract = (((1,), (1,)), ((), ()))
    a_gate = jnp.dot(rows_x, gate_mat, preferred_element_type=jnp.float32)
    a_up = jnp.dot(rows_x, up_mat, preferred_element_type=jnp.float32)
    sigmoid_val = jax.nn.sigmoid(a_gate)
    active = a_gate * sigmoid_val
    hidden = (active * a_up).astype(jnp.bfloat16)
    delta_rows = (rows_w.astype(jnp.float32)[:, None] * rows_g.astype(jnp.float32)).astype(
        jnp.bfloat16
    )
    d_hidden = lax.dot_general(delta_rows, down_mat, contract, preferred_element_type=jnp.float32)
    grad_up = (d_hidden * active).astype(jnp.bfloat16)
    grad_gate = (d_hidden * a_up * sigmoid_val * (1.0 + a_gate * (1.0 - sigmoid_val))).astype(
        jnp.bfloat16
    )
    pair_grad = lax.dot_general(grad_gate, gate_mat, contract, preferred_element_type=jnp.float32)
    pair_grad = pair_grad + lax.dot_general(
        grad_up, up_mat, contract, preferred_element_type=jnp.float32
    )
    left_vec = jnp.dot(delta_rows, left_proj, preferred_element_type=jnp.float32)
    right_vec = jnp.dot(hidden, right_proj, preferred_element_type=jnp.float32)
    outer_prod = (
        (left_vec[:, :, None] * right_vec[:, None, :])
        .reshape(left_vec.shape[0], -1)
        .astype(jnp.bfloat16)
    )
    pair_score = jnp.dot(outer_prod, stored, preferred_element_type=jnp.float32)
    return (pair_grad.astype(jnp.bfloat16), pair_score)


def earlier_same(labels):
    same_label = labels[:, None] == labels[None, :]
    row_iota = lax.broadcasted_iota(jnp.int32, same_label.shape, 0)
    col_iota = lax.broadcasted_iota(jnp.int32, same_label.shape, 1)
    return jnp.sum((same_label & (row_iota > col_iota)).astype(jnp.int32), axis=1)


def pad_rows(values, fill_value):
    extra = jnp.full((1,) + values.shape[1:], fill_value, values.dtype)
    return jnp.concatenate([values, extra], axis=0)


def sum_by_query(values, labels, query_count):
    wanted = lax.iota(jnp.int32, query_count)
    pick_rows = (labels[None, :] == wanted[:, None]).astype(jnp.float32)
    return jnp.dot(
        pick_rows, values, precision=lax.Precision.HIGHEST, preferred_element_type=jnp.float32
    )


def body(
    tokens,
    out_grad,
    expert_ids,
    gate_w,
    query_ids,
    w_gate,
    w_up,
    w_down,
    proj_out,
    proj_in,
    train_grads,
):
    tok_dev, model_width = tokens.shape
    top_count = expert_ids.shape[1]
    experts_here = w_gate.shape[0]
    group_size = lax.axis_size("group")
    expert_size = lax.axis_size("expert")
    exp_group = experts_here * expert_size
    capacity = 2 * tok_dev // exp_group
    query_count = QRY_DEV
    train_count = train_grads.shape[2]
    local_query = query_ids[0]
    flat_experts = expert_ids.reshape(-1)
    pair_ids = jnp.arange(tok_dev * top_count, dtype=jnp.int32)
    pair_token = pair_ids // top_count
    tokens_pad = pad_rows(tokens, 0)
    grads_pad = pad_rows(out_grad, 0)
    weights_pad = pad_rows(gate_w.reshape(-1), 0)
    devices_all = group_size * expert_size
    slot_rank = earlier_same(flat_experts)
    pair_slot = (
        flat_experts // experts_here * (experts_here * capacity)
        + flat_experts % experts_here * capacity
        + slot_rank
    )
    slot_total = devices_all * experts_here * capacity
    slot_pair = jnp.full((slot_total,), tok_dev * top_count, jnp.int32).at[pair_slot].set(pair_ids)
    slot_token = slot_pair // top_count
    shape_out = (devices_all, experts_here, capacity)
    send_rows = tokens_pad[slot_token].reshape(shape_out + (model_width,))
    send_grads = grads_pad[slot_token].reshape(shape_out + (model_width,))
    send_weights = weights_pad[slot_pair].reshape(shape_out)
    rows_x = lax.all_to_all(send_rows, ("group", "expert"), split_axis=0, concat_axis=0, tiled=True)
    rows_g = lax.all_to_all(
        send_grads, ("group", "expert"), split_axis=0, concat_axis=0, tiled=True
    )
    rows_w = lax.all_to_all(
        send_weights, ("group", "expert"), split_axis=0, concat_axis=0, tiled=True
    )
    blocks_in = rows_x.shape[0]
    slot_count = rows_x.shape[2]
    grad_parts = []
    score_parts = []
    for local_idx in range(experts_here):
        grad_rows_one, score_rows_one = pair_terms(
            rows_x[:, local_idx].reshape(-1, model_width),
            rows_g[:, local_idx].reshape(-1, model_width),
            rows_w[:, local_idx].reshape(-1),
            w_gate[local_idx],
            w_up[local_idx],
            w_down[local_idx],
            proj_out[local_idx],
            proj_in[local_idx],
            train_grads[local_idx],
        )
        grad_parts.append(grad_rows_one.reshape(blocks_in, slot_count, model_width))
        score_parts.append(score_rows_one.reshape(blocks_in, slot_count, train_count))
    grad_rows = jnp.stack(grad_parts, axis=1)
    score_rows = jnp.stack(score_parts, axis=1)
    returned = lax.all_to_all(
        grad_rows, ("group", "expert"), split_axis=0, concat_axis=0, tiled=True
    )
    pair_grads = returned.reshape(-1, model_width)[pair_slot]
    score_home = lax.all_to_all(
        score_rows, ("group", "expert"), split_axis=0, concat_axis=0, tiled=True
    )
    pair_scores = score_home.reshape(-1, train_count)[pair_slot]
    scores = sum_by_query(pair_scores, local_query[pair_token], query_count)
    token_grads = jnp.sum(
        pair_grads.reshape(tok_dev, top_count, model_width).astype(jnp.float32), axis=1
    ).astype(jnp.bfloat16)
    return (token_grads, scores)


def solution(mesh):
    return jax.shard_map(
        body,
        mesh=mesh,
        in_specs=(
            P(("group", "expert"), None),
            P(("group", "expert"), None),
            P(("group", "expert"), None),
            P(("group", "expert"), None),
            P(("group", "expert"), None),
            P(("group", "expert"), None, None),
            P(("group", "expert"), None, None),
            P(("group", "expert"), None, None),
            P(("group", "expert"), None, None),
            P(("group", "expert"), None, None),
            P(("group", "expert"), None, None),
        ),
        out_specs=(P(("group", "expert"), None), P(("group", "expert"), None)),
        check_vma=False,
    )
```

profile of v0, /device:TPU:0, one launch (start us, length us, event | category | flops | bytes accessed | tf_op | source)
XLA Modules:
  0.0 158.8 jit_solution(10591262814929262513)
XLA Ops:
  0.6 0.8 copy.86
  1.6 0.8 copy.85
  2.7 1.0 scatter_custom_fusion
  3.8 1.9 %gather_fusion = bf16[256]{0:T(256)(128)(2,1)S(1)} fusion(bf16[129]{0:T(256)(128)(2,1)S(1)} %pad_maximum_fusion.2, s32[1024]{0:T(1024)S(1)} %get-tuple-element.11), kind=kCustom, calls=%fused_computation | custom fusion | bytes 2048 | tf_op jit(solution)/shard_map/gather | solution.py:101
  5.6 0.7 reshape.284
  6.4 7.3 %all-to-all-start = ((bf16[32,2,4]{2,1,0:T(2,128)(2,1)}), bf16[32,2,4]{2,1,0:T(2,128)(2,1)S(1)}, u32[]{:S(2)}, u32[]{:S(2)}) async-start(bf16[32,2,4]{2,1,0:T(2,128)(2,1)} %reshape.284), calls=%async_computation | async-start | bytes 32768 | tf_op jit(solution)/shard_map/all_to_all | solution.py:106
  13.7 0.9 concatenate.11
  14.6 1.4 gather_fusion.2
  16.0 1.2 reshape.286
  17.2 3.5 %all-to-all-done = bf16[32,2,4]{2,1,0:T(2,128)(2,1)S(1)} async-done(((bf16[32,2,4]{2,1,0:T(2,128)(2,1)}), bf16[32,2,4]{2,1,0:T(2,128)(2,1)S(1)}, u32[]{:S(2)}, u32[]{:S(2)}) %all-to-all-start) | async-done | bytes 544 | tf_op jit(solution)/shard_map/all_to_all | solution.py:106
  20.8 2.6 %all-to-all-start.2 = ((bf16[32,2,4,2048]{3,2,1,0:T(4,128)(2,1)}), bf16[32,2,4,2048]{3,2,1,0:T(4,128)(2,1)S(1)}, u32[]{:S(2)}, u32[]{:S(2)}) async-start(bf16[32,2,4,2048]{3,2,1,0:T(4,128)(2,1)} %reshape.286), calls=%async_computation.2 | async-start | bytes 2097152 | tf_op jit(solution)/shard_map/all_to_all | solution.py:102
  23.5 1.4 gather_fusion.1
  24.8 1.2 reshape.285
  26.2 24.6 %all-to-all-done.2 = bf16[32,2,4,2048]{3,2,1,0:T(4,128)(2,1)S(1)} async-done(((bf16[32,2,4,2048]{3,2,1,0:T(4,128)(2,1)}), bf16[32,2,4,2048]{3,2,1,0:T(4,128)(2,1)S(1)}, u32[]{:S(2)}, u32[]{:S(2)}) %all-to-all-start.2) | async-done | bytes 1048608 | tf_op jit(solution)/shard_map/all_to_all | solution.py:102
  50.9 2.8 %all-to-all-start.1 = ((bf16[32,2,4,2048]{3,2,1,0:T(4,128)(2,1)}), bf16[32,2,4,2048]{3,2,1,0:T(4,128)(2,1)S(1)}, u32[]{:S(2)}, u32[]{:S(2)}) async-start(bf16[32,2,4,2048]{3,2,1,0:T(4,128)(2,1)} %reshape.285), calls=%async_computation.1 | async-start | bytes 2097152 | tf_op jit(solution)/shard_map/all_to_all | solution.py:103
  53.9 0.5 fusion.80
  54.7 2.9 %fusion.19 = f32[128,512]{1,0:T(8,128)} fusion(bf16[128,2048]{1,0:T(8,128)(2,1)S(1)} %reshape_squeeze.4, bf16[2,2048,512]{2,1,0:T(8,128)(2,1)} %param.16), kind=kOutput, calls=%fused_computation.30 | convolution fusion | flops 268435456 | bytes 2883584 | tf_op jit(solution)/shard_map/dot_general | solution.py:11
  57.6 3.0 %fusion.22 = f32[128,512]{1,0:T(8,128)} fusion(bf16[128,2048]{1,0:T(8,128)(2,1)S(1)} %reshape_squeeze.4, bf16[2,2048,512]{2,1,0:T(8,128)(2,1)} %param.17), kind=kOutput, calls=%fused_computation.33 | convolution fusion | flops 268435456 | bytes 2883584 | tf_op jit(solution)/shard_map/dot_general | solution.py:12
  60.6 1.2 fusion.10
  61.8 1.1 fusion.13
  62.9 18.1 %all-to-all-done.1 = bf16[32,2,4,2048]{3,2,1,0:T(4,128)(2,1)S(1)} async-done(((bf16[32,2,4,2048]{3,2,1,0:T(4,128)(2,1)}), bf16[32,2,4,2048]{3,2,1,0:T(4,128)(2,1)S(1)}, u32[]{:S(2)}, u32[]{:S(2)}) %all-to-all-start.1) | async-done | bytes 1048608 | tf_op jit(solution)/shard_map/all_to_all | solution.py:103
  81.8 1.4 fusion.46
  83.2 1.3 fusion.44
  84.5 2.6 %fusion.15 = f32[128,512]{1,0:T(8,128)S(1)} fusion(bf16[128,2048]{1,0:T(8,128)(2,1)S(1)} %convert_element_type.113, bf16[2,512,2048]{2,1,0:T(8,128)(2,1)} %param.18), kind=kOutput, calls=%fused_computation.26 | convolution fusion | flops 268435456 | bytes 2883584 | tf_op jit(solution)/shard_map/dot_general | solution.py:19
  87.1 1.1 fusion.53
  88.3 0.8 fusion.8
  89.1 1.6 %fusion.7 = bf16[128,2048]{1,0:T(8,128)(2,1)} fusion(f32[128,2048]{1,0:T(8,128)S(1)} %fusion.8, bf16[2,2048,512]{2,1,0:T(8,128)(2,1)S(1)} %copy-done.9, f32[128,512]{1,0:T(8,128)S(1)} %fusion.15, f32[128,512]{1,0:T(8,128)S(1)} %copy-done.12), kind=kOutput, calls=%fused_computation.18 | convolution fusion | flops 269352960 | bytes 4194304 | tf_op jit(solution)/shard_map/dot_general | solution.py:25
  90.7 1.6 %multiply_convert_fusion = bf16[128,64,64]{2,1,0:T(8,128)(2,1)S(1)} fusion(f32[128,64]{1,0:T(8,128)S(1)} %fusion.53, f32[128,64]{1,0:T(8,128)S(1)} %fusion.44), kind=kLoop, calls=%fused_computation.12 | loop fusion | flops 1048576 | bytes 1114112 | tf_op jit(solution)/shard_map/convert_element_type | solution.py:33
  92.3 1.5 convert_element_type.122
  93.8 1.2 fusion.52
  95.0 1.6 %multiply_convert_fusion.1 = bf16[128,64,64]{2,1,0:T(8,128)(2,1)S(1)} fusion(f32[128,64]{1,0:T(8,128)S(1)} %fusion.52, f32[128,64]{1,0:T(8,128)S(1)} %fusion.46), kind=kLoop, calls=%fused_computation.14 | loop fusion | flops 1048576 | bytes 1114112 | tf_op jit(solution)/shard_map/convert_element_type | solution.py:33
  96.7 2.2 %convert_element_type.119 = bf16[32,4,4096]{2,1,0:T(4,128)(2,1)} reshape(bf16[128,64,64]{2,1,0:T(8,128)(2,1)S(1)} %multiply_convert_fusion.1) | data formatting | bytes 2097152 | tf_op jit(solution)/shard_map/convert_element_type | solution.py:33
  98.9 3.5 %fusion.39 = f32[32,1,4,512]{3,0,2,1:T(8,128)S(1)} fusion(bf16[2,4096,512]{2,1,0:T(8,128)(2,1)} %param.21, bf16[32,4,4096]{2,1,0:T(4,128)(2,1)S(1)} %convert_element_type.122), kind=kOutput, calls=%fused_computation.48 | convolution fusion | flops 536870912 | bytes 5505024 | tf_op jit(solution)/shard_map/dot_general | solution.py:35
  102.4 3.4 %fusion.36 = f32[32,1,4,512]{3,0,2,1:T(8,128)S(1)} fusion(bf16[2,4096,512]{2,1,0:T(8,128)(2,1)} %param.21, bf16[32,4,4096]{2,1,0:T(4,128)(2,1)S(1)} %copy-done.1), kind=kOutput, calls=%fused_computation.47 | convolution fusion | flops 536870912 | bytes 5505024 | tf_op jit(solution)/shard_map/dot_general | solution.py:35
  105.9 1.1 copy.100
  107.1 2.8 %all-to-all-start.4 = ((f32[32,2,4,512]{3,2,1,0:T(4,128)}), f32[32,2,4,512]{3,2,1,0:T(4,128)S(1)}, u32[]{:S(2)}, u32[]{:S(2)}) async-start(f32[32,2,4,512]{3,2,1,0:T(4,128)} %copy.100), calls=%async_computation.4 | async-start | bytes 1048576 | tf_op jit(solution)/shard_map/all_to_all | solution.py:133
  109.9 2.4 %fusion.24 = f32[128,512]{1,0:T(8,128)S(1)} fusion(bf16[128,2048]{1,0:T(8,128)(2,1)S(1)} %copy-done.3, bf16[2,512,2048]{2,1,0:T(8,128)(2,1)} %param.18), kind=kOutput, calls=%fused_computation.35 | convolution fusion | flops 268435456 | bytes 2883584 | tf_op jit(solution)/shard_map/dot_general | solution.py:19
  112.6 2.4 %fusion.17 = f32[128,2048]{1,0:T(8,128)S(1)} fusion(bf16[2,2048,512]{2,1,0:T(8,128)(2,1)} %param.16, f32[128,512]{1,0:T(8,128)S(1)} %copy-done.11, f32[128,512]{1,0:T(8,128)S(1)} %fusion.24, f32[128,512]{1,0:T(8,128)S(1)} %copy-done.13), kind=kOutput, calls=%fused_computation.28 | convolution fusion | flops 269090816 | bytes 3932160 | tf_op jit(solution)/shard_map/dot_general | solution.py:24
  115.0 2.4 %fusion.6 = bf16[128,2048]{1,0:T(8,128)(2,1)S(1)} fusion(f32[128,2048]{1,0:T(8,128)S(1)} %fusion.17, bf16[2,2048,512]{2,1,0:T(8,128)(2,1)} %param.17, f32[128,512]{1,0:T(8,128)S(1)} %fusion.24, f32[128,512]{1,0:T(8,128)S(1)} %copy-done.11), kind=kOutput, calls=%fused_computation.17 | convolution fusion | flops 269352960 | bytes 4194304 | tf_op jit(solution)/shard_map/dot_general | solution.py:25
  117.6 1.7 %pad_maximum_fusion = bf16[32,2,4,2048]{3,2,1,0:T(4,128)(2,1)} fusion(bf16[32,1,4,2048]{3,2,1,0:T(4,128)(2,1)S(1)} %bitcast.82, bf16[32,1,4,2048]{3,2,1,0:T(4,128)(2,1)S(1)} %bitcast.83), kind=kLoop, calls=%fused_computation.49 | loop fusion | flops 524288 | bytes 2097152 | tf_op jit(solution)/shard_map/stack | solution.py:127
  119.3 6.6 %all-to-all-done.4 = f32[32,2,4,512]{3,2,1,0:T(4,128)S(1)} async-done(((f32[32,2,4,512]{3,2,1,0:T(4,128)}), f32[32,2,4,512]{3,2,1,0:T(4,128)S(1)}, u32[]{:S(2)}, u32[]{:S(2)}) %all-to-all-start.4) | async-done | bytes 524320 | tf_op jit(solution)/shard_map/all_to_all | solution.py:133
  125.9 2.6 %all-to-all-start.3 = ((bf16[32,2,4,2048]{3,2,1,0:T(4,128)(2,1)}), bf16[32,2,4,2048]{3,2,1,0:T(4,128)(2,1)S(1)}, u32[]{:S(2)}, u32[]{:S(2)}) async-start(bf16[32,2,4,2048]{3,2,1,0:T(4,128)(2,1)} %pad_maximum_fusion), calls=%async_computation.3 | async-start | bytes 2097152 | tf_op jit(solution)/shard_map/all_to_all | solution.py:129
  128.6 1.2 gather_fusion.4
  130.0 0.8 gather_fusion.5
  130.8 0.8 fusion.65
  131.6 24.4 %all-to-all-done.3 = bf16[32,2,4,2048]{3,2,1,0:T(4,128)(2,1)S(1)} async-done(((bf16[32,2,4,2048]{3,2,1,0:T(4,128)(2,1)}), bf16[32,2,4,2048]{3,2,1,0:T(4,128)(2,1)S(1)}, u32[]{:S(2)}, u32[]{:S(2)}) %all-to-all-start.3) | async-done | bytes 1048608 | tf_op jit(solution)/shard_map/all_to_all | solution.py:129
  156.3 0.9 gather_fusion.3
  157.4 1.4 reduce_sum.25
  (63 shorter events, 3.1 us)
Async XLA Ops:
  0.6 128.0 %copy-start = (s32[1,32]{1,0:T(1,128)S(1)}, s32[1,32]{1,0:T(1,128)}, u32[]{:S(2)}) copy-start(s32[1,32]{1,0:T(1,128)} %param.15) | copy-start | bytes 388
  6.4 14.4 %all-to-all-start = ((bf16[32,2,4]{2,1,0:T(2,128)(2,1)}), bf16[32,2,4]{2,1,0:T(2,128)(2,1)S(1)}, u32[]{:S(2)}, u32[]{:S(2)}) async-start(bf16[32,2,4]{2,1,0:T(2,128)(2,1)} %reshape.284), calls=%async_computation | async-start | bytes 32768 | tf_op jit(solution)/shard_map/all_to_all | solution.py:106
  16.0 7.4 %copy-start.5 = (bf16[32,2048]{1,0:T(8,128)(2,1)S(1)}, bf16[32,2048]{1,0:T(8,128)(2,1)}, u32[]{:S(2)}) copy-start(bf16[32,2048]{1,0:T(8,128)(2,1)} %param.12) | copy-start | bytes 393220
  20.8 30.1 %all-to-all-start.2 = ((bf16[32,2,4,2048]{3,2,1,0:T(4,128)(2,1)}), bf16[32,2,4,2048]{3,2,1,0:T(4,128)(2,1)S(1)}, u32[]{:S(2)}, u32[]{:S(2)}) async-start(bf16[32,2,4,2048]{3,2,1,0:T(4,128)(2,1)} %reshape.286), calls=%async_computation.2 | async-start | bytes 2097152 | tf_op jit(solution)/shard_map/all_to_all | solution.py:102
  50.9 30.1 %all-to-all-start.1 = ((bf16[32,2,4,2048]{3,2,1,0:T(4,128)(2,1)}), bf16[32,2,4,2048]{3,2,1,0:T(4,128)(2,1)S(1)}, u32[]{:S(2)}, u32[]{:S(2)}) async-start(bf16[32,2,4,2048]{3,2,1,0:T(4,128)(2,1)} %reshape.285), calls=%async_computation.1 | async-start | bytes 2097152 | tf_op jit(solution)/shard_map/all_to_all | solution.py:103
  54.7 5.9 %copy-start.6 = (bf16[2,2048,512]{2,1,0:T(8,128)(2,1)S(1)}, bf16[2,2048,512]{2,1,0:T(8,128)(2,1)}, u32[]{:S(2)}) copy-start(bf16[2,2048,512]{2,1,0:T(8,128)(2,1)} %param.16) | copy-start | bytes 12582916
  54.7 7.1 %copy-start.8 = (bf16[2,2048,512]{2,1,0:T(8,128)(2,1)S(1)}, bf16[2,2048,512]{2,1,0:T(8,128)(2,1)}, u32[]{:S(2)}) copy-start(bf16[2,2048,512]{2,1,0:T(8,128)(2,1)} %param.17) | copy-start | bytes 12582916
  62.9 24.2 %copy-start.10 = (bf16[2,512,64]{1,2,0:T(8,128)(2,1)S(1)}, bf16[2,512,64]{1,2,0:T(8,128)(2,1)}, u32[]{:S(2)}) copy-start(bf16[2,512,64]{1,2,0:T(8,128)(2,1)} %param.20) | copy-start | bytes 393220
  81.5 5.6 %copy-start.14 = (f32[128,512]{1,0:T(8,128)S(1)}, f32[128,512]{1,0:T(8,128)}, u32[]{:S(2)}) copy-start(f32[128,512]{1,0:T(8,128)} %fusion.13) | copy-start | bytes 786436
  81.5 6.8 %copy-start.12 = (f32[128,512]{1,0:T(8,128)S(1)}, f32[128,512]{1,0:T(8,128)}, u32[]{:S(2)}) copy-start(f32[128,512]{1,0:T(8,128)} %fusion.10) | copy-start | bytes 786436
  81.6 7.5 %copy-start.2 = (bf16[128,2048]{1,0:T(8,128)(2,1)}, bf16[128,2048]{1,0:T(8,128)(2,1)S(1)}, u32[]{:S(2)}) copy-start(bf16[128,2048]{1,0:T(8,128)(2,1)S(1)} %convert_element_type.105) | copy-start | bytes 1572868
  81.7 6.6 %copy-start.15 = (f32[128,512]{1,0:T(8,128)S(1)}, f32[128,512]{1,0:T(8,128)}, u32[]{:S(2)}) copy-start(f32[128,512]{1,0:T(8,128)} %fusion.13) | copy-start | bytes 786436
  81.8 6.5 %copy-start.7 = (bf16[2,2048,512]{2,1,0:T(8,128)(2,1)S(1)}, bf16[2,2048,512]{2,1,0:T(8,128)(2,1)}, u32[]{:S(2)}) copy-start(bf16[2,2048,512]{2,1,0:T(8,128)(2,1)} %param.16) | copy-start | bytes 12582916
  84.5 4.6 %copy-start.9 = (bf16[2,2048,512]{2,1,0:T(8,128)(2,1)S(1)}, bf16[2,2048,512]{2,1,0:T(8,128)(2,1)}, u32[]{:S(2)}) copy-start(bf16[2,2048,512]{2,1,0:T(8,128)(2,1)} %param.17) | copy-start | bytes 12582916
  98.9 3.5 %copy-start.1 = (bf16[32,4,4096]{2,1,0:T(4,128)(2,1)S(1)}, bf16[32,4,4096]{2,1,0:T(4,128)(2,1)}, u32[]{:S(2)}) copy-start(bf16[32,4,4096]{2,1,0:T(4,128)(2,1)} %convert_element_type.119) | copy-start | bytes 3145732
  102.4 7.5 %copy-start.3 = (bf16[128,2048]{1,0:T(8,128)(2,1)S(1)}, bf16[128,2048]{1,0:T(8,128)(2,1)}, u32[]{:S(2)}) copy-start(bf16[128,2048]{1,0:T(8,128)(2,1)} %copy-done.2) | copy-start | bytes 1572868
  105.8 6.5 %copy-start.4 = (bf16[128,2048]{1,0:T(8,128)(2,1)S(1)}, bf16[128,2048]{1,0:T(8,128)(2,1)}, u32[]{:S(2)}) copy-start(bf16[128,2048]{1,0:T(8,128)(2,1)} %fusion.7) | copy-start | bytes 1572868
  105.9 6.7 %copy-start.11 = (f32[128,512]{1,0:T(8,128)S(1)}, f32[128,512]{1,0:T(8,128)}, u32[]{:S(2)}) copy-start(f32[128,512]{1,0:T(8,128)} %fusion.19) | copy-start | bytes 786436
  105.9 6.7 %copy-start.13 = (f32[128,512]{1,0:T(8,128)S(1)}, f32[128,512]{1,0:T(8,128)}, u32[]{:S(2)}) copy-start(f32[128,512]{1,0:T(8,128)} %fusion.22) | copy-start | bytes 786436
  107.1 18.8 %all-to-all-start.4 = ((f32[32,2,4,512]{3,2,1,0:T(4,128)}), f32[32,2,4,512]{3,2,1,0:T(4,128)S(1)}, u32[]{:S(2)}, u32[]{:S(2)}) async-start(f32[32,2,4,512]{3,2,1,0:T(4,128)} %copy.100), calls=%async_computation.4 | async-start | bytes 1048576 | tf_op jit(solution)/shard_map/all_to_all | solution.py:133
  125.9 30.1 %all-to-all-start.3 = ((bf16[32,2,4,2048]{3,2,1,0:T(4,128)(2,1)}), bf16[32,2,4,2048]{3,2,1,0:T(4,128)(2,1)S(1)}, u32[]{:S(2)}, u32[]{:S(2)}) async-start(bf16[32,2,4,2048]{3,2,1,0:T(4,128)(2,1)} %pad_maximum_fusion), calls=%async_computation.3 | async-start | bytes 2097152 | tf_op jit(solution)/shard_map/all_to_all | solution.py:129
where the time goes:
time: 159 us
  waiting for transfers between devices  77.3 us (49%)
  matrix products  33.2 us (21%)
  local copies, waits for them, and re-layouts  21.8 us (14%)
  starting transfers between devices  18.3 us (12%)
  other arithmetic  7.03 us (4%)
    all_to_all x1, waiting for transfers between devices, body(): lax.all_to_all(send_rows, ('group', 'expert'), split_axis=0, concat_axis=...  24.6 us
    all_to_all x1, waiting for transfers between devices, body(): lax.all_to_all(grad_rows, ('group', 'expert'), split_axis=0, concat_axis=...  24.4 us
    all_to_all x1, waiting for transfers between devices, body(): lax.all_to_all(send_grads, ('group', 'expert'), split_axis=0, concat_axis...  18.1 us
    all_to_all x1, starting transfers between devices, body(): lax.all_to_all(send_weights, ('group', 'expert'), split_axis=0, concat_ax...  7.33 us
    dot_general x2, matrix products, pair_terms(): pair_score = jnp.dot(outer_prod, stored, preferred_element_type=jnp.float32)  6.91 us
    all_to_all x1, waiting for transfers between devices, body(): lax.all_to_all(score_rows, ('group', 'expert'), split_axis=0, concat_axis...  6.63 us
    dot_general x2, matrix products, pair_terms(): lax.dot_general(delta_rows, down_mat, contract, preferred_element_type=jn...  5.01 us
    dot_general x2, matrix products, pair_terms(): a_up = jnp.dot(rows_x, up_mat, preferred_element_type=jnp.float32)  4.14 us
  transfers between devices with their start and end apart: 5, of which 5 were waited for; matrix products, arithmetic and copies ran while one was open for 17% of the time, Pallas kernels for 0%

commit v1 on v0

v1 whole, which is shorter than its diff:
```python
import functools

import jax
import jax.numpy as jnp
from jax import lax
from jax.experimental import pallas as pl
from jax.experimental.pallas import tpu as pltpu
from jax.sharding import Mesh, PartitionSpec as P

QRY_DEV = 8
HALVES = 2
LANES = 128
F32 = jnp.float32
BF16 = jnp.bfloat16
NT = (((1,), (1,)), ((), ()))


def dot(a, b):
    return jnp.dot(a, b, preferred_element_type=F32)


def slot_masks(meta, half, sizes):
    tok, top, rows, span, capacity = sizes
    shape = (tok, rows)
    slot = lax.broadcasted_iota(jnp.int32, shape, 1)
    rank = (slot % capacity).astype(F32)
    expert = (slot // (span * capacity)) * (HALVES * span) + half * span + slot // capacity % span
    expert = expert.astype(F32)
    named = jnp.zeros(shape, F32)
    weight = jnp.zeros(shape, F32)
    for k in range(top):
        hit = jnp.where(meta[:, k : k + 1] == expert, 1.0, 0.0)
        named = named + hit
        weight = weight + hit * meta[:, top + k : top + k + 1]
    row = lax.broadcasted_iota(jnp.int32, (tok, tok), 0)
    col = lax.broadcasted_iota(jnp.int32, (tok, tok), 1)
    earlier = dot(jnp.where(col < row, 1.0, 0.0).astype(BF16), named.astype(BF16))
    place = jnp.where(earlier == rank, named, 0.0)
    return place, place * weight


def fill_slots(place, weighted, x, g, send_ref, place_ref):
    width = x.shape[1]
    place_ref[...] = place.astype(BF16)
    pick = place.T.astype(BF16)
    scale = jnp.sum(weighted.T, axis=1, keepdims=True)
    send_ref[:, :width] = dot(pick, x).astype(BF16)
    send_ref[:, width:] = (scale * dot(pick, g)).astype(BF16)


def own_kernel(sizes, half_ref, ids_ref, w_ref, x_ref, g_ref, pay_ref, send_ref, place_ref):
    tok, top = sizes[:2]
    width = x_ref.shape[1]
    flat = jnp.concatenate([ids_ref[...].astype(F32), w_ref[...].astype(F32)], axis=0)
    flat = jnp.concatenate([flat, jnp.zeros((LANES - 2 * top, tok), F32)], axis=0)
    flat = jnp.concatenate([flat, jnp.zeros((LANES, LANES - tok), F32)], axis=1)
    meta = flat.T[:tok, :]
    pay_ref[:, :width] = x_ref[...]
    pay_ref[:, width : 2 * width] = g_ref[...]
    pay_ref[:, 2 * width :] = meta.astype(BF16)
    place, weighted = slot_masks(meta, half_ref[0], sizes)
    fill_slots(place, weighted, x_ref[...], g_ref[...], send_ref, place_ref)


def guest_kernel(sizes, half_ref, pay_ref, send_ref, place_ref):
    width = send_ref.shape[1] // 2
    meta = pay_ref[:, 2 * width :].astype(F32)
    place, weighted = slot_masks(meta, half_ref[0], sizes)
    fill_slots(
        place, weighted, pay_ref[:, :width], pay_ref[:, width : 2 * width], send_ref, place_ref
    )


def expert_kernel(capacity, rows_ref, *refs):
    hbm, out_ref, vmem, outer_ref, sem = refs[:6], refs[6], refs[7:13], refs[13], refs[14]
    experts, width, hidden_width = hbm[0].shape
    rank = hbm[3].shape[2]
    rows = rows_ref.shape[0]
    order = (0, 1, 2, 3, 4, 5)

    def copy(i, j):
        return pltpu.make_async_copy(hbm[i].at[j], vmem[i].at[j], sem.at[i, j])

    for j in range(experts):
        for i in (0, 1, 2, 3, 4):
            copy(i, j).start()
    for j in range(experts):
        copy(5, j).start()
    gate, up, down, left_proj, right_proj, stored = vmem
    x = rows_ref[:, :width]
    delta = rows_ref[:, width:]
    owner = lax.broadcasted_iota(jnp.int32, (rows, 1), 0) // capacity % experts
    left = jnp.zeros((rows, rank), F32)
    right = jnp.zeros((rows, rank), F32)
    grad = jnp.zeros((rows, width), F32)
    for j in range(experts):
        mine = owner == j
        copy(0, j).wait()
        a_gate = dot(x, gate[j])
        copy(1, j).wait()
        a_up = dot(x, up[j])
        copy(2, j).wait()
        d_hidden = lax.dot_general(delta, down[j], NT, preferred_element_type=F32)
        sig = jax.nn.sigmoid(a_gate)
        active = a_gate * sig
        hidden = (active * a_up).astype(BF16)
        grad_up = jnp.where(mine, d_hidden * active, 0.0).astype(BF16)
        grad_gate = jnp.where(
            mine, d_hidden * a_up * sig * (1.0 + a_gate * (1.0 - sig)), 0.0
        ).astype(BF16)
        grad = grad + lax.dot_general(grad_gate, gate[j], NT, preferred_element_type=F32)
        grad = grad + lax.dot_general(grad_up, up[j], NT, preferred_element_type=F32)
        copy(3, j).wait()
        left = jnp.where(mine, dot(delta, left_proj[j]), left)
        copy(4, j).wait()
        right = jnp.where(mine, dot(hidden, right_proj[j]), right)
    out_ref[:, :width] = grad.astype(BF16)
    per = LANES // rank
    wide = jnp.concatenate([right] * per, axis=1)
    lane = lax.broadcasted_iota(jnp.int32, (rows, LANES), 1) // rank
    for c in range(rank // per):
        factor = left[:, c * per : c * per + 1]
        for k in range(1, per):
            factor = jnp.where(lane == k, left[:, c * per + k : c * per + k + 1], factor)
        outer = factor * wide
        for j in range(experts):
            outer_ref[j, :, c * LANES : (c + 1) * LANES] = jnp.where(owner == j, outer, 0.0).astype(
                BF16
            )
    score = jnp.zeros((rows, stored.shape[2]), F32)
    for j in range(experts):
        copy(5, j).wait()
        score = score + dot(outer_ref[j], stored[j])
    out_ref[:, width:] = score.astype(BF16)


def part_kernel(place_ref, rows_ref, out_ref):
    out_ref[...] = dot(place_ref[...], rows_ref[...]).astype(BF16)


def final_kernel(place_ref, rows_ref, part_ref, query_ref, grad_ref, score_ref):
    width = grad_ref.shape[1]
    total = dot(place_ref[...], rows_ref[...]) + part_ref[...].astype(F32)
    grad_ref[...] = total[:, :width].astype(BF16)
    wanted = lax.broadcasted_iota(jnp.int32, (score_ref.shape[0], query_ref.shape[1]), 0)
    pick = jnp.where(query_ref[...] == wanted, 1.0, 0.0)
    score_ref[...] = jnp.dot(
        pick, total[:, width:], precision=lax.Precision.HIGHEST, preferred_element_type=F32
    )


VMEM = pl.BlockSpec(memory_space=pltpu.VMEM)
SMEM = pl.BlockSpec(memory_space=pltpu.SMEM)
ANY = pl.BlockSpec(memory_space=pl.ANY)


def call(kernel, outs, in_specs, args, scratch=(), flops=1_000_000, moved=1_000_000, limit=None):
    return pl.pallas_call(
        kernel,
        out_shape=outs,
        in_specs=in_specs,
        out_specs=jax.tree.map(lambda _: VMEM, outs),
        scratch_shapes=scratch,
        compiler_params=pltpu.CompilerParams(vmem_limit_bytes=limit),
        cost_estimate=pl.CostEstimate(flops=flops, bytes_accessed=moved, transcendentals=0),
    )(*args)


def body(tokens, out_grad, expert_ids, gate_w, query_ids, *weights):
    tok, width = tokens.shape
    top = expert_ids.shape[1]
    experts, _, hidden_width = weights[0].shape
    train = weights[5].shape[2]
    groups, depth = lax.axis_size("group"), lax.axis_size("deep")
    capacity = 2 * tok // (experts * HALVES * depth)
    span = experts * depth
    rows = groups * span * capacity
    sizes = (tok, top, rows, span, capacity)
    half = lax.axis_index("half").reshape(1)
    cube = ("group", "deep")
    send_type = jax.ShapeDtypeStruct((rows, 2 * width), BF16)
    place_type = jax.ShapeDtypeStruct((tok, rows), BF16)
    pay_type = jax.ShapeDtypeStruct((tok, 2 * width + LANES), BF16)
    pay, own_send, own_place = call(
        functools.partial(own_kernel, sizes),
        (pay_type, send_type, place_type),
        [SMEM, VMEM, VMEM, VMEM, VMEM],
        (half, expert_ids.T, gate_w.T, tokens, out_grad),
    )
    swap = [(0, 1), (1, 0)]
    guest = lax.ppermute(pay, "half", swap)
    own_rows = lax.all_to_all(own_send, cube, 0, 0, tiled=True)
    guest_send, guest_place = call(
        functools.partial(guest_kernel, sizes), (send_type, place_type), [SMEM, VMEM], (half, guest)
    )
    guest_rows = lax.all_to_all(guest_send, cube, 0, 0, tiled=True)
    out_type = jax.ShapeDtypeStruct((rows, width + train), BF16)
    scratch = [pltpu.VMEM(w.shape, w.dtype) for w in weights]
    scratch += [
        pltpu.VMEM((experts, rows, weights[5].shape[1]), BF16),
        pltpu.SemaphoreType.DMA((len(weights), experts)),
    ]
    moved = sum(w.size * 2 for w in weights)
    compute = functools.partial(
        call,
        functools.partial(expert_kernel, capacity),
        out_type,
        [VMEM] + [ANY] * len(weights),
        scratch=scratch,
        flops=2 * rows * moved,
        moved=moved,
        limit=48 << 20,
    )
    own_out = compute((own_rows,) + weights)
    guest_out = compute((guest_rows,) + weights)
    guest_home = lax.all_to_all(guest_out, cube, 0, 0, tiled=True)
    part = call(
        part_kernel,
        jax.ShapeDtypeStruct((tok, width + train), BF16),
        [VMEM, VMEM],
        (guest_place, guest_home),
    )
    part = lax.ppermute(part, "half", swap)
    own_home = lax.all_to_all(own_out, cube, 0, 0, tiled=True)
    return call(
        final_kernel,
        (
            jax.ShapeDtypeStruct((tok, width), BF16),
            jax.ShapeDtypeStruct((QRY_DEV, train), F32),
        ),
        [VMEM, VMEM, VMEM, VMEM],
        (own_place, own_home, part, query_ids),
    )


def solution(mesh):
    groups, line = mesh.shape["group"], mesh.shape["expert"]
    devices = mesh.devices.reshape(groups, HALVES, line // HALVES)
    split = Mesh(devices, ("group", "half", "deep"))
    spread = ("group", "half", "deep")
    return jax.shard_map(
        body,
        mesh=split,
        in_specs=(P(spread, None),) * 5 + (P(spread, None, None),) * 6,
        out_specs=(P(spread, None), P(spread, None)),
        check_vma=False,
    )
```

time: 159 us -> 101 us (0.64)
  waiting for transfers between devices: 77.3 us -> 21.5 us
  Pallas kernels: 0 us -> 34.2 us
  matrix products: 33.2 us -> 0 us
  blocking collectives: 0 us -> 19 us
  local copies, waits for them, and re-layouts: 21.8 us -> 4.17 us
  other arithmetic: 7.03 us -> 0 us
  starting transfers between devices: 18.3 us -> 21 us
    all_to_all x5 -> x3, waiting for transfers between devices: 77.3 us -> 9 us  [the longest x1 8.83 us: body(): own_home = lax.all_to_all(own_out, cube, 0, 0, tiled=True)]
    pallas_call x0 -> x6, Pallas kernels: none -> 34.2 us  [call(): pl.pallas_call(kernel, out_shape=outs, in_specs=in_specs, out_specs=jax.t...]
    dot_general x17 -> x0, matrix products: 33.2 us -> none  [the longest x2 6.91 us: pair_terms(): pair_score = jnp.dot(outer_prod, stored, preferred_element_type=jnp.float32)]
    all_to_all x0 -> x1, blocking collectives: none -> 19 us  [body(): guest_rows = lax.all_to_all(guest_send, cube, 0, 0, tiled=True)]
    ppermute x0 -> x2, waiting for transfers between devices: none -> 12.5 us  [the longest x1 12.5 us: body(): guest = lax.ppermute(pay, 'half', swap)]
    gather x6 -> x0, local copies, waits for them, and re-layouts: 7.51 us -> none  [the longest x1 1.87 us: body(): send_weights = weights_pad[slot_pair].reshape(shape_out)]
    ppermute x0 -> x2, starting transfers between devices: none -> 7.32 us  [the longest x1 4.06 us: body(): guest = lax.ppermute(pay, 'half', swap)]
    all_to_all x5 -> x3, starting transfers between devices: 18.3 us -> 13.7 us  [the longest x1 5.11 us: body(): own_home = lax.all_to_all(own_out, cube, 0, 0, tiled=True)]
  transfers between devices with their start and end apart: 5 -> 5, of which waited for: 5 -> 3; matrix products, arithmetic and copies ran while one was open for 17% -> 2% of each run, Pallas kernels for 0% -> 27%
where the time goes in v1:
time: 101 us
  Pallas kernels  34.2 us (34%)
  waiting for transfers between devices  21.5 us (21%)
  starting transfers between devices  21 us (21%)
  blocking collectives  19 us (19%)
  local copies, waits for them, and re-layouts  4.17 us (4%)
    pallas_call x6, Pallas kernels, call(): pl.pallas_call(kernel, out_shape=outs, in_specs=in_specs, out_specs=jax.t...  34.2 us
    all_to_all x1, blocking collectives, body(): guest_rows = lax.all_to_all(guest_send, cube, 0, 0, tiled=True)  19 us
    ppermute x1, waiting for transfers between devices, body(): guest = lax.ppermute(pay, 'half', swap)  12.5 us
    all_to_all x1, waiting for transfers between devices, body(): own_home = lax.all_to_all(own_out, cube, 0, 0, tiled=True)  8.83 us
    all_to_all x1, starting transfers between devices, body(): own_home = lax.all_to_all(own_out, cube, 0, 0, tiled=True)  5.11 us
    all_to_all x1, starting transfers between devices, body(): guest_home = lax.all_to_all(guest_out, cube, 0, 0, tiled=True)  4.9 us
    unnamed x14, local copies, waits for them, and re-layouts  4.17 us
    ppermute x1, starting transfers between devices, body(): guest = lax.ppermute(pay, 'half', swap)  4.06 us
  transfers between devices with their start and end apart: 5, of which 3 were waited for; matrix products, arithmetic and copies ran while one was open for 2% of the time, Pallas kernels for 27%

profile of v1, /device:TPU:0, one launch (start us, length us, event | category | flops | bytes accessed | tf_op | source)
XLA Modules:
  0.0 100.6 jit_solution(15067015459185010635)
XLA Ops:
  0.6 0.0 copy-start.5
  0.6 2.8 %shard_map.122 = (bf16[32,4224]{1,0:T(8,128)(2,1)}, bf16[128,4096]{1,0:T(8,128)(2,1)}, bf16[32,128]{1,0:T(8,128)(2,1)}) custom-call(s32[1]{0:T(128)} %bitcast.half_ref, s32[4,32]{1,0:T(4,128)} %bitcast.18, bf16[4,32]{1,0:T(4,128)(2,1)} %bitcast.19, bf16[32,2048]{1,0:T(8,128)(2,1)} %x_ref.1, bf16[32,2048]{1,0:T(8,128)(2,1)} %g_ref.1), custom_call_target="tpu_custom_call" | custom-call | flops 1000000 | bytes 1000000 | tf_op jit(solution)/shard_map/pallas_call | solution.py:158
  3.5 4.1 %collective-permute-start = (bf16[32,4224]{1,0:T(8,128)(2,1)}, bf16[32,4224]{1,0:T(8,128)(2,1)S(1)}, u32[]{:S(2)}, u32[]{:S(2)}) collective-permute-start(bf16[32,4224]{1,0:T(8,128)(2,1)} %get-tuple-element.9), channel_id=1, source_target_pairs={{0,4},{4,0},{1,5},{5,1},{2,6},{6,2},{3,7},{7,3},{8,12},{12,8},{9,1... | collective-permute-start | bytes 811016 | tf_op jit(solution)/shard_map/ppermute | solution.py:191
  7.5 12.5 %collective-permute-done.pay_ref = bf16[32,4224]{1,0:T(8,128)(2,1)S(1)} collective-permute-done((bf16[32,4224]{1,0:T(8,128)(2,1)}, bf16[32,4224]{1,0:T(8,128)(2,1)S(1)}, u32[]{:S(2)}, u32[]{:S(2)}) %collective-permute-start) | collective-permute-done | bytes 270368 | tf_op jit(solution)/shard_map/ppermute | solution.py:191
  20.0 0.0 copy-start.3
  20.0 0.7 copy-done.3
  20.7 2.6 %shard_map.124 = (bf16[128,4096]{1,0:T(8,128)(2,1)}, bf16[32,128]{1,0:T(8,128)(2,1)}) custom-call(s32[1]{0:T(128)} %bitcast.half_ref, bf16[32,4224]{1,0:T(8,128)(2,1)} %copy-done.3), custom_call_target="tpu_custom_call" | custom-call | flops 1000000 | bytes 1000000 | tf_op jit(solution)/shard_map/pallas_call | solution.py:158
  23.4 19.0 %all_to_all.44 = bf16[16,8,4096]{2,1,0:T(8,128)(2,1)S(1)} all-to-all(bf16[16,8,4096]{2,1,0:T(8,128)(2,1)} %bitcast.17), channel_id=1, replica_groups=mesh['group'=4,'half'=2,'deep'=4] {'group','deep'}, dimensions={0} | all-to-all | bytes 2097152 | tf_op jit(solution)/shard_map/all_to_all | solution.py:196
  42.4 3.7 %all-to-all-start = ((bf16[16,8,4096]{2,1,0:T(8,128)(2,1)}), bf16[16,8,4096]{2,1,0:T(8,128)(2,1)S(1)}, u32[]{:S(2)}, u32[]{:S(2)}) async-start(bf16[16,8,4096]{2,1,0:T(8,128)(2,1)} %bitcast.16), calls=%async_computation | async-start | bytes 2097152 | tf_op jit(solution)/shard_map/all_to_all | solution.py:192
  46.0 1.5 %copy.13.refs_3_ = bf16[2,2048,64]{2,1,0:T(8,128)(2,1)S(1)} copy(bf16[2,2048,64]{1,2,0:T(8,128)(2,1)} %param.19) | data formatting | bytes 1048576 | tf_op args[8]
  47.6 0.0 copy-done.5
  47.6 0.2 copy.14.refs_4_
  47.8 11.9 %shard_map.125 = bf16[128,2560]{1,0:T(8,128)(2,1)S(1)} custom-call(bf16[128,4096]{1,0:T(8,128)(2,1)S(1)} %bitcast.12, bf16[2,2048,512]{2,1,0:T(8,128)(2,1)} %refs_0_.3, bf16[2,2048,512]{2,1,0:T(8,128)(2,1)} %refs_1_.3, bf16[2,512,2048]{2,1,0:T(8,128)(2,1)} %refs_2_.3, bf16[2,2048,64]{2,1,0:T(8,128)(2,1)S(1)} %copy.13.refs_3_, ...), custom_call_target="tpu_custom_call" | custom-call | flops 5536481280 | bytes 21626880 | tf_op jit(solution)/shard_map/pallas_call | solution.py:158
  59.7 0.0 copy-start
  59.7 0.9 copy-done
  60.5 0.2 all-to-all-done
  60.7 4.9 %all-to-all-start.3 = ((bf16[16,8,2560]{2,1,0:T(8,128)(2,1)}), bf16[16,8,2560]{2,1,0:T(8,128)(2,1)S(1)}, u32[]{:S(2)}, u32[]{:S(2)}) async-start(bf16[16,8,2560]{2,1,0:T(8,128)(2,1)} %bitcast.13), calls=%async_computation.3 | async-start | bytes 1310720 | tf_op jit(solution)/shard_map/all_to_all | solution.py:216
  65.6 12.8 %shard_map.123 = bf16[128,2560]{1,0:T(8,128)(2,1)} custom-call(bf16[128,4096]{1,0:T(8,128)(2,1)S(1)} %bitcast.11, bf16[2,2048,512]{2,1,0:T(8,128)(2,1)} %refs_0_.3, bf16[2,2048,512]{2,1,0:T(8,128)(2,1)} %refs_1_.3, bf16[2,512,2048]{2,1,0:T(8,128)(2,1)} %refs_2_.3, bf16[2,2048,64]{2,1,0:T(8,128)(2,1)S(1)} %copy.13.refs_3_, ...), custom_call_target="tpu_custom_call" | custom-call | flops 5536481280 | bytes 21626880 | tf_op jit(solution)/shard_map/pallas_call | solution.py:158
  78.4 0.0 all-to-all-done.3
  78.4 0.0 copy-start.2
  78.4 5.1 %all-to-all-start.1 = ((bf16[16,8,2560]{2,1,0:T(8,128)(2,1)}), bf16[16,8,2560]{2,1,0:T(8,128)(2,1)S(1)}, u32[]{:S(2)}, u32[]{:S(2)}) async-start(bf16[16,8,2560]{2,1,0:T(8,128)(2,1)} %bitcast.5), calls=%async_computation.1 | async-start | bytes 1310720 | tf_op jit(solution)/shard_map/all_to_all | solution.py:224
  83.5 0.0 copy-done.2
  83.5 2.0 %shard_map.126 = bf16[32,2560]{1,0:T(8,128)(2,1)} custom-call(bf16[32,128]{1,0:T(8,128)(2,1)} %get-tuple-element.10.place_ref, bf16[128,2560]{1,0:T(8,128)(2,1)} %bitcast.15), custom_call_target="tpu_custom_call" | custom-call | flops 1000000 | bytes 1000000 | tf_op jit(solution)/shard_map/pallas_call | solution.py:158
  85.5 3.3 %collective-permute-start.1 = (bf16[32,2560]{1,0:T(8,128)(2,1)}, bf16[32,2560]{1,0:T(8,128)(2,1)S(1)}, u32[]{:S(2)}, u32[]{:S(2)}) collective-permute-start(bf16[32,2560]{1,0:T(8,128)(2,1)} %shard_map.126), channel_id=1, source_target_pairs={{0,4},{4,0},{1,5},{5,1},{2,6},{6,2},{3,7},{7,3},{8,12},{12,8},{9,1... | collective-permute-start | bytes 491528 | tf_op jit(solution)/shard_map/ppermute | solution.py:223
  88.8 8.8 %all-to-all-done.1 = bf16[16,8,2560]{2,1,0:T(8,128)(2,1)S(1)} async-done(((bf16[16,8,2560]{2,1,0:T(8,128)(2,1)}), bf16[16,8,2560]{2,1,0:T(8,128)(2,1)S(1)}, u32[]{:S(2)}, u32[]{:S(2)}) %all-to-all-start.1) | async-done | bytes 655392 | tf_op jit(solution)/shard_map/all_to_all | solution.py:224
  97.6 0.0 copy-start.1
  97.6 0.0 collective-permute-done.1.part_ref
  97.6 0.0 copy-start.4
  97.6 0.8 copy-done.1
  98.5 0.1 copy-done.4
  98.5 2.1 %shard_map.127 = (bf16[32,2048]{1,0:T(8,128)(2,1)}, f32[8,512]{1,0:T(8,128)}) custom-call(bf16[32,128]{1,0:T(8,128)(2,1)} %get-tuple-element.7.place_ref, bf16[128,2560]{1,0:T(8,128)(2,1)} %bitcast.14, bf16[32,2560]{1,0:T(8,128)(2,1)} %copy-done.4, s32[1,32]{1,0:T(1,128)} %query_ref.1), custom_call_target="tpu_custom_call" | custom-call | flops 1000000 | bytes 1000000 | tf_op jit(solution)/shard_map/pallas_call | solution.py:158
Async XLA Ops:
  0.6 46.9 %copy-start.5 = (bf16[2,512,64]{1,2,0:T(8,128)(2,1)S(1)}, bf16[2,512,64]{1,2,0:T(8,128)(2,1)}, u32[]{:S(2)}) copy-start(bf16[2,512,64]{1,2,0:T(8,128)(2,1)} %param.20) | copy-start | bytes 393220
  3.5 16.5 %collective-permute-start = (bf16[32,4224]{1,0:T(8,128)(2,1)}, bf16[32,4224]{1,0:T(8,128)(2,1)S(1)}, u32[]{:S(2)}, u32[]{:S(2)}) collective-permute-start(bf16[32,4224]{1,0:T(8,128)(2,1)} %get-tuple-element.9), channel_id=1, source_target_pairs={{0,4},{4,0},{1,5},{5,1},{2,6},{6,2},{3,7},{7,3},{8,12},{12,8},{9,1... | collective-permute-start | bytes 811016 | tf_op jit(solution)/shard_map/ppermute | solution.py:191
  20.0 0.7 copy-start.3
  42.4 18.3 %all-to-all-start = ((bf16[16,8,4096]{2,1,0:T(8,128)(2,1)}), bf16[16,8,4096]{2,1,0:T(8,128)(2,1)S(1)}, u32[]{:S(2)}, u32[]{:S(2)}) async-start(bf16[16,8,4096]{2,1,0:T(8,128)(2,1)} %bitcast.16), calls=%async_computation | async-start | bytes 2097152 | tf_op jit(solution)/shard_map/all_to_all | solution.py:192
  59.7 0.9 copy-start
  60.7 17.7 %all-to-all-start.3 = ((bf16[16,8,2560]{2,1,0:T(8,128)(2,1)}), bf16[16,8,2560]{2,1,0:T(8,128)(2,1)S(1)}, u32[]{:S(2)}, u32[]{:S(2)}) async-start(bf16[16,8,2560]{2,1,0:T(8,128)(2,1)} %bitcast.13), calls=%async_computation.3 | async-start | bytes 1310720 | tf_op jit(solution)/shard_map/all_to_all | solution.py:216
  78.4 5.1 %copy-start.2 = (bf16[16,8,2560]{2,1,0:T(8,128)(2,1)}, bf16[16,8,2560]{2,1,0:T(8,128)(2,1)S(1)}, u32[]{:S(2)}) copy-start(bf16[16,8,2560]{2,1,0:T(8,128)(2,1)S(1)} %all-to-all-done.3) | copy-start | bytes 1966084
  78.4 19.2 %all-to-all-start.1 = ((bf16[16,8,2560]{2,1,0:T(8,128)(2,1)}), bf16[16,8,2560]{2,1,0:T(8,128)(2,1)S(1)}, u32[]{:S(2)}, u32[]{:S(2)}) async-start(bf16[16,8,2560]{2,1,0:T(8,128)(2,1)} %bitcast.5), calls=%async_computation.1 | async-start | bytes 1310720 | tf_op jit(solution)/shard_map/all_to_all | solution.py:224
  85.5 12.1 %collective-permute-start.1 = (bf16[32,2560]{1,0:T(8,128)(2,1)}, bf16[32,2560]{1,0:T(8,128)(2,1)S(1)}, u32[]{:S(2)}, u32[]{:S(2)}) collective-permute-start(bf16[32,2560]{1,0:T(8,128)(2,1)} %shard_map.126), channel_id=1, source_target_pairs={{0,4},{4,0},{1,5},{5,1},{2,6},{6,2},{3,7},{7,3},{8,12},{12,8},{9,1... | collective-permute-start | bytes 491528 | tf_op jit(solution)/shard_map/ppermute | solution.py:223
  97.6 0.8 copy-start.1
  97.6 0.9 copy-start.4

commit v2 on v1

v2 whole, which is shorter than its diff:
```python
import functools

import jax
import jax.numpy as jnp
from jax import lax
from jax.experimental import pallas as pl
from jax.experimental.pallas import tpu as pltpu
from jax.sharding import Mesh, PartitionSpec as P


QRY_DEV = 8
PAIR = 2
LANES = 128
F32 = jnp.float32
BF16 = jnp.bfloat16
NT = (((1,), (1,)), ((), ()))
AXES = ("row", "core", "half", "deep")


def dot(a, b):
    return jnp.dot(a, b, preferred_element_type=F32)


def dot_nt(a, b):
    return lax.dot_general(a, b, NT, preferred_element_type=F32)


def pay_kernel(ids_ref, w_ref, x_ref, g_ref, pay_ref):
    top, tok = ids_ref.shape
    width = x_ref.shape[1]
    flat = jnp.concatenate([ids_ref[...].astype(F32), w_ref[...].astype(F32)], axis=0)
    flat = jnp.concatenate([flat, jnp.zeros((LANES - 2 * top, tok), F32)], axis=0)
    flat = jnp.concatenate([flat, jnp.zeros((LANES, LANES - tok), F32)], axis=1)
    pay_ref[:, :width] = x_ref[...]
    pay_ref[:, width : 2 * width] = g_ref[...]
    pay_ref[:, 2 * width :] = flat.T[:tok, :].astype(BF16)


def pack_kernel(top, experts, capacity, deep, here_ref, first_ref, second_ref, *outs):
    place_ref, sends = outs[-1], outs[:-1]
    tok = first_ref.shape[0]
    width = sends[0].shape[1] // 2
    piece = sends[0].shape[0]
    shape = (PAIR * tok, piece * len(sends))
    both = jnp.concatenate([first_ref[...], second_ref[...]], axis=0)
    meta = both[:, 2 * width :].astype(F32)
    slot = lax.broadcasted_iota(jnp.int32, shape, 1)
    block = lax.broadcasted_iota(jnp.int32, shape, 0) // tok
    chip = slot // piece
    to_row, to_deep = here_ref[0] ^ (chip // deep), here_ref[3] ^ (chip % deep)
    device = ((to_row * PAIR + here_ref[1]) * PAIR + here_ref[2]) * deep + to_deep
    expert = (device * experts + slot // (PAIR * capacity) % experts).astype(F32)
    meant = jnp.where(slot // capacity % PAIR == block, 1.0, 0.0)
    named = jnp.zeros(shape, F32)
    weight = jnp.zeros(shape, F32)
    for k in range(top):
        hit = jnp.where(meta[:, k : k + 1] == expert, meant, 0.0)
        named = named + hit
        weight = weight + hit * meta[:, top + k : top + k + 1]
    row = lax.broadcasted_iota(jnp.int32, (PAIR * tok, PAIR * tok), 0)
    col = lax.broadcasted_iota(jnp.int32, (PAIR * tok, PAIR * tok), 1)
    earlier = dot(jnp.where(col < row, 1.0, 0.0).astype(BF16), named.astype(BF16))
    place = jnp.where(earlier == (slot % capacity).astype(F32), named, 0.0)
    place_ref[...] = place.astype(BF16)
    pick = place.T.astype(BF16)
    scale = jnp.sum((place * weight).T, axis=1, keepdims=True)
    x = dot(pick, both[:, :width]).astype(BF16)
    delta = (scale * dot(pick, both[:, width : 2 * width])).astype(BF16)
    for i, send in enumerate(sends):
        send[:, :width] = x[i * piece : (i + 1) * piece]
        send[:, width:] = delta[i * piece : (i + 1) * piece]


def expert_kernel(count, group, *refs):
    ins, hbm, outs, vmem = (
        refs[:count],
        refs[count : count + 6],
        refs[count + 6 : 2 * count + 6],
        refs[2 * count + 6 : 2 * count + 12],
    )
    outer_ref, sem = refs[2 * count + 12 :]
    gate, up, down, left_proj, right_proj, stored = vmem
    experts, width, _ = gate.shape
    rank = left_proj.shape[1]
    piece = ins[0].shape[0]
    rows = piece * count

    def copy(i, j):
        return pltpu.make_async_copy(hbm[i].at[j], vmem[i].at[j], sem.at[i, j])

    for j in range(experts):
        for i in range(5):
            copy(i, j).start()
    for j in range(experts):
        copy(5, j).start()
    x = jnp.concatenate([r[:, :width] for r in ins], axis=0)
    delta = jnp.concatenate([r[:, width:] for r in ins], axis=0)
    owner = lax.broadcasted_iota(jnp.int32, (rows, 1), 0) // group % experts
    left = jnp.zeros((rows, rank), F32)
    right = jnp.zeros((rows, rank), F32)
    grad = jnp.zeros((rows, width), F32)
    for j in range(experts):
        mine = owner == j
        copy(0, j).wait()
        a_gate = dot(x, gate[j])
        copy(1, j).wait()
        a_up = dot(x, up[j])
        copy(2, j).wait()
        d_hidden = dot_nt(delta, down[j])
        sig = jax.nn.sigmoid(a_gate)
        active = a_gate * sig
        hidden = (active * a_up).astype(BF16)
        grad_up = jnp.where(mine, d_hidden * active, 0.0).astype(BF16)
        grad_gate = jnp.where(
            mine, d_hidden * a_up * sig * (1.0 + a_gate * (1.0 - sig)), 0.0
        ).astype(BF16)
        grad = grad + dot_nt(grad_gate, gate[j])
        grad = grad + dot_nt(grad_up, up[j])
        copy(3, j).wait()
        left = jnp.where(mine, dot_nt(delta, left_proj[j]), left)
        copy(4, j).wait()
        right = jnp.where(mine, dot_nt(hidden, right_proj[j]), right)
    grad = grad.astype(BF16)
    per = LANES // rank
    wide = jnp.concatenate([right] * per, axis=1)
    lane = lax.broadcasted_iota(jnp.int32, (rows, LANES), 1) // rank
    for c in range(rank // per):
        factor = left[:, c * per : c * per + 1]
        for k in range(1, per):
            factor = jnp.where(lane == k, left[:, c * per + k : c * per + k + 1], factor)
        outer = factor * wide
        for j in range(experts):
            outer_ref[j, :, c * LANES : (c + 1) * LANES] = jnp.where(owner == j, outer, 0.0).astype(
                BF16
            )
    score = jnp.zeros((rows, stored.shape[2]), F32)
    for j in range(experts):
        copy(5, j).wait()
        score = score + dot(outer_ref[j], stored[j])
    score = score.astype(BF16)
    for i, out in enumerate(outs):
        out[:, :width] = grad[i * piece : (i + 1) * piece]
        out[:, width:] = score[i * piece : (i + 1) * piece]


def part_kernel(place_ref, *refs):
    ins, keep_ref, give_ref = refs[:-2], refs[-2], refs[-1]
    tok = keep_ref.shape[0]
    total = dot(place_ref[...], jnp.concatenate([r[...] for r in ins], axis=0))
    keep_ref[...] = total[:tok]
    give_ref[...] = total[tok:].astype(BF16)


def join_kernel(keep_ref, more_ref, out_ref):
    out_ref[...] = (keep_ref[...] + more_ref[...].astype(F32)).astype(BF16)


def final_kernel(keep_ref, more_ref, far_ref, query_ref, grad_ref, score_ref):
    width = grad_ref.shape[1]
    total = keep_ref[...] + more_ref[...].astype(F32) + far_ref[...].astype(F32)
    grad_ref[...] = total[:, :width].astype(BF16)
    wanted = lax.broadcasted_iota(jnp.int32, (score_ref.shape[0], query_ref.shape[1]), 0)
    pick = jnp.where(query_ref[...] == wanted, 1.0, 0.0)
    score_ref[...] = jnp.dot(
        pick, total[:, width:], precision=lax.Precision.HIGHEST, preferred_element_type=F32
    )


VMEM = pl.BlockSpec(memory_space=pltpu.VMEM)
SMEM = pl.BlockSpec(memory_space=pltpu.SMEM)
HBM = pl.BlockSpec(memory_space=pltpu.HBM)


def call(kernel, outs, in_specs, args, scratch=(), flops=1_000_000, moved=1_000_000, limit=8 << 20):
    return pl.pallas_call(
        kernel,
        out_shape=outs,
        in_specs=in_specs,
        out_specs=jax.tree.map(lambda _: VMEM, outs),
        scratch_shapes=scratch,
        compiler_params=pltpu.CompilerParams(vmem_limit_bytes=limit),
        cost_estimate=pl.CostEstimate(flops=flops, bytes_accessed=moved, transcendentals=0),
    )(*args)


def layer(tokens, out_grad, expert_ids, gate_w, query_ids, *weights):
    weights = weights[:3] + tuple(w.transpose(0, 2, 1) for w in weights[3:5]) + weights[5:]
    tok, width = tokens.shape
    top = expert_ids.shape[1]
    experts = weights[0].shape[0]
    train = weights[5].shape[2]
    row_size, deep = lax.axis_size("row"), lax.axis_size("deep")
    chips = row_size * deep
    capacity = 2 * tok // (experts * PAIR * deep)
    piece = experts * PAIR * capacity
    here = jnp.stack([lax.axis_index(a) for a in AXES]).astype(jnp.int32)
    shape = jax.ShapeDtypeStruct

    def swap(value, row=0, core=0, half=0, far=0):
        pairs = []
        for r in range(row_size):
            for c in range(PAIR):
                for h in range(PAIR):
                    for d in range(deep):
                        source = ((r * PAIR + c) * PAIR + h) * deep + d
                        target = (((r ^ row) * PAIR + (c ^ core)) * PAIR + (h ^ half)) * deep
                        pairs.append((source, target + (d ^ far)))
        return lax.ppermute(value, AXES, pairs)

    def exchange(pieces):
        order = sorted(range(1, chips), key=lambda o: -bin(o).count("1"))
        moved = {o: swap(pieces[o], row=o // deep, far=o % deep) for o in order}
        return [pieces[0]] + [moved[o] for o in range(1, chips)]

    def pack(first, second):
        outs = (shape((piece, 2 * width), BF16),) * chips
        outs += (shape((PAIR * tok, piece * chips), BF16),)
        kernel = functools.partial(pack_kernel, top, experts, capacity, deep)
        filled = call(kernel, outs, [SMEM, VMEM, VMEM], (here, first, second), limit=12 << 20)
        return filled[:-1], filled[-1]

    def part(place, pieces):
        outs = (shape((tok, width + train), F32), shape((tok, width + train), BF16))
        return call(part_kernel, outs, [VMEM] * (1 + chips), (place, *pieces))

    pay = call(
        pay_kernel,
        shape((tok, 2 * width + LANES), BF16),
        [VMEM] * 4,
        (expert_ids.T, gate_w.T, tokens, out_grad),
    )
    guest = swap(pay, half=1)
    other = swap(pay, core=1)
    own_send, own_place = pack(pay, other)
    own_rows = exchange(own_send)
    other = swap(guest, core=1)
    guest_send, guest_place = pack(guest, other)
    guest_rows = exchange(guest_send)
    rows = 2 * chips * piece
    size = sum(w.size for w in weights)
    outs = call(
        functools.partial(expert_kernel, 2 * chips, PAIR * capacity),
        (shape((piece, width + train), BF16),) * (2 * chips),
        [VMEM] * (2 * chips) + [HBM] * len(weights),
        (*own_rows, *guest_rows, *weights),
        scratch=[pltpu.VMEM(w.shape, w.dtype) for w in weights]
        + [
            pltpu.VMEM((experts, rows, weights[5].shape[1]), BF16),
            pltpu.SemaphoreType.DMA((len(weights), experts)),
        ],
        flops=2 * rows * size,
        moved=2 * size,
        limit=50 << 20,
    )
    guest_back = exchange(outs[chips:])
    own_back = exchange(outs[:chips])
    guest_keep, guest_give = part(guest_place, guest_back)
    more = swap(guest_give, core=1)
    far = call(join_kernel, shape((tok, width + train), BF16), [VMEM] * 2, (guest_keep, more))
    far = swap(far, half=1)
    own_keep, own_give = part(own_place, own_back)
    more = swap(own_give, core=1)
    return call(
        final_kernel,
        (shape((tok, width), BF16), shape((QRY_DEV, train), F32)),
        [VMEM] * 4,
        (own_keep, more, far, query_ids),
    )


def solution(mesh):
    groups, line = mesh.shape["group"], mesh.shape["expert"]
    devices = mesh.devices.reshape(groups // PAIR, PAIR, PAIR, line // PAIR)
    return jax.shard_map(
        layer,
        mesh=Mesh(devices, AXES),
        in_specs=(P(AXES, None),) * 5 + (P(AXES, None, None),) * 6,
        out_specs=(P(AXES, None), P(AXES, None)),
        check_vma=False,
    )
```

time: 101 us -> 109 us (1.079)
  starting transfers between devices: 21 us -> 44.8 us
  blocking collectives: 19 us -> 0 us
  waiting for transfers between devices: 21.5 us -> 38.9 us
  Pallas kernels: 34.2 us -> 19.5 us
    ppermute x2 -> x34, starting transfers between devices: 7.32 us -> 44.8 us  [swap(): return lax.ppermute(value, AXES, pairs)]
    ppermute x2 -> x34, waiting for transfers between devices: 12.5 us -> 38.9 us  [swap(): return lax.ppermute(value, AXES, pairs)]
    all_to_all x1 -> x0, blocking collectives: 19 us -> none  [body(): guest_rows = lax.all_to_all(guest_send, cube, 0, 0, tiled=True)]
    pallas_call x6 -> x8, Pallas kernels: 34.2 us -> 19.5 us  [call(): pl.pallas_call(kernel, out_shape=outs, in_specs=in_specs, out_specs=jax.t...]
    all_to_all x3 -> x0, starting transfers between devices: 13.7 us -> none  [the longest x1 5.11 us: body(): own_home = lax.all_to_all(own_out, cube, 0, 0, tiled=True)]
    all_to_all x3 -> x0, waiting for transfers between devices: 9 us -> none  [the longest x1 8.83 us: body(): own_home = lax.all_to_all(own_out, cube, 0, 0, tiled=True)]
  transfers between devices with their start and end apart: 5 -> 34, of which waited for: 3 -> 7; matrix products, arithmetic and copies ran while one was open for 2% -> 0% of each run, Pallas kernels for 27% -> 3%
where the time goes in v2:
time: 109 us
  starting transfers between devices  44.8 us (41%)
  waiting for transfers between devices  38.9 us (36%)
  Pallas kernels  19.5 us (18%)
  local copies, waits for them, and re-layouts  5.1 us (5%)
    ppermute x34, starting transfers between devices, swap(): return lax.ppermute(value, AXES, pairs)  44.8 us
    ppermute x34, waiting for transfers between devices, swap(): return lax.ppermute(value, AXES, pairs)  38.9 us
    pallas_call x8, Pallas kernels, call(): pl.pallas_call(kernel, out_shape=outs, in_specs=in_specs, out_specs=jax.t...  19.5 us
    unnamed x14, local copies, waits for them, and re-layouts  5.1 us
  transfers between devices with their start and end apart: 34, of which 7 were waited for; matrix products, arithmetic and copies ran while one was open for 0% of the time, Pallas kernels for 3%

profile of v2, /device:TPU:0, one launch (start us, length us, event | category | flops | bytes accessed | tf_op | source)
XLA Modules:
  0.0 109.1 jit_solution(10441233700291632094)
XLA Ops:
  0.6 0.9 copy-done.2
  1.5 0.9 copy-done.3
  2.4 0.7 copy-done.4
  3.1 0.7 copy-done.5
  3.9 4.1 %collective-permute-start.8 = (bf16[32,4224]{1,0:T(8,128)(2,1)S(1)}, bf16[32,4224]{1,0:T(8,128)(2,1)S(1)}, u32[]{:S(2)}, u32[]{:S(2)}) collective-permute-start(bf16[32,4224]{1,0:T(8,128)(2,1)S(1)} %shard_map.122.first_ref), channel_id=1, source_target_pairs={{0,4},{1,5},{2,6},{3,7},{4,0},{5,1},{6,2},{7,3},{8,12},{9,13},{10,... | collective-permute-start | bytes 811016 | tf_op jit(solution)/shard_map/ppermute | solution.py:208
  8.0 12.3 %collective-permute-done.8.first_ref = bf16[32,4224]{1,0:T(8,128)(2,1)S(1)} collective-permute-done((bf16[32,4224]{1,0:T(8,128)(2,1)S(1)}, bf16[32,4224]{1,0:T(8,128)(2,1)S(1)}, u32[]{:S(2)}, u32[]{:S(2)}) %collective-permute-start.8) | collective-permute-done | bytes 270368 | tf_op jit(solution)/shard_map/ppermute | solution.py:208
  20.3 1.2 %shard_map.123 = (bf16[16,4096]{1,0:T(8,128)(2,1)S(1)}, bf16[16,4096]{1,0:T(8,128)(2,1)S(1)}, bf16[16,4096]{1,0:T(8,128)(2,1)S(1)}, bf16[16,4096]{1,0:T(8,128)(2...) custom-call(s32[4]{0:T(128)S(1)} %pad_add_fusion.here_ref, ...), custom_call_target="tpu_custom_call" | custom-call | flops 1000000 | bytes 1000000 | tf_op jit(solution)/shard_map/pallas_call | solution.py:175
  21.6 1.6 %collective-permute-start.1 = (bf16[16,4096]{1,0:T(8,128)(2,1)S(1)}, bf16[16,4096]{1,0:T(8,128)(2,1)S(1)}, u32[]{:S(2)}, u32[]{:S(2)}) collective-permute-start(bf16[16,4096]{1,0:T(8,128)(2,1)S(1)} %get-tuple-element.42), channel_id=1, source_target_pairs={{0,1},{1,0},{2,3},{3,2},{4,5},{5,4},{6,7},{7,6},{8,9},{9,8},{10,11... | collective-permute-start | bytes 393224 | tf_op jit(solution)/shard_map/ppermute | solution.py:208
  23.2 0.7 collective-permute-start.2
  23.8 1.3 %collective-permute-start.3 = (bf16[16,4096]{1,0:T(8,128)(2,1)S(1)}, bf16[16,4096]{1,0:T(8,128)(2,1)S(1)}, u32[]{:S(2)}, u32[]{:S(2)}) collective-permute-start(bf16[16,4096]{1,0:T(8,128)(2,1)S(1)} %get-tuple-element.44), channel_id=1, source_target_pairs={{0,3},{1,2},{2,1},{3,0},{4,7},{5,6},{6,5},{7,4},{8,11},{9,10},{10,... | collective-permute-start | bytes 393224 | tf_op jit(solution)/shard_map/ppermute | solution.py:208
  25.1 1.6 %collective-permute-start.4 = (bf16[16,4096]{1,0:T(8,128)(2,1)S(1)}, bf16[16,4096]{1,0:T(8,128)(2,1)S(1)}, u32[]{:S(2)}, u32[]{:S(2)}) collective-permute-start(bf16[16,4096]{1,0:T(8,128)(2,1)S(1)} %get-tuple-element.45), channel_id=1, source_target_pairs={{0,16},{1,17},{2,18},{3,19},{4,20},{5,21},{6,22},{7,23},{8,24},{9,... | collective-permute-start | bytes 393224 | tf_op jit(solution)/shard_map/ppermute | solution.py:208
  26.7 1.4 %collective-permute-start.5 = (bf16[16,4096]{1,0:T(8,128)(2,1)S(1)}, bf16[16,4096]{1,0:T(8,128)(2,1)S(1)}, u32[]{:S(2)}, u32[]{:S(2)}) collective-permute-start(bf16[16,4096]{1,0:T(8,128)(2,1)S(1)} %get-tuple-element.46), channel_id=1, source_target_pairs={{0,17},{1,16},{2,19},{3,18},{4,21},{5,20},{6,23},{7,22},{8,25},{9,... | collective-permute-start | bytes 393224 | tf_op jit(solution)/shard_map/ppermute | solution.py:208
  28.1 1.2 %shard_map.124 = (bf16[16,4096]{1,0:T(8,128)(2,1)S(1)}, bf16[16,4096]{1,0:T(8,128)(2,1)S(1)}, bf16[16,4096]{1,0:T(8,128)(2,1)S(1)}, bf16[16,4096]{1,0:T(8,128)(2...) custom-call(s32[4]{0:T(128)S(1)} %pad_add_fusion.here_ref, ...), custom_call_target="tpu_custom_call" | custom-call | flops 1000000 | bytes 1000000 | tf_op jit(solution)/shard_map/pallas_call | solution.py:175
  29.4 1.7 %collective-permute-start.6 = (bf16[16,4096]{1,0:T(8,128)(2,1)S(1)}, bf16[16,4096]{1,0:T(8,128)(2,1)S(1)}, u32[]{:S(2)}, u32[]{:S(2)}) collective-permute-start(bf16[16,4096]{1,0:T(8,128)(2,1)S(1)} %get-tuple-element.47), channel_id=1, source_target_pairs={{0,18},{1,19},{2,16},{3,17},{4,22},{5,23},{6,20},{7,21},{8,26},{9,... | collective-permute-start | bytes 393224 | tf_op jit(solution)/shard_map/ppermute | solution.py:208
  31.1 1.2 %collective-permute-start.7 = (bf16[16,4096]{1,0:T(8,128)(2,1)S(1)}, bf16[16,4096]{1,0:T(8,128)(2,1)S(1)}, u32[]{:S(2)}, u32[]{:S(2)}) collective-permute-start(bf16[16,4096]{1,0:T(8,128)(2,1)S(1)} %get-tuple-element.48), channel_id=1, source_target_pairs={{0,19},{1,18},{2,17},{3,16},{4,23},{5,22},{6,21},{7,20},{8,27},{9,... | collective-permute-start | bytes 393224 | tf_op jit(solution)/shard_map/ppermute | solution.py:208
  32.3 1.5 %collective-permute-start.10 = (bf16[16,4096]{1,0:T(8,128)(2,1)S(1)}, bf16[16,4096]{1,0:T(8,128)(2,1)S(1)}, u32[]{:S(2)}, u32[]{:S(2)}) collective-permute-start(bf16[16,4096]{1,0:T(8,128)(2,1)S(1)} %get-tuple-element.50), channel_id=1, source_target_pairs={{0,1},{1,0},{2,3},{3,2},{4,5},{5,4},{6,7},{7,6},{8,9},{9,8},{10,11... | collective-permute-start | bytes 393224 | tf_op jit(solution)/shard_map/ppermute | solution.py:208
  33.8 0.7 collective-permute-start.11
  34.5 6.4 %collective-permute-done.5.refs_5_ = bf16[16,4096]{1,0:T(8,128)(2,1)S(1)} collective-permute-done((bf16[16,4096]{1,0:T(8,128)(2,1)S(1)}, bf16[16,4096]{1,0:T(8,128)(2,1)S(1)}, u32[]{:S(2)}, u32[]{:S(2)}) %collective-permute-start.5) | collective-permute-done | bytes 131104 | tf_op jit(solution)/shard_map/ppermute | solution.py:208
  40.9 0.9 collective-permute-start.12
  41.8 0.4 collective-permute-start.13
  42.2 1.9 %collective-permute-start.14 = (bf16[16,4096]{1,0:T(8,128)(2,1)S(1)}, bf16[16,4096]{1,0:T(8,128)(2,1)S(1)}, u32[]{:S(2)}, u32[]{:S(2)}) collective-permute-start(bf16[16,4096]{1,0:T(8,128)(2,1)S(1)} %get-tuple-element.54), channel_id=1, source_target_pairs={{0,17},{1,16},{2,19},{3,18},{4,21},{5,20},{6,23},{7,22},{8,25},{9,... | collective-permute-start | bytes 393224 | tf_op jit(solution)/shard_map/ppermute | solution.py:208
  44.1 1.4 %collective-permute-start.15 = (bf16[16,4096]{1,0:T(8,128)(2,1)S(1)}, bf16[16,4096]{1,0:T(8,128)(2,1)S(1)}, u32[]{:S(2)}, u32[]{:S(2)}) collective-permute-start(bf16[16,4096]{1,0:T(8,128)(2,1)S(1)} %get-tuple-element.55), channel_id=1, source_target_pairs={{0,18},{1,19},{2,16},{3,17},{4,22},{5,23},{6,20},{7,21},{8,26},{9,... | collective-permute-start | bytes 393224 | tf_op jit(solution)/shard_map/ppermute | solution.py:208
  45.5 2.2 %collective-permute-start.16 = (bf16[16,4096]{1,0:T(8,128)(2,1)S(1)}, bf16[16,4096]{1,0:T(8,128)(2,1)S(1)}, u32[]{:S(2)}, u32[]{:S(2)}) collective-permute-start(bf16[16,4096]{1,0:T(8,128)(2,1)S(1)} %get-tuple-element.56), channel_id=1, source_target_pairs={{0,19},{1,18},{2,17},{3,16},{4,23},{5,22},{6,21},{7,20},{8,27},{9,... | collective-permute-start | bytes 393224 | tf_op jit(solution)/shard_map/ppermute | solution.py:208
  47.7 6.5 %collective-permute-done.13.refs_12_ = bf16[16,4096]{1,0:T(8,128)(2,1)S(1)} collective-permute-done((bf16[16,4096]{1,0:T(8,128)(2,1)S(1)}, bf16[16,4096]{1,0:T(8,128)(2,1)S(1)}, u32[]{:S(2)}, u32[]{:S(2)}) %collective-permute-start.13) | collective-permute-done | bytes 131104 | tf_op jit(solution)/shard_map/ppermute | solution.py:208
  54.2 1.0 copy-done
  55.3 0.9 copy-done.1
  56.2 15.7 %shard_map.125 = (bf16[16,2560]{1,0:T(8,128)(2,1)S(1)}, bf16[16,2560]{1,0:T(8,128)(2,1)S(1)}, bf16[16,2560]{1,0:T(8,128)(2,1)S(1)}, bf16[16,2560]{1,0:T(8,128)(2...) custom-call(bf16[16,4096]{1,0:T(8,128)(2,1)S(1)} %get-tuple-element., ...), custom_call_target="tpu_custom_call" | custom-call | flops 5536481280 | bytes 21626880 | tf_op jit(solution)/shard_map/pallas_call | solution.py:175
  71.9 1.2 %collective-permute-start.25 = (bf16[16,2560]{1,0:T(8,128)(2,1)S(1)}, bf16[16,2560]{1,0:T(8,128)(2,1)S(1)}, u32[]{:S(2)}, u32[]{:S(2)}) collective-permute-start(bf16[16,2560]{1,0:T(8,128)(2,1)S(1)} %get-tuple-element.69), channel_id=1, source_target_pairs={{0,1},{1,0},{2,3},{3,2},{4,5},{5,4},{6,7},{7,6},{8,9},{9,8},{10,11... | collective-permute-start | bytes 245768 | tf_op jit(solution)/shard_map/ppermute | solution.py:208
  73.1 1.3 %collective-permute-start.26 = (bf16[16,2560]{1,0:T(8,128)(2,1)S(1)}, bf16[16,2560]{1,0:T(8,128)(2,1)S(1)}, u32[]{:S(2)}, u32[]{:S(2)}) collective-permute-start(bf16[16,2560]{1,0:T(8,128)(2,1)S(1)} %get-tuple-element.70), channel_id=1, source_target_pairs={{0,2},{1,3},{2,0},{3,1},{4,6},{5,7},{6,4},{7,5},{8,10},{9,11},{10,... | collective-permute-start | bytes 245768 | tf_op jit(solution)/shard_map/ppermute | solution.py:208
  74.3 1.1 collective-permute-start.27
  75.4 0.5 collective-permute-start.28
  75.9 2.1 %collective-permute-start.29 = (bf16[16,2560]{1,0:T(8,128)(2,1)S(1)}, bf16[16,2560]{1,0:T(8,128)(2,1)S(1)}, u32[]{:S(2)}, u32[]{:S(2)}) collective-permute-start(bf16[16,2560]{1,0:T(8,128)(2,1)S(1)} %get-tuple-element.73), channel_id=1, source_target_pairs={{0,17},{1,16},{2,19},{3,18},{4,21},{5,20},{6,23},{7,22},{8,25},{9,... | collective-permute-start | bytes 245768 | tf_op jit(solution)/shard_map/ppermute | solution.py:208
  78.0 0.8 collective-permute-start.30
  78.8 2.5 %collective-permute-start.31 = (bf16[16,2560]{1,0:T(8,128)(2,1)S(1)}, bf16[16,2560]{1,0:T(8,128)(2,1)S(1)}, u32[]{:S(2)}, u32[]{:S(2)}) collective-permute-start(bf16[16,2560]{1,0:T(8,128)(2,1)S(1)} %get-tuple-element.75), channel_id=1, source_target_pairs={{0,19},{1,18},{2,17},{3,16},{4,23},{5,22},{6,21},{7,20},{8,27},{9,... | collective-permute-start | bytes 245768 | tf_op jit(solution)/shard_map/ppermute | solution.py:208
  81.3 1.1 %collective-permute-start.17 = (bf16[16,2560]{1,0:T(8,128)(2,1)S(1)}, bf16[16,2560]{1,0:T(8,128)(2,1)S(1)}, u32[]{:S(2)}, u32[]{:S(2)}) collective-permute-start(bf16[16,2560]{1,0:T(8,128)(2,1)S(1)} %get-tuple-element.58), channel_id=1, source_target_pairs={{0,1},{1,0},{2,3},{3,2},{4,5},{5,4},{6,7},{7,6},{8,9},{9,8},{10,11... | collective-permute-start | bytes 245768 | tf_op jit(solution)/shard_map/ppermute | solution.py:208
  82.4 1.3 %collective-permute-start.18 = (bf16[16,2560]{1,0:T(8,128)(2,1)S(1)}, bf16[16,2560]{1,0:T(8,128)(2,1)S(1)}, u32[]{:S(2)}, u32[]{:S(2)}) collective-permute-start(bf16[16,2560]{1,0:T(8,128)(2,1)S(1)} %get-tuple-element.59), channel_id=1, source_target_pairs={{0,2},{1,3},{2,0},{3,1},{4,6},{5,7},{6,4},{7,5},{8,10},{9,11},{10,... | collective-permute-start | bytes 245768 | tf_op jit(solution)/shard_map/ppermute | solution.py:208
  83.7 1.1 collective-permute-start.19
  84.8 0.3 collective-permute-done.31.refs_7_
  85.1 0.2 shard_map.127
  85.4 2.1 %collective-permute-start.20 = (bf16[16,2560]{1,0:T(8,128)(2,1)S(1)}, bf16[16,2560]{1,0:T(8,128)(2,1)S(1)}, u32[]{:S(2)}, u32[]{:S(2)}) collective-permute-start(bf16[16,2560]{1,0:T(8,128)(2,1)S(1)} %get-tuple-element.61), channel_id=1, source_target_pairs={{0,16},{1,17},{2,18},{3,19},{4,20},{5,21},{6,22},{7,23},{8,24},{9,... | collective-permute-start | bytes 245768 | tf_op jit(solution)/shard_map/ppermute | solution.py:208
  87.5 0.9 collective-permute-start.21
  88.4 1.6 %collective-permute-start.22 = (bf16[16,2560]{1,0:T(8,128)(2,1)S(1)}, bf16[16,2560]{1,0:T(8,128)(2,1)S(1)}, u32[]{:S(2)}, u32[]{:S(2)}) collective-permute-start(bf16[16,2560]{1,0:T(8,128)(2,1)S(1)} %get-tuple-element.63), channel_id=1, source_target_pairs={{0,18},{1,19},{2,16},{3,17},{4,22},{5,23},{6,20},{7,21},{8,26},{9,... | collective-permute-start | bytes 245768 | tf_op jit(solution)/shard_map/ppermute | solution.py:208
  89.9 1.5 %collective-permute-start.23 = (bf16[16,2560]{1,0:T(8,128)(2,1)S(1)}, bf16[16,2560]{1,0:T(8,128)(2,1)S(1)}, u32[]{:S(2)}, u32[]{:S(2)}) collective-permute-start(bf16[16,2560]{1,0:T(8,128)(2,1)S(1)} %get-tuple-element.64), channel_id=1, source_target_pairs={{0,19},{1,18},{2,17},{3,16},{4,23},{5,22},{6,21},{7,20},{8,27},{9,... | collective-permute-start | bytes 245768 | tf_op jit(solution)/shard_map/ppermute | solution.py:208
  91.4 3.7 %collective-permute-done.20.refs_4_ = bf16[16,2560]{1,0:T(8,128)(2,1)S(1)} collective-permute-done((bf16[16,2560]{1,0:T(8,128)(2,1)S(1)}, bf16[16,2560]{1,0:T(8,128)(2,1)S(1)}, u32[]{:S(2)}, u32[]{:S(2)}) %collective-permute-start.20) | collective-permute-done | bytes 81952 | tf_op jit(solution)/shard_map/ppermute | solution.py:208
  95.1 1.3 %collective-permute-done.23.refs_7_ = bf16[16,2560]{1,0:T(8,128)(2,1)S(1)} collective-permute-done((bf16[16,2560]{1,0:T(8,128)(2,1)S(1)}, bf16[16,2560]{1,0:T(8,128)(2,1)S(1)}, u32[]{:S(2)}, u32[]{:S(2)}) %collective-permute-start.23) | collective-permute-done | bytes 81952 | tf_op jit(solution)/shard_map/ppermute | solution.py:208
  96.8 3.2 %collective-permute-start.33 = (bf16[32,2560]{1,0:T(8,128)(2,1)S(1)}, bf16[32,2560]{1,0:T(8,128)(2,1)S(1)}, u32[]{:S(2)}, u32[]{:S(2)}) collective-permute-start(bf16[32,2560]{1,0:T(8,128)(2,1)S(1)} %shard_map.128), channel_id=1, source_target_pairs={{0,4},{1,5},{2,6},{3,7},{4,0},{5,1},{6,2},{7,3},{8,12},{9,13},{10,... | collective-permute-start | bytes 491528 | tf_op jit(solution)/shard_map/ppermute | solution.py:208
  100.0 8.4 %collective-permute-done.33.far_ref = bf16[32,2560]{1,0:T(8,128)(2,1)S(1)} collective-permute-done((bf16[32,2560]{1,0:T(8,128)(2,1)S(1)}, bf16[32,2560]{1,0:T(8,128)(2,1)S(1)}, u32[]{:S(2)}, u32[]{:S(2)}) %collective-permute-start.33) | collective-permute-done | bytes 163872 | tf_op jit(solution)/shard_map/ppermute | solution.py:208
  108.4 0.8 shard_map.129
  (43 shorter events, 0.7 us)
Async XLA Ops:
  0.6 0.9 copy-start.2
  1.5 0.9 copy-start.3
  2.4 0.7 copy-start.4
  3.1 0.7 copy-start.5
  3.9 16.4 %collective-permute-start.8 = (bf16[32,4224]{1,0:T(8,128)(2,1)S(1)}, bf16[32,4224]{1,0:T(8,128)(2,1)S(1)}, u32[]{:S(2)}, u32[]{:S(2)}) collective-permute-start(bf16[32,4224]{1,0:T(8,128)(2,1)S(1)} %shard_map.122.first_ref), channel_id=1, source_target_pairs={{0,4},{1,5},{2,6},{3,7},{4,0},{5,1},{6,2},{7,3},{8,12},{9,13},{10,... | collective-permute-start | bytes 811016 | tf_op jit(solution)/shard_map/ppermute | solution.py:208
  8.0 12.4 %collective-permute-start = (bf16[32,4224]{1,0:T(8,128)(2,1)S(1)}, bf16[32,4224]{1,0:T(8,128)(2,1)S(1)}, u32[]{:S(2)}, u32[]{:S(2)}) collective-permute-start(bf16[32,4224]{1,0:T(8,128)(2,1)S(1)} %shard_map.122.first_ref), channel_id=1, source_target_pairs={{0,8},{1,9},{2,10},{3,11},{4,12},{5,13},{6,14},{7,15},{8,0},{9,1},... | collective-permute-start | bytes 811016 | tf_op jit(solution)/shard_map/ppermute | solution.py:208
  20.2 6.4 %collective-permute-start.9 = (bf16[32,4224]{1,0:T(8,128)(2,1)S(1)}, bf16[32,4224]{1,0:T(8,128)(2,1)S(1)}, u32[]{:S(2)}, u32[]{:S(2)}) collective-permute-start(bf16[32,4224]{1,0:T(8,128)(2,1)S(1)} %collective-permute-done.8.first_ref), channel_id=1, source_target_pairs={{0,8},{1,9},{2,10},{3,11},{4,12},{5,13},{6,14},{7,15},{8,0},{9,1},... | collective-permute-start | bytes 811016 | tf_op jit(solution)/shard_map/ppermute | solution.py:208
  21.6 7.8 %collective-permute-start.1 = (bf16[16,4096]{1,0:T(8,128)(2,1)S(1)}, bf16[16,4096]{1,0:T(8,128)(2,1)S(1)}, u32[]{:S(2)}, u32[]{:S(2)}) collective-permute-start(bf16[16,4096]{1,0:T(8,128)(2,1)S(1)} %get-tuple-element.42), channel_id=1, source_target_pairs={{0,1},{1,0},{2,3},{3,2},{4,5},{5,4},{6,7},{7,6},{8,9},{9,8},{10,11... | collective-permute-start | bytes 393224 | tf_op jit(solution)/shard_map/ppermute | solution.py:208
  23.2 7.9 %collective-permute-start.2 = (bf16[16,4096]{1,0:T(8,128)(2,1)S(1)}, bf16[16,4096]{1,0:T(8,128)(2,1)S(1)}, u32[]{:S(2)}, u32[]{:S(2)}) collective-permute-start(bf16[16,4096]{1,0:T(8,128)(2,1)S(1)} %get-tuple-element.43), channel_id=1, source_target_pairs={{0,2},{1,3},{2,0},{3,1},{4,6},{5,7},{6,4},{7,5},{8,10},{9,11},{10,... | collective-permute-start | bytes 393224 | tf_op jit(solution)/shard_map/ppermute | solution.py:208
  23.8 8.4 %collective-permute-start.3 = (bf16[16,4096]{1,0:T(8,128)(2,1)S(1)}, bf16[16,4096]{1,0:T(8,128)(2,1)S(1)}, u32[]{:S(2)}, u32[]{:S(2)}) collective-permute-start(bf16[16,4096]{1,0:T(8,128)(2,1)S(1)} %get-tuple-element.44), channel_id=1, source_target_pairs={{0,3},{1,2},{2,1},{3,0},{4,7},{5,6},{6,5},{7,4},{8,11},{9,10},{10,... | collective-permute-start | bytes 393224 | tf_op jit(solution)/shard_map/ppermute | solution.py:208
  25.1 8.7 %collective-permute-start.4 = (bf16[16,4096]{1,0:T(8,128)(2,1)S(1)}, bf16[16,4096]{1,0:T(8,128)(2,1)S(1)}, u32[]{:S(2)}, u32[]{:S(2)}) collective-permute-start(bf16[16,4096]{1,0:T(8,128)(2,1)S(1)} %get-tuple-element.45), channel_id=1, source_target_pairs={{0,16},{1,17},{2,18},{3,19},{4,20},{5,21},{6,22},{7,23},{8,24},{9,... | collective-permute-start | bytes 393224 | tf_op jit(solution)/shard_map/ppermute | solution.py:208
  26.7 14.2 %collective-permute-start.5 = (bf16[16,4096]{1,0:T(8,128)(2,1)S(1)}, bf16[16,4096]{1,0:T(8,128)(2,1)S(1)}, u32[]{:S(2)}, u32[]{:S(2)}) collective-permute-start(bf16[16,4096]{1,0:T(8,128)(2,1)S(1)} %get-tuple-element.46), channel_id=1, source_target_pairs={{0,17},{1,16},{2,19},{3,18},{4,21},{5,20},{6,23},{7,22},{8,25},{9,... | collective-permute-start | bytes 393224 | tf_op jit(solution)/shard_map/ppermute | solution.py:208
  29.4 12.5 %collective-permute-start.6 = (bf16[16,4096]{1,0:T(8,128)(2,1)S(1)}, bf16[16,4096]{1,0:T(8,128)(2,1)S(1)}, u32[]{:S(2)}, u32[]{:S(2)}) collective-permute-start(bf16[16,4096]{1,0:T(8,128)(2,1)S(1)} %get-tuple-element.47), channel_id=1, source_target_pairs={{0,18},{1,19},{2,16},{3,17},{4,22},{5,23},{6,20},{7,21},{8,26},{9,... | collective-permute-start | bytes 393224 | tf_op jit(solution)/shard_map/ppermute | solution.py:208
  31.1 11.1 %collective-permute-start.7 = (bf16[16,4096]{1,0:T(8,128)(2,1)S(1)}, bf16[16,4096]{1,0:T(8,128)(2,1)S(1)}, u32[]{:S(2)}, u32[]{:S(2)}) collective-permute-start(bf16[16,4096]{1,0:T(8,128)(2,1)S(1)} %get-tuple-element.48), channel_id=1, source_target_pairs={{0,19},{1,18},{2,17},{3,16},{4,23},{5,22},{6,21},{7,20},{8,27},{9,... | collective-permute-start | bytes 393224 | tf_op jit(solution)/shard_map/ppermute | solution.py:208
  32.3 11.8 %collective-permute-start.10 = (bf16[16,4096]{1,0:T(8,128)(2,1)S(1)}, bf16[16,4096]{1,0:T(8,128)(2,1)S(1)}, u32[]{:S(2)}, u32[]{:S(2)}) collective-permute-start(bf16[16,4096]{1,0:T(8,128)(2,1)S(1)} %get-tuple-element.50), channel_id=1, source_target_pairs={{0,1},{1,0},{2,3},{3,2},{4,5},{5,4},{6,7},{7,6},{8,9},{9,8},{10,11... | collective-permute-start | bytes 393224 | tf_op jit(solution)/shard_map/ppermute | solution.py:208
  33.8 11.7 %collective-permute-start.11 = (bf16[16,4096]{1,0:T(8,128)(2,1)S(1)}, bf16[16,4096]{1,0:T(8,128)(2,1)S(1)}, u32[]{:S(2)}, u32[]{:S(2)}) collective-permute-start(bf16[16,4096]{1,0:T(8,128)(2,1)S(1)} %get-tuple-element.51), channel_id=1, source_target_pairs={{0,2},{1,3},{2,0},{3,1},{4,6},{5,7},{6,4},{7,5},{8,10},{9,11},{10,... | collective-permute-start | bytes 393224 | tf_op jit(solution)/shard_map/ppermute | solution.py:208
  40.9 6.8 %collective-permute-start.12 = (bf16[16,4096]{1,0:T(8,128)(2,1)S(1)}, bf16[16,4096]{1,0:T(8,128)(2,1)S(1)}, u32[]{:S(2)}, u32[]{:S(2)}) collective-permute-start(bf16[16,4096]{1,0:T(8,128)(2,1)S(1)} %get-tuple-element.52), channel_id=1, source_target_pairs={{0,3},{1,2},{2,1},{3,0},{4,7},{5,6},{6,5},{7,4},{8,11},{9,10},{10,... | collective-permute-start | bytes 393224 | tf_op jit(solution)/shard_map/ppermute | solution.py:208
  41.8 12.4 %collective-permute-start.13 = (bf16[16,4096]{1,0:T(8,128)(2,1)S(1)}, bf16[16,4096]{1,0:T(8,128)(2,1)S(1)}, u32[]{:S(2)}, u32[]{:S(2)}) collective-permute-start(bf16[16,4096]{1,0:T(8,128)(2,1)S(1)} %get-tuple-element.53), channel_id=1, source_target_pairs={{0,16},{1,17},{2,18},{3,19},{4,20},{5,21},{6,22},{7,23},{8,24},{9,... | collective-permute-start | bytes 393224 | tf_op jit(solution)/shard_map/ppermute | solution.py:208
  42.2 12.0 %collective-permute-start.14 = (bf16[16,4096]{1,0:T(8,128)(2,1)S(1)}, bf16[16,4096]{1,0:T(8,128)(2,1)S(1)}, u32[]{:S(2)}, u32[]{:S(2)}) collective-permute-start(bf16[16,4096]{1,0:T(8,128)(2,1)S(1)} %get-tuple-element.54), channel_id=1, source_target_pairs={{0,17},{1,16},{2,19},{3,18},{4,21},{5,20},{6,23},{7,22},{8,25},{9,... | collective-permute-start | bytes 393224 | tf_op jit(solution)/shard_map/ppermute | solution.py:208
  44.1 10.1 %collective-permute-start.15 = (bf16[16,4096]{1,0:T(8,128)(2,1)S(1)}, bf16[16,4096]{1,0:T(8,128)(2,1)S(1)}, u32[]{:S(2)}, u32[]{:S(2)}) collective-permute-start(bf16[16,4096]{1,0:T(8,128)(2,1)S(1)} %get-tuple-element.55), channel_id=1, source_target_pairs={{0,18},{1,19},{2,16},{3,17},{4,22},{5,23},{6,20},{7,21},{8,26},{9,... | collective-permute-start | bytes 393224 | tf_op jit(solution)/shard_map/ppermute | solution.py:208
  45.5 8.7 %collective-permute-start.16 = (bf16[16,4096]{1,0:T(8,128)(2,1)S(1)}, bf16[16,4096]{1,0:T(8,128)(2,1)S(1)}, u32[]{:S(2)}, u32[]{:S(2)}) collective-permute-start(bf16[16,4096]{1,0:T(8,128)(2,1)S(1)} %get-tuple-element.56), channel_id=1, source_target_pairs={{0,19},{1,18},{2,17},{3,16},{4,23},{5,22},{6,21},{7,20},{8,27},{9,... | collective-permute-start | bytes 393224 | tf_op jit(solution)/shard_map/ppermute | solution.py:208
  54.2 1.0 copy-start
  55.3 0.9 copy-start.1
  56.2 52.2 %copy-start.6 = (s32[1,32]{1,0:T(1,128)S(1)}, s32[1,32]{1,0:T(1,128)}, u32[]{:S(2)}) copy-start(s32[1,32]{1,0:T(1,128)} %query_ref.1) | copy-start | bytes 388
  71.9 6.2 %collective-permute-start.25 = (bf16[16,2560]{1,0:T(8,128)(2,1)S(1)}, bf16[16,2560]{1,0:T(8,128)(2,1)S(1)}, u32[]{:S(2)}, u32[]{:S(2)}) collective-permute-start(bf16[16,2560]{1,0:T(8,128)(2,1)S(1)} %get-tuple-element.69), channel_id=1, source_target_pairs={{0,1},{1,0},{2,3},{3,2},{4,5},{5,4},{6,7},{7,6},{8,9},{9,8},{10,11... | collective-permute-start | bytes 245768 | tf_op jit(solution)/shard_map/ppermute | solution.py:208
  73.1 5.7 %collective-permute-start.26 = (bf16[16,2560]{1,0:T(8,128)(2,1)S(1)}, bf16[16,2560]{1,0:T(8,128)(2,1)S(1)}, u32[]{:S(2)}, u32[]{:S(2)}) collective-permute-start(bf16[16,2560]{1,0:T(8,128)(2,1)S(1)} %get-tuple-element.70), channel_id=1, source_target_pairs={{0,2},{1,3},{2,0},{3,1},{4,6},{5,7},{6,4},{7,5},{8,10},{9,11},{10,... | collective-permute-start | bytes 245768 | tf_op jit(solution)/shard_map/ppermute | solution.py:208
  74.3 6.9 %collective-permute-start.27 = (bf16[16,2560]{1,0:T(8,128)(2,1)S(1)}, bf16[16,2560]{1,0:T(8,128)(2,1)S(1)}, u32[]{:S(2)}, u32[]{:S(2)}) collective-permute-start(bf16[16,2560]{1,0:T(8,128)(2,1)S(1)} %get-tuple-element.71), channel_id=1, source_target_pairs={{0,3},{1,2},{2,1},{3,0},{4,7},{5,6},{6,5},{7,4},{8,11},{9,10},{10,... | collective-permute-start | bytes 245768 | tf_op jit(solution)/shard_map/ppermute | solution.py:208
  75.4 7.0 %collective-permute-start.28 = (bf16[16,2560]{1,0:T(8,128)(2,1)S(1)}, bf16[16,2560]{1,0:T(8,128)(2,1)S(1)}, u32[]{:S(2)}, u32[]{:S(2)}) collective-permute-start(bf16[16,2560]{1,0:T(8,128)(2,1)S(1)} %get-tuple-element.72), channel_id=1, source_target_pairs={{0,16},{1,17},{2,18},{3,19},{4,20},{5,21},{6,22},{7,23},{8,24},{9,... | collective-permute-start | bytes 245768 | tf_op jit(solution)/shard_map/ppermute | solution.py:208
  75.9 7.8 %collective-permute-start.29 = (bf16[16,2560]{1,0:T(8,128)(2,1)S(1)}, bf16[16,2560]{1,0:T(8,128)(2,1)S(1)}, u32[]{:S(2)}, u32[]{:S(2)}) collective-permute-start(bf16[16,2560]{1,0:T(8,128)(2,1)S(1)} %get-tuple-element.73), channel_id=1, source_target_pairs={{0,17},{1,16},{2,19},{3,18},{4,21},{5,20},{6,23},{7,22},{8,25},{9,... | collective-permute-start | bytes 245768 | tf_op jit(solution)/shard_map/ppermute | solution.py:208
  78.0 6.8 %collective-permute-start.30 = (bf16[16,2560]{1,0:T(8,128)(2,1)S(1)}, bf16[16,2560]{1,0:T(8,128)(2,1)S(1)}, u32[]{:S(2)}, u32[]{:S(2)}) collective-permute-start(bf16[16,2560]{1,0:T(8,128)(2,1)S(1)} %get-tuple-element.74), channel_id=1, source_target_pairs={{0,18},{1,19},{2,16},{3,17},{4,22},{5,23},{6,20},{7,21},{8,26},{9,... | collective-permute-start | bytes 245768 | tf_op jit(solution)/shard_map/ppermute | solution.py:208
  78.8 6.3 %collective-permute-start.31 = (bf16[16,2560]{1,0:T(8,128)(2,1)S(1)}, bf16[16,2560]{1,0:T(8,128)(2,1)S(1)}, u32[]{:S(2)}, u32[]{:S(2)}) collective-permute-start(bf16[16,2560]{1,0:T(8,128)(2,1)S(1)} %get-tuple-element.75), channel_id=1, source_target_pairs={{0,19},{1,18},{2,17},{3,16},{4,23},{5,22},{6,21},{7,20},{8,27},{9,... | collective-permute-start | bytes 245768 | tf_op jit(solution)/shard_map/ppermute | solution.py:208
  81.3 6.2 %collective-permute-start.17 = (bf16[16,2560]{1,0:T(8,128)(2,1)S(1)}, bf16[16,2560]{1,0:T(8,128)(2,1)S(1)}, u32[]{:S(2)}, u32[]{:S(2)}) collective-permute-start(bf16[16,2560]{1,0:T(8,128)(2,1)S(1)} %get-tuple-element.58), channel_id=1, source_target_pairs={{0,1},{1,0},{2,3},{3,2},{4,5},{5,4},{6,7},{7,6},{8,9},{9,8},{10,11... | collective-permute-start | bytes 245768 | tf_op jit(solution)/shard_map/ppermute | solution.py:208
  82.4 5.9 %collective-permute-start.18 = (bf16[16,2560]{1,0:T(8,128)(2,1)S(1)}, bf16[16,2560]{1,0:T(8,128)(2,1)S(1)}, u32[]{:S(2)}, u32[]{:S(2)}) collective-permute-start(bf16[16,2560]{1,0:T(8,128)(2,1)S(1)} %get-tuple-element.59), channel_id=1, source_target_pairs={{0,2},{1,3},{2,0},{3,1},{4,6},{5,7},{6,4},{7,5},{8,10},{9,11},{10,... | collective-permute-start | bytes 245768 | tf_op jit(solution)/shard_map/ppermute | solution.py:208
  83.7 6.2 %collective-permute-start.19 = (bf16[16,2560]{1,0:T(8,128)(2,1)S(1)}, bf16[16,2560]{1,0:T(8,128)(2,1)S(1)}, u32[]{:S(2)}, u32[]{:S(2)}) collective-permute-start(bf16[16,2560]{1,0:T(8,128)(2,1)S(1)} %get-tuple-element.60), channel_id=1, source_target_pairs={{0,3},{1,2},{2,1},{3,0},{4,7},{5,6},{6,5},{7,4},{8,11},{9,10},{10,... | collective-permute-start | bytes 245768 | tf_op jit(solution)/shard_map/ppermute | solution.py:208
  85.3 11.4 %collective-permute-start.32 = (bf16[32,2560]{1,0:T(8,128)(2,1)S(1)}, bf16[32,2560]{1,0:T(8,128)(2,1)S(1)}, u32[]{:S(2)}, u32[]{:S(2)}) collective-permute-start(bf16[32,2560]{1,0:T(8,128)(2,1)S(1)} %get-tuple-element.77), channel_id=1, source_target_pairs={{0,8},{1,9},{2,10},{3,11},{4,12},{5,13},{6,14},{7,15},{8,0},{9,1},... | collective-permute-start | bytes 491528 | tf_op jit(solution)/shard_map/ppermute | solution.py:208
  85.4 9.7 %collective-permute-start.20 = (bf16[16,2560]{1,0:T(8,128)(2,1)S(1)}, bf16[16,2560]{1,0:T(8,128)(2,1)S(1)}, u32[]{:S(2)}, u32[]{:S(2)}) collective-permute-start(bf16[16,2560]{1,0:T(8,128)(2,1)S(1)} %get-tuple-element.61), channel_id=1, source_target_pairs={{0,16},{1,17},{2,18},{3,19},{4,20},{5,21},{6,22},{7,23},{8,24},{9,... | collective-permute-start | bytes 245768 | tf_op jit(solution)/shard_map/ppermute | solution.py:208
  87.5 7.6 %collective-permute-start.21 = (bf16[16,2560]{1,0:T(8,128)(2,1)S(1)}, bf16[16,2560]{1,0:T(8,128)(2,1)S(1)}, u32[]{:S(2)}, u32[]{:S(2)}) collective-permute-start(bf16[16,2560]{1,0:T(8,128)(2,1)S(1)} %get-tuple-element.62), channel_id=1, source_target_pairs={{0,17},{1,16},{2,19},{3,18},{4,21},{5,20},{6,23},{7,22},{8,25},{9,... | collective-permute-start | bytes 245768 | tf_op jit(solution)/shard_map/ppermute | solution.py:208
  88.4 6.7 %collective-permute-start.22 = (bf16[16,2560]{1,0:T(8,128)(2,1)S(1)}, bf16[16,2560]{1,0:T(8,128)(2,1)S(1)}, u32[]{:S(2)}, u32[]{:S(2)}) collective-permute-start(bf16[16,2560]{1,0:T(8,128)(2,1)S(1)} %get-tuple-element.63), channel_id=1, source_target_pairs={{0,18},{1,19},{2,16},{3,17},{4,22},{5,23},{6,20},{7,21},{8,26},{9,... | collective-permute-start | bytes 245768 | tf_op jit(solution)/shard_map/ppermute | solution.py:208
  89.9 6.4 %collective-permute-start.23 = (bf16[16,2560]{1,0:T(8,128)(2,1)S(1)}, bf16[16,2560]{1,0:T(8,128)(2,1)S(1)}, u32[]{:S(2)}, u32[]{:S(2)}) collective-permute-start(bf16[16,2560]{1,0:T(8,128)(2,1)S(1)} %get-tuple-element.64), channel_id=1, source_target_pairs={{0,19},{1,18},{2,17},{3,16},{4,23},{5,22},{6,21},{7,20},{8,27},{9,... | collective-permute-start | bytes 245768 | tf_op jit(solution)/shard_map/ppermute | solution.py:208
  96.6 3.4 %collective-permute-start.24 = (bf16[32,2560]{1,0:T(8,128)(2,1)S(1)}, bf16[32,2560]{1,0:T(8,128)(2,1)S(1)}, u32[]{:S(2)}, u32[]{:S(2)}) collective-permute-start(bf16[32,2560]{1,0:T(8,128)(2,1)S(1)} %get-tuple-element.66), channel_id=1, source_target_pairs={{0,8},{1,9},{2,10},{3,11},{4,12},{5,13},{6,14},{7,15},{8,0},{9,1},... | collective-permute-start | bytes 491528 | tf_op jit(solution)/shard_map/ppermute | solution.py:208
  96.8 11.6 %collective-permute-start.33 = (bf16[32,2560]{1,0:T(8,128)(2,1)S(1)}, bf16[32,2560]{1,0:T(8,128)(2,1)S(1)}, u32[]{:S(2)}, u32[]{:S(2)}) collective-permute-start(bf16[32,2560]{1,0:T(8,128)(2,1)S(1)} %shard_map.128), channel_id=1, source_target_pairs={{0,4},{1,5},{2,6},{3,7},{4,0},{5,1},{6,2},{7,3},{8,12},{9,13},{10,... | collective-permute-start | bytes 491528 | tf_op jit(solution)/shard_map/ppermute | solution.py:208

commit v3 on v2

--- a/solution.py
+++ b/solution.py
@@ -25,15 +25,23 @@
     return lax.dot_general(a, b, NT, preferred_element_type=F32)
 
 
-def pay_kernel(ids_ref, w_ref, x_ref, g_ref, pay_ref):
+def pay_kernel(ids_hbm, w_hbm, x_hbm, g_hbm, pay_ref, ids_ref, w_ref, x_ref, g_ref, sem):
     top, tok = ids_ref.shape
     width = x_ref.shape[1]
+    pairs = ((ids_hbm, ids_ref), (w_hbm, w_ref), (x_hbm, x_ref), (g_hbm, g_ref))
+    copies = [pltpu.make_async_copy(a, b, sem.at[i]) for i, (a, b) in enumerate(pairs)]
+    for copy in copies:
+        copy.start()
+    copies[0].wait()
+    copies[1].wait()
     flat = jnp.concatenate([ids_ref[...].astype(F32), w_ref[...].astype(F32)], axis=0)
     flat = jnp.concatenate([flat, jnp.zeros((LANES - 2 * top, tok), F32)], axis=0)
     flat = jnp.concatenate([flat, jnp.zeros((LANES, LANES - tok), F32)], axis=1)
+    pay_ref[:, 2 * width :] = flat.T[:tok, :].astype(BF16)
+    copies[2].wait()
     pay_ref[:, :width] = x_ref[...]
+    copies[3].wait()
     pay_ref[:, width : 2 * width] = g_ref[...]
-    pay_ref[:, 2 * width :] = flat.T[:tok, :].astype(BF16)
 
 
 def pack_kernel(top, experts, capacity, deep, here_ref, first_ref, second_ref, *outs):
@@ -171,6 +179,10 @@
 HBM = pl.BlockSpec(memory_space=pltpu.HBM)
 
 
+def in_hbm(value):
+    return pltpu.with_memory_space_constraint(value, pltpu.HBM)
+
+
 def call(kernel, outs, in_specs, args, scratch=(), flops=1_000_000, moved=1_000_000, limit=8 << 20):
     return pl.pallas_call(
         kernel,
@@ -185,6 +197,7 @@
 
 def layer(tokens, out_grad, expert_ids, gate_w, query_ids, *weights):
     weights = weights[:3] + tuple(w.transpose(0, 2, 1) for w in weights[3:5]) + weights[5:]
+    weights = tuple(in_hbm(w) for w in weights)
     tok, width = tokens.shape
     top = expert_ids.shape[1]
     experts = weights[0].shape[0]
@@ -223,11 +236,14 @@
         outs = (shape((tok, width + train), F32), shape((tok, width + train), BF16))
         return call(part_kernel, outs, [VMEM] * (1 + chips), (place, *pieces))
 
+    inputs = tuple(in_hbm(v) for v in (expert_ids.T, gate_w.T, tokens, out_grad))
     pay = call(
         pay_kernel,
         shape((tok, 2 * width + LANES), BF16),
-        [VMEM] * 4,
-        (expert_ids.T, gate_w.T, tokens, out_grad),
+        [HBM] * 4,
+        inputs,
+        scratch=[pltpu.VMEM(v.shape, v.dtype) for v in inputs]
+        + [pltpu.SemaphoreType.DMA((len(inputs),))],
     )
     guest = swap(pay, half=1)
     other = swap(pay, core=1)

time: 109 us -> 105 us (0.963)
  local copies, waits for them, and re-layouts: 5.1 us -> 0.01 us
    unnamed x14 -> x2, local copies, waits for them, and re-layouts: 5.1 us -> 0.01 us
where the time goes in v3:
time: 105 us
  starting transfers between devices  45.1 us (43%)
  waiting for transfers between devices  38.6 us (37%)
  Pallas kernels  20.5 us (20%)
    ppermute x34, starting transfers between devices, swap(): return lax.ppermute(value, AXES, pairs)  45.1 us
    ppermute x34, waiting for transfers between devices, swap(): return lax.ppermute(value, AXES, pairs)  38.6 us
    pallas_call x8, Pallas kernels, call(): pl.pallas_call(kernel, out_shape=outs, in_specs=in_specs, out_specs=jax.t...  20.5 us
  transfers between devices with their start and end apart: 34, of which 7 were waited for; matrix products, arithmetic and copies ran while one was open for 0% of the time, Pallas kernels for 3%

profile of v3, /device:TPU:0, one launch (start us, length us, event | category | flops | bytes accessed | tf_op | source)
XLA Modules:
  0.0 105.1 jit_solution(15493556597175327037)
XLA Ops:
  0.6 1.0 shard_map.122.first_ref
  1.7 4.1 %collective-permute-start.8 = (bf16[32,4224]{1,0:T(8,128)(2,1)S(1)}, bf16[32,4224]{1,0:T(8,128)(2,1)S(1)}, u32[]{:S(2)}, u32[]{:S(2)}) collective-permute-start(bf16[32,4224]{1,0:T(8,128)(2,1)S(1)} %shard_map.122.first_ref), channel_id=1, source_target_pairs={{0,4},{1,5},{2,6},{3,7},{4,0},{5,1},{6,2},{7,3},{8,12},{9,13},{10,... | collective-permute-start | bytes 811016 | tf_op jit(solution)/shard_map/ppermute | solution.py:221
  5.8 12.3 %collective-permute-done.8.first_ref = bf16[32,4224]{1,0:T(8,128)(2,1)S(1)} collective-permute-done((bf16[32,4224]{1,0:T(8,128)(2,1)S(1)}, bf16[32,4224]{1,0:T(8,128)(2,1)S(1)}, u32[]{:S(2)}, u32[]{:S(2)}) %collective-permute-start.8) | collective-permute-done | bytes 270368 | tf_op jit(solution)/shard_map/ppermute | solution.py:221
  18.1 0.1 pad_add_fusion.here_ref
  18.2 1.2 %shard_map.123 = (bf16[16,4096]{1,0:T(8,128)(2,1)S(1)}, bf16[16,4096]{1,0:T(8,128)(2,1)S(1)}, bf16[16,4096]{1,0:T(8,128)(2,1)S(1)}, bf16[16,4096]{1,0:T(8,128)(2...) custom-call(s32[4]{0:T(128)S(1)} %pad_add_fusion.here_ref, ...), custom_call_target="tpu_custom_call" | custom-call | flops 1000000 | bytes 1000000 | tf_op jit(solution)/shard_map/pallas_call | solution.py:187
  19.4 1.6 %collective-permute-start.1 = (bf16[16,4096]{1,0:T(8,128)(2,1)S(1)}, bf16[16,4096]{1,0:T(8,128)(2,1)S(1)}, u32[]{:S(2)}, u32[]{:S(2)}) collective-permute-start(bf16[16,4096]{1,0:T(8,128)(2,1)S(1)} %get-tuple-element.42), channel_id=1, source_target_pairs={{0,1},{1,0},{2,3},{3,2},{4,5},{5,4},{6,7},{7,6},{8,9},{9,8},{10,11... | collective-permute-start | bytes 393224 | tf_op jit(solution)/shard_map/ppermute | solution.py:221
  21.0 0.7 collective-permute-start.2
  21.7 1.3 %collective-permute-start.3 = (bf16[16,4096]{1,0:T(8,128)(2,1)S(1)}, bf16[16,4096]{1,0:T(8,128)(2,1)S(1)}, u32[]{:S(2)}, u32[]{:S(2)}) collective-permute-start(bf16[16,4096]{1,0:T(8,128)(2,1)S(1)} %get-tuple-element.44), channel_id=1, source_target_pairs={{0,3},{1,2},{2,1},{3,0},{4,7},{5,6},{6,5},{7,4},{8,11},{9,10},{10,... | collective-permute-start | bytes 393224 | tf_op jit(solution)/shard_map/ppermute | solution.py:221
  23.0 1.6 %collective-permute-start.4 = (bf16[16,4096]{1,0:T(8,128)(2,1)S(1)}, bf16[16,4096]{1,0:T(8,128)(2,1)S(1)}, u32[]{:S(2)}, u32[]{:S(2)}) collective-permute-start(bf16[16,4096]{1,0:T(8,128)(2,1)S(1)} %get-tuple-element.45), channel_id=1, source_target_pairs={{0,16},{1,17},{2,18},{3,19},{4,20},{5,21},{6,22},{7,23},{8,24},{9,... | collective-permute-start | bytes 393224 | tf_op jit(solution)/shard_map/ppermute | solution.py:221
  24.5 1.4 %collective-permute-start.5 = (bf16[16,4096]{1,0:T(8,128)(2,1)S(1)}, bf16[16,4096]{1,0:T(8,128)(2,1)S(1)}, u32[]{:S(2)}, u32[]{:S(2)}) collective-permute-start(bf16[16,4096]{1,0:T(8,128)(2,1)S(1)} %get-tuple-element.46), channel_id=1, source_target_pairs={{0,17},{1,16},{2,19},{3,18},{4,21},{5,20},{6,23},{7,22},{8,25},{9,... | collective-permute-start | bytes 393224 | tf_op jit(solution)/shard_map/ppermute | solution.py:221
  26.0 1.2 %shard_map.124 = (bf16[16,4096]{1,0:T(8,128)(2,1)S(1)}, bf16[16,4096]{1,0:T(8,128)(2,1)S(1)}, bf16[16,4096]{1,0:T(8,128)(2,1)S(1)}, bf16[16,4096]{1,0:T(8,128)(2...) custom-call(s32[4]{0:T(128)S(1)} %pad_add_fusion.here_ref, ...), custom_call_target="tpu_custom_call" | custom-call | flops 1000000 | bytes 1000000 | tf_op jit(solution)/shard_map/pallas_call | solution.py:187
  27.2 1.7 %collective-permute-start.6 = (bf16[16,4096]{1,0:T(8,128)(2,1)S(1)}, bf16[16,4096]{1,0:T(8,128)(2,1)S(1)}, u32[]{:S(2)}, u32[]{:S(2)}) collective-permute-start(bf16[16,4096]{1,0:T(8,128)(2,1)S(1)} %get-tuple-element.47), channel_id=1, source_target_pairs={{0,18},{1,19},{2,16},{3,17},{4,22},{5,23},{6,20},{7,21},{8,26},{9,... | collective-permute-start | bytes 393224 | tf_op jit(solution)/shard_map/ppermute | solution.py:221
  28.9 1.2 %collective-permute-start.7 = (bf16[16,4096]{1,0:T(8,128)(2,1)S(1)}, bf16[16,4096]{1,0:T(8,128)(2,1)S(1)}, u32[]{:S(2)}, u32[]{:S(2)}) collective-permute-start(bf16[16,4096]{1,0:T(8,128)(2,1)S(1)} %get-tuple-element.48), channel_id=1, source_target_pairs={{0,19},{1,18},{2,17},{3,16},{4,23},{5,22},{6,21},{7,20},{8,27},{9,... | collective-permute-start | bytes 393224 | tf_op jit(solution)/shard_map/ppermute | solution.py:221
  30.1 1.5 %collective-permute-start.10 = (bf16[16,4096]{1,0:T(8,128)(2,1)S(1)}, bf16[16,4096]{1,0:T(8,128)(2,1)S(1)}, u32[]{:S(2)}, u32[]{:S(2)}) collective-permute-start(bf16[16,4096]{1,0:T(8,128)(2,1)S(1)} %get-tuple-element.50), channel_id=1, source_target_pairs={{0,1},{1,0},{2,3},{3,2},{4,5},{5,4},{6,7},{7,6},{8,9},{9,8},{10,11... | collective-permute-start | bytes 393224 | tf_op jit(solution)/shard_map/ppermute | solution.py:221
  31.7 0.7 collective-permute-start.11
  32.4 6.4 %collective-permute-done.5.refs_5_ = bf16[16,4096]{1,0:T(8,128)(2,1)S(1)} collective-permute-done((bf16[16,4096]{1,0:T(8,128)(2,1)S(1)}, bf16[16,4096]{1,0:T(8,128)(2,1)S(1)}, u32[]{:S(2)}, u32[]{:S(2)}) %collective-permute-start.5) | collective-permute-done | bytes 131104 | tf_op jit(solution)/shard_map/ppermute | solution.py:221
  38.8 0.9 collective-permute-start.12
  39.7 0.4 collective-permute-start.13
  40.0 1.9 %collective-permute-start.14 = (bf16[16,4096]{1,0:T(8,128)(2,1)S(1)}, bf16[16,4096]{1,0:T(8,128)(2,1)S(1)}, u32[]{:S(2)}, u32[]{:S(2)}) collective-permute-start(bf16[16,4096]{1,0:T(8,128)(2,1)S(1)} %get-tuple-element.54), channel_id=1, source_target_pairs={{0,17},{1,16},{2,19},{3,18},{4,21},{5,20},{6,23},{7,22},{8,25},{9,... | collective-permute-start | bytes 393224 | tf_op jit(solution)/shard_map/ppermute | solution.py:221
  41.9 1.5 %collective-permute-start.15 = (bf16[16,4096]{1,0:T(8,128)(2,1)S(1)}, bf16[16,4096]{1,0:T(8,128)(2,1)S(1)}, u32[]{:S(2)}, u32[]{:S(2)}) collective-permute-start(bf16[16,4096]{1,0:T(8,128)(2,1)S(1)} %get-tuple-element.55), channel_id=1, source_target_pairs={{0,18},{1,19},{2,16},{3,17},{4,22},{5,23},{6,20},{7,21},{8,26},{9,... | collective-permute-start | bytes 393224 | tf_op jit(solution)/shard_map/ppermute | solution.py:221
  43.4 2.1 %collective-permute-start.16 = (bf16[16,4096]{1,0:T(8,128)(2,1)S(1)}, bf16[16,4096]{1,0:T(8,128)(2,1)S(1)}, u32[]{:S(2)}, u32[]{:S(2)}) collective-permute-start(bf16[16,4096]{1,0:T(8,128)(2,1)S(1)} %get-tuple-element.56), channel_id=1, source_target_pairs={{0,19},{1,18},{2,17},{3,16},{4,23},{5,22},{6,21},{7,20},{8,27},{9,... | collective-permute-start | bytes 393224 | tf_op jit(solution)/shard_map/ppermute | solution.py:221
  45.5 6.3 %collective-permute-done.13.refs_12_ = bf16[16,4096]{1,0:T(8,128)(2,1)S(1)} collective-permute-done((bf16[16,4096]{1,0:T(8,128)(2,1)S(1)}, bf16[16,4096]{1,0:T(8,128)(2,1)S(1)}, u32[]{:S(2)}, u32[]{:S(2)}) %collective-permute-start.13) | collective-permute-done | bytes 131104 | tf_op jit(solution)/shard_map/ppermute | solution.py:221
  51.8 0.0 copy-start
  51.9 15.7 %shard_map.125 = (bf16[16,2560]{1,0:T(8,128)(2,1)S(1)}, bf16[16,2560]{1,0:T(8,128)(2,1)S(1)}, bf16[16,2560]{1,0:T(8,128)(2,1)S(1)}, bf16[16,2560]{1,0:T(8,128)(2...) custom-call(bf16[16,4096]{1,0:T(8,128)(2,1)S(1)} %get-tuple-element., ...), custom_call_target="tpu_custom_call" | custom-call | flops 5536481280 | bytes 21626880 | tf_op jit(solution)/shard_map/pallas_call | solution.py:187
  67.6 1.4 %collective-permute-start.25 = (bf16[16,2560]{1,0:T(8,128)(2,1)S(1)}, bf16[16,2560]{1,0:T(8,128)(2,1)S(1)}, u32[]{:S(2)}, u32[]{:S(2)}) collective-permute-start(bf16[16,2560]{1,0:T(8,128)(2,1)S(1)} %get-tuple-element.69), channel_id=1, source_target_pairs={{0,1},{1,0},{2,3},{3,2},{4,5},{5,4},{6,7},{7,6},{8,9},{9,8},{10,11... | collective-permute-start | bytes 245768 | tf_op jit(solution)/shard_map/ppermute | solution.py:221
  69.0 1.8 %collective-permute-start.26 = (bf16[16,2560]{1,0:T(8,128)(2,1)S(1)}, bf16[16,2560]{1,0:T(8,128)(2,1)S(1)}, u32[]{:S(2)}, u32[]{:S(2)}) collective-permute-start(bf16[16,2560]{1,0:T(8,128)(2,1)S(1)} %get-tuple-element.70), channel_id=1, source_target_pairs={{0,2},{1,3},{2,0},{3,1},{4,6},{5,7},{6,4},{7,5},{8,10},{9,11},{10,... | collective-permute-start | bytes 245768 | tf_op jit(solution)/shard_map/ppermute | solution.py:221
  70.8 0.4 collective-permute-start.27
  71.2 1.5 %collective-permute-start.28 = (bf16[16,2560]{1,0:T(8,128)(2,1)S(1)}, bf16[16,2560]{1,0:T(8,128)(2,1)S(1)}, u32[]{:S(2)}, u32[]{:S(2)}) collective-permute-start(bf16[16,2560]{1,0:T(8,128)(2,1)S(1)} %get-tuple-element.72), channel_id=1, source_target_pairs={{0,16},{1,17},{2,18},{3,19},{4,20},{5,21},{6,22},{7,23},{8,24},{9,... | collective-permute-start | bytes 245768 | tf_op jit(solution)/shard_map/ppermute | solution.py:221
  72.7 1.3 %collective-permute-start.29 = (bf16[16,2560]{1,0:T(8,128)(2,1)S(1)}, bf16[16,2560]{1,0:T(8,128)(2,1)S(1)}, u32[]{:S(2)}, u32[]{:S(2)}) collective-permute-start(bf16[16,2560]{1,0:T(8,128)(2,1)S(1)} %get-tuple-element.73), channel_id=1, source_target_pairs={{0,17},{1,16},{2,19},{3,18},{4,21},{5,20},{6,23},{7,22},{8,25},{9,... | collective-permute-start | bytes 245768 | tf_op jit(solution)/shard_map/ppermute | solution.py:221
  73.9 1.9 %collective-permute-start.30 = (bf16[16,2560]{1,0:T(8,128)(2,1)S(1)}, bf16[16,2560]{1,0:T(8,128)(2,1)S(1)}, u32[]{:S(2)}, u32[]{:S(2)}) collective-permute-start(bf16[16,2560]{1,0:T(8,128)(2,1)S(1)} %get-tuple-element.74), channel_id=1, source_target_pairs={{0,18},{1,19},{2,16},{3,17},{4,22},{5,23},{6,20},{7,21},{8,26},{9,... | collective-permute-start | bytes 245768 | tf_op jit(solution)/shard_map/ppermute | solution.py:221
  75.8 1.2 %collective-permute-start.31 = (bf16[16,2560]{1,0:T(8,128)(2,1)S(1)}, bf16[16,2560]{1,0:T(8,128)(2,1)S(1)}, u32[]{:S(2)}, u32[]{:S(2)}) collective-permute-start(bf16[16,2560]{1,0:T(8,128)(2,1)S(1)} %get-tuple-element.75), channel_id=1, source_target_pairs={{0,19},{1,18},{2,17},{3,16},{4,23},{5,22},{6,21},{7,20},{8,27},{9,... | collective-permute-start | bytes 245768 | tf_op jit(solution)/shard_map/ppermute | solution.py:221
  77.0 1.3 %collective-permute-start.17 = (bf16[16,2560]{1,0:T(8,128)(2,1)S(1)}, bf16[16,2560]{1,0:T(8,128)(2,1)S(1)}, u32[]{:S(2)}, u32[]{:S(2)}) collective-permute-start(bf16[16,2560]{1,0:T(8,128)(2,1)S(1)} %get-tuple-element.58), channel_id=1, source_target_pairs={{0,1},{1,0},{2,3},{3,2},{4,5},{5,4},{6,7},{7,6},{8,9},{9,8},{10,11... | collective-permute-start | bytes 245768 | tf_op jit(solution)/shard_map/ppermute | solution.py:221
  78.3 1.8 %collective-permute-start.18 = (bf16[16,2560]{1,0:T(8,128)(2,1)S(1)}, bf16[16,2560]{1,0:T(8,128)(2,1)S(1)}, u32[]{:S(2)}, u32[]{:S(2)}) collective-permute-start(bf16[16,2560]{1,0:T(8,128)(2,1)S(1)} %get-tuple-element.59), channel_id=1, source_target_pairs={{0,2},{1,3},{2,0},{3,1},{4,6},{5,7},{6,4},{7,5},{8,10},{9,11},{10,... | collective-permute-start | bytes 245768 | tf_op jit(solution)/shard_map/ppermute | solution.py:221
  80.1 1.2 %collective-permute-start.19 = (bf16[16,2560]{1,0:T(8,128)(2,1)S(1)}, bf16[16,2560]{1,0:T(8,128)(2,1)S(1)}, u32[]{:S(2)}, u32[]{:S(2)}) collective-permute-start(bf16[16,2560]{1,0:T(8,128)(2,1)S(1)} %get-tuple-element.60), channel_id=1, source_target_pairs={{0,3},{1,2},{2,1},{3,0},{4,7},{5,6},{6,5},{7,4},{8,11},{9,10},{10,... | collective-permute-start | bytes 245768 | tf_op jit(solution)/shard_map/ppermute | solution.py:221
  81.4 0.7 collective-permute-done.31.refs_7_
  82.1 0.2 shard_map.127
  82.3 0.1 collective-permute-start.32
  82.4 1.5 %collective-permute-start.20 = (bf16[16,2560]{1,0:T(8,128)(2,1)S(1)}, bf16[16,2560]{1,0:T(8,128)(2,1)S(1)}, u32[]{:S(2)}, u32[]{:S(2)}) collective-permute-start(bf16[16,2560]{1,0:T(8,128)(2,1)S(1)} %get-tuple-element.61), channel_id=1, source_target_pairs={{0,16},{1,17},{2,18},{3,19},{4,20},{5,21},{6,22},{7,23},{8,24},{9,... | collective-permute-start | bytes 245768 | tf_op jit(solution)/shard_map/ppermute | solution.py:221
  83.9 0.4 collective-permute-start.21
  84.3 1.4 %collective-permute-start.22 = (bf16[16,2560]{1,0:T(8,128)(2,1)S(1)}, bf16[16,2560]{1,0:T(8,128)(2,1)S(1)}, u32[]{:S(2)}, u32[]{:S(2)}) collective-permute-start(bf16[16,2560]{1,0:T(8,128)(2,1)S(1)} %get-tuple-element.63), channel_id=1, source_target_pairs={{0,18},{1,19},{2,16},{3,17},{4,22},{5,23},{6,20},{7,21},{8,26},{9,... | collective-permute-start | bytes 245768 | tf_op jit(solution)/shard_map/ppermute | solution.py:221
  85.7 2.7 %collective-permute-start.23 = (bf16[16,2560]{1,0:T(8,128)(2,1)S(1)}, bf16[16,2560]{1,0:T(8,128)(2,1)S(1)}, u32[]{:S(2)}, u32[]{:S(2)}) collective-permute-start(bf16[16,2560]{1,0:T(8,128)(2,1)S(1)} %get-tuple-element.64), channel_id=1, source_target_pairs={{0,19},{1,18},{2,17},{3,16},{4,23},{5,22},{6,21},{7,20},{8,27},{9,... | collective-permute-start | bytes 245768 | tf_op jit(solution)/shard_map/ppermute | solution.py:221
  88.4 2.3 %collective-permute-done.20.refs_4_ = bf16[16,2560]{1,0:T(8,128)(2,1)S(1)} collective-permute-done((bf16[16,2560]{1,0:T(8,128)(2,1)S(1)}, bf16[16,2560]{1,0:T(8,128)(2,1)S(1)}, u32[]{:S(2)}, u32[]{:S(2)}) %collective-permute-start.20) | collective-permute-done | bytes 81952 | tf_op jit(solution)/shard_map/ppermute | solution.py:221
  90.6 2.2 %collective-permute-done.21.refs_5_ = bf16[16,2560]{1,0:T(8,128)(2,1)S(1)} collective-permute-done((bf16[16,2560]{1,0:T(8,128)(2,1)S(1)}, bf16[16,2560]{1,0:T(8,128)(2,1)S(1)}, u32[]{:S(2)}, u32[]{:S(2)}) %collective-permute-start.21) | collective-permute-done | bytes 81952 | tf_op jit(solution)/shard_map/ppermute | solution.py:221
  92.8 0.2 shard_map.126
  93.1 0.1 collective-permute-start.24
  93.2 2.8 %collective-permute-start.33 = (bf16[32,2560]{1,0:T(8,128)(2,1)S(1)}, bf16[32,2560]{1,0:T(8,128)(2,1)S(1)}, u32[]{:S(2)}, u32[]{:S(2)}) collective-permute-start(bf16[32,2560]{1,0:T(8,128)(2,1)S(1)} %shard_map.128), channel_id=1, source_target_pairs={{0,4},{1,5},{2,6},{3,7},{4,0},{5,1},{6,2},{7,3},{8,12},{9,13},{10,... | collective-permute-start | bytes 491528 | tf_op jit(solution)/shard_map/ppermute | solution.py:221
  96.0 8.4 %collective-permute-done.33.far_ref = bf16[32,2560]{1,0:T(8,128)(2,1)S(1)} collective-permute-done((bf16[32,2560]{1,0:T(8,128)(2,1)S(1)}, bf16[32,2560]{1,0:T(8,128)(2,1)S(1)}, u32[]{:S(2)}, u32[]{:S(2)}) %collective-permute-start.33) | collective-permute-done | bytes 163872 | tf_op jit(solution)/shard_map/ppermute | solution.py:221
  104.3 0.8 shard_map.129
  (31 shorter events, 0.1 us)
Async XLA Ops:
  1.7 16.4 %collective-permute-start.8 = (bf16[32,4224]{1,0:T(8,128)(2,1)S(1)}, bf16[32,4224]{1,0:T(8,128)(2,1)S(1)}, u32[]{:S(2)}, u32[]{:S(2)}) collective-permute-start(bf16[32,4224]{1,0:T(8,128)(2,1)S(1)} %shard_map.122.first_ref), channel_id=1, source_target_pairs={{0,4},{1,5},{2,6},{3,7},{4,0},{5,1},{6,2},{7,3},{8,12},{9,13},{10,... | collective-permute-start | bytes 811016 | tf_op jit(solution)/shard_map/ppermute | solution.py:221
  5.8 12.4 %collective-permute-start = (bf16[32,4224]{1,0:T(8,128)(2,1)S(1)}, bf16[32,4224]{1,0:T(8,128)(2,1)S(1)}, u32[]{:S(2)}, u32[]{:S(2)}) collective-permute-start(bf16[32,4224]{1,0:T(8,128)(2,1)S(1)} %shard_map.122.first_ref), channel_id=1, source_target_pairs={{0,8},{1,9},{2,10},{3,11},{4,12},{5,13},{6,14},{7,15},{8,0},{9,1},... | collective-permute-start | bytes 811016 | tf_op jit(solution)/shard_map/ppermute | solution.py:221
  18.1 6.4 %collective-permute-start.9 = (bf16[32,4224]{1,0:T(8,128)(2,1)S(1)}, bf16[32,4224]{1,0:T(8,128)(2,1)S(1)}, u32[]{:S(2)}, u32[]{:S(2)}) collective-permute-start(bf16[32,4224]{1,0:T(8,128)(2,1)S(1)} %collective-permute-done.8.first_ref), channel_id=1, source_target_pairs={{0,8},{1,9},{2,10},{3,11},{4,12},{5,13},{6,14},{7,15},{8,0},{9,1},... | collective-permute-start | bytes 811016 | tf_op jit(solution)/shard_map/ppermute | solution.py:221
  19.4 7.8 %collective-permute-start.1 = (bf16[16,4096]{1,0:T(8,128)(2,1)S(1)}, bf16[16,4096]{1,0:T(8,128)(2,1)S(1)}, u32[]{:S(2)}, u32[]{:S(2)}) collective-permute-start(bf16[16,4096]{1,0:T(8,128)(2,1)S(1)} %get-tuple-element.42), channel_id=1, source_target_pairs={{0,1},{1,0},{2,3},{3,2},{4,5},{5,4},{6,7},{7,6},{8,9},{9,8},{10,11... | collective-permute-start | bytes 393224 | tf_op jit(solution)/shard_map/ppermute | solution.py:221
  21.0 7.9 %collective-permute-start.2 = (bf16[16,4096]{1,0:T(8,128)(2,1)S(1)}, bf16[16,4096]{1,0:T(8,128)(2,1)S(1)}, u32[]{:S(2)}, u32[]{:S(2)}) collective-permute-start(bf16[16,4096]{1,0:T(8,128)(2,1)S(1)} %get-tuple-element.43), channel_id=1, source_target_pairs={{0,2},{1,3},{2,0},{3,1},{4,6},{5,7},{6,4},{7,5},{8,10},{9,11},{10,... | collective-permute-start | bytes 393224 | tf_op jit(solution)/shard_map/ppermute | solution.py:221
  21.7 8.4 %collective-permute-start.3 = (bf16[16,4096]{1,0:T(8,128)(2,1)S(1)}, bf16[16,4096]{1,0:T(8,128)(2,1)S(1)}, u32[]{:S(2)}, u32[]{:S(2)}) collective-permute-start(bf16[16,4096]{1,0:T(8,128)(2,1)S(1)} %get-tuple-element.44), channel_id=1, source_target_pairs={{0,3},{1,2},{2,1},{3,0},{4,7},{5,6},{6,5},{7,4},{8,11},{9,10},{10,... | collective-permute-start | bytes 393224 | tf_op jit(solution)/shard_map/ppermute | solution.py:221
  23.0 8.7 %collective-permute-start.4 = (bf16[16,4096]{1,0:T(8,128)(2,1)S(1)}, bf16[16,4096]{1,0:T(8,128)(2,1)S(1)}, u32[]{:S(2)}, u32[]{:S(2)}) collective-permute-start(bf16[16,4096]{1,0:T(8,128)(2,1)S(1)} %get-tuple-element.45), channel_id=1, source_target_pairs={{0,16},{1,17},{2,18},{3,19},{4,20},{5,21},{6,22},{7,23},{8,24},{9,... | collective-permute-start | bytes 393224 | tf_op jit(solution)/shard_map/ppermute | solution.py:221
  24.5 14.3 %collective-permute-start.5 = (bf16[16,4096]{1,0:T(8,128)(2,1)S(1)}, bf16[16,4096]{1,0:T(8,128)(2,1)S(1)}, u32[]{:S(2)}, u32[]{:S(2)}) collective-permute-start(bf16[16,4096]{1,0:T(8,128)(2,1)S(1)} %get-tuple-element.46), channel_id=1, source_target_pairs={{0,17},{1,16},{2,19},{3,18},{4,21},{5,20},{6,23},{7,22},{8,25},{9,... | collective-permute-start | bytes 393224 | tf_op jit(solution)/shard_map/ppermute | solution.py:221
  27.2 12.5 %collective-permute-start.6 = (bf16[16,4096]{1,0:T(8,128)(2,1)S(1)}, bf16[16,4096]{1,0:T(8,128)(2,1)S(1)}, u32[]{:S(2)}, u32[]{:S(2)}) collective-permute-start(bf16[16,4096]{1,0:T(8,128)(2,1)S(1)} %get-tuple-element.47), channel_id=1, source_target_pairs={{0,18},{1,19},{2,16},{3,17},{4,22},{5,23},{6,20},{7,21},{8,26},{9,... | collective-permute-start | bytes 393224 | tf_op jit(solution)/shard_map/ppermute | solution.py:221
  28.9 11.1 %collective-permute-start.7 = (bf16[16,4096]{1,0:T(8,128)(2,1)S(1)}, bf16[16,4096]{1,0:T(8,128)(2,1)S(1)}, u32[]{:S(2)}, u32[]{:S(2)}) collective-permute-start(bf16[16,4096]{1,0:T(8,128)(2,1)S(1)} %get-tuple-element.48), channel_id=1, source_target_pairs={{0,19},{1,18},{2,17},{3,16},{4,23},{5,22},{6,21},{7,20},{8,27},{9,... | collective-permute-start | bytes 393224 | tf_op jit(solution)/shard_map/ppermute | solution.py:221
  30.1 11.8 %collective-permute-start.10 = (bf16[16,4096]{1,0:T(8,128)(2,1)S(1)}, bf16[16,4096]{1,0:T(8,128)(2,1)S(1)}, u32[]{:S(2)}, u32[]{:S(2)}) collective-permute-start(bf16[16,4096]{1,0:T(8,128)(2,1)S(1)} %get-tuple-element.50), channel_id=1, source_target_pairs={{0,1},{1,0},{2,3},{3,2},{4,5},{5,4},{6,7},{7,6},{8,9},{9,8},{10,11... | collective-permute-start | bytes 393224 | tf_op jit(solution)/shard_map/ppermute | solution.py:221
  31.7 11.7 %collective-permute-start.11 = (bf16[16,4096]{1,0:T(8,128)(2,1)S(1)}, bf16[16,4096]{1,0:T(8,128)(2,1)S(1)}, u32[]{:S(2)}, u32[]{:S(2)}) collective-permute-start(bf16[16,4096]{1,0:T(8,128)(2,1)S(1)} %get-tuple-element.51), channel_id=1, source_target_pairs={{0,2},{1,3},{2,0},{3,1},{4,6},{5,7},{6,4},{7,5},{8,10},{9,11},{10,... | collective-permute-start | bytes 393224 | tf_op jit(solution)/shard_map/ppermute | solution.py:221
  38.8 6.7 %collective-permute-start.12 = (bf16[16,4096]{1,0:T(8,128)(2,1)S(1)}, bf16[16,4096]{1,0:T(8,128)(2,1)S(1)}, u32[]{:S(2)}, u32[]{:S(2)}) collective-permute-start(bf16[16,4096]{1,0:T(8,128)(2,1)S(1)} %get-tuple-element.52), channel_id=1, source_target_pairs={{0,3},{1,2},{2,1},{3,0},{4,7},{5,6},{6,5},{7,4},{8,11},{9,10},{10,... | collective-permute-start | bytes 393224 | tf_op jit(solution)/shard_map/ppermute | solution.py:221
  39.7 12.2 %collective-permute-start.13 = (bf16[16,4096]{1,0:T(8,128)(2,1)S(1)}, bf16[16,4096]{1,0:T(8,128)(2,1)S(1)}, u32[]{:S(2)}, u32[]{:S(2)}) collective-permute-start(bf16[16,4096]{1,0:T(8,128)(2,1)S(1)} %get-tuple-element.53), channel_id=1, source_target_pairs={{0,16},{1,17},{2,18},{3,19},{4,20},{5,21},{6,22},{7,23},{8,24},{9,... | collective-permute-start | bytes 393224 | tf_op jit(solution)/shard_map/ppermute | solution.py:221
  40.0 11.8 %collective-permute-start.14 = (bf16[16,4096]{1,0:T(8,128)(2,1)S(1)}, bf16[16,4096]{1,0:T(8,128)(2,1)S(1)}, u32[]{:S(2)}, u32[]{:S(2)}) collective-permute-start(bf16[16,4096]{1,0:T(8,128)(2,1)S(1)} %get-tuple-element.54), channel_id=1, source_target_pairs={{0,17},{1,16},{2,19},{3,18},{4,21},{5,20},{6,23},{7,22},{8,25},{9,... | collective-permute-start | bytes 393224 | tf_op jit(solution)/shard_map/ppermute | solution.py:221
  41.9 9.9 %collective-permute-start.15 = (bf16[16,4096]{1,0:T(8,128)(2,1)S(1)}, bf16[16,4096]{1,0:T(8,128)(2,1)S(1)}, u32[]{:S(2)}, u32[]{:S(2)}) collective-permute-start(bf16[16,4096]{1,0:T(8,128)(2,1)S(1)} %get-tuple-element.55), channel_id=1, source_target_pairs={{0,18},{1,19},{2,16},{3,17},{4,22},{5,23},{6,20},{7,21},{8,26},{9,... | collective-permute-start | bytes 393224 | tf_op jit(solution)/shard_map/ppermute | solution.py:221
  43.4 8.4 %collective-permute-start.16 = (bf16[16,4096]{1,0:T(8,128)(2,1)S(1)}, bf16[16,4096]{1,0:T(8,128)(2,1)S(1)}, u32[]{:S(2)}, u32[]{:S(2)}) collective-permute-start(bf16[16,4096]{1,0:T(8,128)(2,1)S(1)} %get-tuple-element.56), channel_id=1, source_target_pairs={{0,19},{1,18},{2,17},{3,16},{4,23},{5,22},{6,21},{7,20},{8,27},{9,... | collective-permute-start | bytes 393224 | tf_op jit(solution)/shard_map/ppermute | solution.py:221
  51.8 52.5 %copy-start = (s32[1,32]{1,0:T(1,128)S(1)}, s32[1,32]{1,0:T(1,128)}, u32[]{:S(2)}) copy-start(s32[1,32]{1,0:T(1,128)} %query_ref.1) | copy-start | bytes 388
  67.6 6.3 %collective-permute-start.25 = (bf16[16,2560]{1,0:T(8,128)(2,1)S(1)}, bf16[16,2560]{1,0:T(8,128)(2,1)S(1)}, u32[]{:S(2)}, u32[]{:S(2)}) collective-permute-start(bf16[16,2560]{1,0:T(8,128)(2,1)S(1)} %get-tuple-element.69), channel_id=1, source_target_pairs={{0,1},{1,0},{2,3},{3,2},{4,5},{5,4},{6,7},{7,6},{8,9},{9,8},{10,11... | collective-permute-start | bytes 245768 | tf_op jit(solution)/shard_map/ppermute | solution.py:221
  69.0 6.8 %collective-permute-start.26 = (bf16[16,2560]{1,0:T(8,128)(2,1)S(1)}, bf16[16,2560]{1,0:T(8,128)(2,1)S(1)}, u32[]{:S(2)}, u32[]{:S(2)}) collective-permute-start(bf16[16,2560]{1,0:T(8,128)(2,1)S(1)} %get-tuple-element.70), channel_id=1, source_target_pairs={{0,2},{1,3},{2,0},{3,1},{4,6},{5,7},{6,4},{7,5},{8,10},{9,11},{10,... | collective-permute-start | bytes 245768 | tf_op jit(solution)/shard_map/ppermute | solution.py:221
  70.8 6.2 %collective-permute-start.27 = (bf16[16,2560]{1,0:T(8,128)(2,1)S(1)}, bf16[16,2560]{1,0:T(8,128)(2,1)S(1)}, u32[]{:S(2)}, u32[]{:S(2)}) collective-permute-start(bf16[16,2560]{1,0:T(8,128)(2,1)S(1)} %get-tuple-element.71), channel_id=1, source_target_pairs={{0,3},{1,2},{2,1},{3,0},{4,7},{5,6},{6,5},{7,4},{8,11},{9,10},{10,... | collective-permute-start | bytes 245768 | tf_op jit(solution)/shard_map/ppermute | solution.py:221
  71.2 7.2 %collective-permute-start.28 = (bf16[16,2560]{1,0:T(8,128)(2,1)S(1)}, bf16[16,2560]{1,0:T(8,128)(2,1)S(1)}, u32[]{:S(2)}, u32[]{:S(2)}) collective-permute-start(bf16[16,2560]{1,0:T(8,128)(2,1)S(1)} %get-tuple-element.72), channel_id=1, source_target_pairs={{0,16},{1,17},{2,18},{3,19},{4,20},{5,21},{6,22},{7,23},{8,24},{9,... | collective-permute-start | bytes 245768 | tf_op jit(solution)/shard_map/ppermute | solution.py:221
  72.7 7.5 %collective-permute-start.29 = (bf16[16,2560]{1,0:T(8,128)(2,1)S(1)}, bf16[16,2560]{1,0:T(8,128)(2,1)S(1)}, u32[]{:S(2)}, u32[]{:S(2)}) collective-permute-start(bf16[16,2560]{1,0:T(8,128)(2,1)S(1)} %get-tuple-element.73), channel_id=1, source_target_pairs={{0,17},{1,16},{2,19},{3,18},{4,21},{5,20},{6,23},{7,22},{8,25},{9,... | collective-permute-start | bytes 245768 | tf_op jit(solution)/shard_map/ppermute | solution.py:221
  73.9 7.4 %collective-permute-start.30 = (bf16[16,2560]{1,0:T(8,128)(2,1)S(1)}, bf16[16,2560]{1,0:T(8,128)(2,1)S(1)}, u32[]{:S(2)}, u32[]{:S(2)}) collective-permute-start(bf16[16,2560]{1,0:T(8,128)(2,1)S(1)} %get-tuple-element.74), channel_id=1, source_target_pairs={{0,18},{1,19},{2,16},{3,17},{4,22},{5,23},{6,20},{7,21},{8,26},{9,... | collective-permute-start | bytes 245768 | tf_op jit(solution)/shard_map/ppermute | solution.py:221
  75.8 6.3 %collective-permute-start.31 = (bf16[16,2560]{1,0:T(8,128)(2,1)S(1)}, bf16[16,2560]{1,0:T(8,128)(2,1)S(1)}, u32[]{:S(2)}, u32[]{:S(2)}) collective-permute-start(bf16[16,2560]{1,0:T(8,128)(2,1)S(1)} %get-tuple-element.75), channel_id=1, source_target_pairs={{0,19},{1,18},{2,17},{3,16},{4,23},{5,22},{6,21},{7,20},{8,27},{9,... | collective-permute-start | bytes 245768 | tf_op jit(solution)/shard_map/ppermute | solution.py:221
  77.0 6.9 %collective-permute-start.17 = (bf16[16,2560]{1,0:T(8,128)(2,1)S(1)}, bf16[16,2560]{1,0:T(8,128)(2,1)S(1)}, u32[]{:S(2)}, u32[]{:S(2)}) collective-permute-start(bf16[16,2560]{1,0:T(8,128)(2,1)S(1)} %get-tuple-element.58), channel_id=1, source_target_pairs={{0,1},{1,0},{2,3},{3,2},{4,5},{5,4},{6,7},{7,6},{8,9},{9,8},{10,11... | collective-permute-start | bytes 245768 | tf_op jit(solution)/shard_map/ppermute | solution.py:221
  78.3 6.0 %collective-permute-start.18 = (bf16[16,2560]{1,0:T(8,128)(2,1)S(1)}, bf16[16,2560]{1,0:T(8,128)(2,1)S(1)}, u32[]{:S(2)}, u32[]{:S(2)}) collective-permute-start(bf16[16,2560]{1,0:T(8,128)(2,1)S(1)} %get-tuple-element.59), channel_id=1, source_target_pairs={{0,2},{1,3},{2,0},{3,1},{4,6},{5,7},{6,4},{7,5},{8,10},{9,11},{10,... | collective-permute-start | bytes 245768 | tf_op jit(solution)/shard_map/ppermute | solution.py:221
  80.1 5.5 %collective-permute-start.19 = (bf16[16,2560]{1,0:T(8,128)(2,1)S(1)}, bf16[16,2560]{1,0:T(8,128)(2,1)S(1)}, u32[]{:S(2)}, u32[]{:S(2)}) collective-permute-start(bf16[16,2560]{1,0:T(8,128)(2,1)S(1)} %get-tuple-element.60), channel_id=1, source_target_pairs={{0,3},{1,2},{2,1},{3,0},{4,7},{5,6},{6,5},{7,4},{8,11},{9,10},{10,... | collective-permute-start | bytes 245768 | tf_op jit(solution)/shard_map/ppermute | solution.py:221
  82.3 10.8 %collective-permute-start.32 = (bf16[32,2560]{1,0:T(8,128)(2,1)S(1)}, bf16[32,2560]{1,0:T(8,128)(2,1)S(1)}, u32[]{:S(2)}, u32[]{:S(2)}) collective-permute-start(bf16[32,2560]{1,0:T(8,128)(2,1)S(1)} %get-tuple-element.77), channel_id=1, source_target_pairs={{0,8},{1,9},{2,10},{3,11},{4,12},{5,13},{6,14},{7,15},{8,0},{9,1},... | collective-permute-start | bytes 491528 | tf_op jit(solution)/shard_map/ppermute | solution.py:221
  82.4 8.2 %collective-permute-start.20 = (bf16[16,2560]{1,0:T(8,128)(2,1)S(1)}, bf16[16,2560]{1,0:T(8,128)(2,1)S(1)}, u32[]{:S(2)}, u32[]{:S(2)}) collective-permute-start(bf16[16,2560]{1,0:T(8,128)(2,1)S(1)} %get-tuple-element.61), channel_id=1, source_target_pairs={{0,16},{1,17},{2,18},{3,19},{4,20},{5,21},{6,22},{7,23},{8,24},{9,... | collective-permute-start | bytes 245768 | tf_op jit(solution)/shard_map/ppermute | solution.py:221
  83.9 8.9 %collective-permute-start.21 = (bf16[16,2560]{1,0:T(8,128)(2,1)S(1)}, bf16[16,2560]{1,0:T(8,128)(2,1)S(1)}, u32[]{:S(2)}, u32[]{:S(2)}) collective-permute-start(bf16[16,2560]{1,0:T(8,128)(2,1)S(1)} %get-tuple-element.62), channel_id=1, source_target_pairs={{0,17},{1,16},{2,19},{3,18},{4,21},{5,20},{6,23},{7,22},{8,25},{9,... | collective-permute-start | bytes 245768 | tf_op jit(solution)/shard_map/ppermute | solution.py:221
  84.3 8.5 %collective-permute-start.22 = (bf16[16,2560]{1,0:T(8,128)(2,1)S(1)}, bf16[16,2560]{1,0:T(8,128)(2,1)S(1)}, u32[]{:S(2)}, u32[]{:S(2)}) collective-permute-start(bf16[16,2560]{1,0:T(8,128)(2,1)S(1)} %get-tuple-element.63), channel_id=1, source_target_pairs={{0,18},{1,19},{2,16},{3,17},{4,22},{5,23},{6,20},{7,21},{8,26},{9,... | collective-permute-start | bytes 245768 | tf_op jit(solution)/shard_map/ppermute | solution.py:221
  85.7 7.2 %collective-permute-start.23 = (bf16[16,2560]{1,0:T(8,128)(2,1)S(1)}, bf16[16,2560]{1,0:T(8,128)(2,1)S(1)}, u32[]{:S(2)}, u32[]{:S(2)}) collective-permute-start(bf16[16,2560]{1,0:T(8,128)(2,1)S(1)} %get-tuple-element.64), channel_id=1, source_target_pairs={{0,19},{1,18},{2,17},{3,16},{4,23},{5,22},{6,21},{7,20},{8,27},{9,... | collective-permute-start | bytes 245768 | tf_op jit(solution)/shard_map/ppermute | solution.py:221
  93.1 2.9 %collective-permute-start.24 = (bf16[32,2560]{1,0:T(8,128)(2,1)S(1)}, bf16[32,2560]{1,0:T(8,128)(2,1)S(1)}, u32[]{:S(2)}, u32[]{:S(2)}) collective-permute-start(bf16[32,2560]{1,0:T(8,128)(2,1)S(1)} %get-tuple-element.66), channel_id=1, source_target_pairs={{0,8},{1,9},{2,10},{3,11},{4,12},{5,13},{6,14},{7,15},{8,0},{9,1},... | collective-permute-start | bytes 491528 | tf_op jit(solution)/shard_map/ppermute | solution.py:221
  93.2 11.1 %collective-permute-start.33 = (bf16[32,2560]{1,0:T(8,128)(2,1)S(1)}, bf16[32,2560]{1,0:T(8,128)(2,1)S(1)}, u32[]{:S(2)}, u32[]{:S(2)}) collective-permute-start(bf16[32,2560]{1,0:T(8,128)(2,1)S(1)} %shard_map.128), channel_id=1, source_target_pairs={{0,4},{1,5},{2,6},{3,7},{4,0},{5,1},{6,2},{7,3},{8,12},{9,13},{10,... | collective-permute-start | bytes 491528 | tf_op jit(solution)/shard_map/ppermute | solution.py:221

commit v4 on v3

--- a/solution.py
+++ b/solution.py
@@ -79,28 +79,24 @@
         send[:, width:] = delta[i * piece : (i + 1) * piece]
 
 
+def load_kernel(*refs):
+    count = len(refs) // 2
+    sem = refs[-1]
+    copies = [pltpu.make_async_copy(refs[i], refs[count + i], sem.at[i]) for i in range(count)]
+    for copy in copies:
+        copy.start()
+    for copy in copies:
+        copy.wait()
+
+
 def expert_kernel(count, group, *refs):
-    ins, hbm, outs, vmem = (
-        refs[:count],
-        refs[count : count + 6],
-        refs[count + 6 : 2 * count + 6],
-        refs[2 * count + 6 : 2 * count + 12],
-    )
-    outer_ref, sem = refs[2 * count + 12 :]
-    gate, up, down, left_proj, right_proj, stored = vmem
+    ins, weights, outs = refs[:count], refs[count : count + 6], refs[count + 6 : 2 * count + 6]
+    gate, up, down, left_proj, right_proj, stored = weights
+    outer_ref = refs[-1]
     experts, width, _ = gate.shape
     rank = left_proj.shape[1]
     piece = ins[0].shape[0]
     rows = piece * count
-
-    def copy(i, j):
-        return pltpu.make_async_copy(hbm[i].at[j], vmem[i].at[j], sem.at[i, j])
-
-    for j in range(experts):
-        for i in range(5):
-            copy(i, j).start()
-    for j in range(experts):
-        copy(5, j).start()
     x = jnp.concatenate([r[:, :width] for r in ins], axis=0)
     delta = jnp.concatenate([r[:, width:] for r in ins], axis=0)
     owner = lax.broadcasted_iota(jnp.int32, (rows, 1), 0) // group % experts
@@ -109,11 +105,8 @@
     grad = jnp.zeros((rows, width), F32)
     for j in range(experts):
         mine = owner == j
-        copy(0, j).wait()
         a_gate = dot(x, gate[j])
-        copy(1, j).wait()
         a_up = dot(x, up[j])
-        copy(2, j).wait()
         d_hidden = dot_nt(delta, down[j])
         sig = jax.nn.sigmoid(a_gate)
         active = a_gate * sig
@@ -124,9 +117,7 @@
         ).astype(BF16)
         grad = grad + dot_nt(grad_gate, gate[j])
         grad = grad + dot_nt(grad_up, up[j])
-        copy(3, j).wait()
         left = jnp.where(mine, dot_nt(delta, left_proj[j]), left)
-        copy(4, j).wait()
         right = jnp.where(mine, dot_nt(hidden, right_proj[j]), right)
     grad = grad.astype(BF16)
     per = LANES // rank
@@ -143,7 +134,6 @@
             )
     score = jnp.zeros((rows, stored.shape[2]), F32)
     for j in range(experts):
-        copy(5, j).wait()
         score = score + dot(outer_ref[j], stored[j])
     score = score.astype(BF16)
     for i, out in enumerate(outs):
@@ -220,9 +210,13 @@
                         pairs.append((source, target + (d ^ far)))
         return lax.ppermute(value, AXES, pairs)
 
+    order = sorted(range(1, chips), key=lambda o: (-bin(o).count("1"), -o))
+
+    def move(pieces, offsets):
+        return {o: swap(pieces[o], row=o // deep, far=o % deep) for o in offsets}
+
     def exchange(pieces):
-        order = sorted(range(1, chips), key=lambda o: -bin(o).count("1"))
-        moved = {o: swap(pieces[o], row=o // deep, far=o % deep) for o in order}
+        moved = move(pieces, order)
         return [pieces[0]] + [moved[o] for o in range(1, chips)]
 
     def pack(first, second):
@@ -252,24 +246,31 @@
     other = swap(guest, core=1)
     guest_send, guest_place = pack(guest, other)
     guest_rows = exchange(guest_send)
+    held = pl.pallas_call(
+        load_kernel,
+        out_shape=tuple(pltpu.VMEM(w.shape, w.dtype) for w in weights),
+        in_specs=[HBM] * len(weights),
+        out_specs=(VMEM,) * len(weights),
+        scratch_shapes=[pltpu.SemaphoreType.DMA((len(weights),))],
+        compiler_params=pltpu.CompilerParams(vmem_limit_bytes=1 << 20),
+    )(*weights)
     rows = 2 * chips * piece
     size = sum(w.size for w in weights)
     outs = call(
         functools.partial(expert_kernel, 2 * chips, PAIR * capacity),
         (shape((piece, width + train), BF16),) * (2 * chips),
-        [VMEM] * (2 * chips) + [HBM] * len(weights),
-        (*own_rows, *guest_rows, *weights),
-        scratch=[pltpu.VMEM(w.shape, w.dtype) for w in weights]
-        + [
-            pltpu.VMEM((experts, rows, weights[5].shape[1]), BF16),
-            pltpu.SemaphoreType.DMA((len(weights), experts)),
-        ],
+        [VMEM] * (2 * chips + len(weights)),
+        (*own_rows, *guest_rows, *held),
+        scratch=[pltpu.VMEM((experts, rows, weights[5].shape[1]), BF16)],
         flops=2 * rows * size,
         moved=2 * size,
-        limit=50 << 20,
+        limit=rows * (76 << 10),
     )
     guest_back = exchange(outs[chips:])
-    own_back = exchange(outs[:chips])
+    early = (chips - 1) // 2
+    moved = move(outs[:chips], order[:early])
+    moved.update(move(outs[:chips], order[early:]))
+    own_back = [outs[0]] + [moved[o] for o in range(1, chips)]
     guest_keep, guest_give = part(guest_place, guest_back)
     more = swap(guest_give, core=1)
     far = call(join_kernel, shape((tok, width + train), BF16), [VMEM] * 2, (guest_keep, more))

time: 105 us -> 101 us (0.962)
  waiting for transfers between devices: 38.6 us -> 32.7 us
  Pallas kernels: 20.5 us -> 22.6 us
    pallas_call x0 -> x1, Pallas kernels: none -> 7.28 us  [layer(): pl.pallas_call(load_kernel, out_shape=tuple((pltpu.VMEM(w.shape, w.dtype)...]
    ppermute x34, waiting for transfers between devices: 38.6 us -> 32.7 us  [swap(): return lax.ppermute(value, AXES, pairs)]
    pallas_call x8, Pallas kernels: 20.5 us -> 15.3 us  [call(): pl.pallas_call(kernel, out_shape=outs, in_specs=in_specs, out_specs=jax.t...]
  transfers between devices with their start and end apart: 34 -> 34, of which waited for: 7 -> 8; matrix products, arithmetic and copies ran while one was open for 0% -> 0% of each run, Pallas kernels for 3% -> 10%
where the time goes in v4:
time: 101 us
  starting transfers between devices  44.6 us (44%)
  waiting for transfers between devices  32.7 us (32%)
  Pallas kernels  22.6 us (22%)
    ppermute x34, starting transfers between devices, swap(): return lax.ppermute(value, AXES, pairs)  44.6 us
    ppermute x34, waiting for transfers between devices, swap(): return lax.ppermute(value, AXES, pairs)  32.7 us
    pallas_call x8, Pallas kernels, call(): pl.pallas_call(kernel, out_shape=outs, in_specs=in_specs, out_specs=jax.t...  15.3 us
    pallas_call x1, Pallas kernels, layer(): pl.pallas_call(load_kernel, out_shape=tuple((pltpu.VMEM(w.shape, w.dtype)...  7.28 us
  transfers between devices with their start and end apart: 34, of which 8 were waited for; matrix products, arithmetic and copies ran while one was open for 0% of the time, Pallas kernels for 10%

profile of v4, /device:TPU:0, one launch (start us, length us, event | category | flops | bytes accessed | tf_op | source)
XLA Modules:
  0.0 100.7 jit_solution(3672070032092247688)
XLA Ops:
  0.6 1.0 %shard_map.122.first_ref = bf16[32,4224]{1,0:T(8,128)(2,1)S(1)} custom-call(s32[4,32]{1,0:T(4,128)} %bitcast.10, bf16[4,32]{1,0:T(4,128)(2,1)} %bitcast.11, bf16[32,2048]{1,0:T(8,128)(2,1)} %x_hbm.1, bf16[32,2048]{1,0:T(8,128)(2,1)} %g_hbm.1), custom_call_target="tpu_custom_call" | custom-call | flops 1000000 | bytes 1000000 | tf_op jit(solution)/shard_map/pallas_call | solution.py:177
  1.7 4.1 %collective-permute-start.8 = (bf16[32,4224]{1,0:T(8,128)(2,1)S(1)}, bf16[32,4224]{1,0:T(8,128)(2,1)S(1)}, u32[]{:S(2)}, u32[]{:S(2)}) collective-permute-start(bf16[32,4224]{1,0:T(8,128)(2,1)S(1)} %shard_map.122.first_ref), channel_id=1, source_target_pairs={{0,4},{1,5},{2,6},{3,7},{4,0},{5,1},{6,2},{7,3},{8,12},{9,13},{10,... | collective-permute-start | bytes 811016 | tf_op jit(solution)/shard_map/ppermute | solution.py:211
  5.8 12.3 %collective-permute-done.8.first_ref = bf16[32,4224]{1,0:T(8,128)(2,1)S(1)} collective-permute-done((bf16[32,4224]{1,0:T(8,128)(2,1)S(1)}, bf16[32,4224]{1,0:T(8,128)(2,1)S(1)}, u32[]{:S(2)}, u32[]{:S(2)}) %collective-permute-start.8) | collective-permute-done | bytes 270368 | tf_op jit(solution)/shard_map/ppermute | solution.py:211
  18.1 0.1 pad_add_fusion.here_ref
  18.2 1.2 %shard_map.123 = (bf16[16,4096]{1,0:T(8,128)(2,1)S(1)}, bf16[16,4096]{1,0:T(8,128)(2,1)S(1)}, bf16[16,4096]{1,0:T(8,128)(2,1)S(1)}, bf16[16,4096]{1,0:T(8,128)(2...) custom-call(s32[4]{0:T(128)S(1)} %pad_add_fusion.here_ref, ...), custom_call_target="tpu_custom_call" | custom-call | flops 1000000 | bytes 1000000 | tf_op jit(solution)/shard_map/pallas_call | solution.py:177
  19.4 1.6 %collective-permute-start.1 = (bf16[16,4096]{1,0:T(8,128)(2,1)S(1)}, bf16[16,4096]{1,0:T(8,128)(2,1)S(1)}, u32[]{:S(2)}, u32[]{:S(2)}) collective-permute-start(bf16[16,4096]{1,0:T(8,128)(2,1)S(1)} %get-tuple-element.48), channel_id=1, source_target_pairs={{0,1},{1,0},{2,3},{3,2},{4,5},{5,4},{6,7},{7,6},{8,9},{9,8},{10,11... | collective-permute-start | bytes 393224 | tf_op jit(solution)/shard_map/ppermute | solution.py:211
  21.0 0.7 collective-permute-start.2
  21.7 1.3 %collective-permute-start.3 = (bf16[16,4096]{1,0:T(8,128)(2,1)S(1)}, bf16[16,4096]{1,0:T(8,128)(2,1)S(1)}, u32[]{:S(2)}, u32[]{:S(2)}) collective-permute-start(bf16[16,4096]{1,0:T(8,128)(2,1)S(1)} %get-tuple-element.50), channel_id=1, source_target_pairs={{0,3},{1,2},{2,1},{3,0},{4,7},{5,6},{6,5},{7,4},{8,11},{9,10},{10,... | collective-permute-start | bytes 393224 | tf_op jit(solution)/shard_map/ppermute | solution.py:211
  23.0 1.6 %collective-permute-start.4 = (bf16[16,4096]{1,0:T(8,128)(2,1)S(1)}, bf16[16,4096]{1,0:T(8,128)(2,1)S(1)}, u32[]{:S(2)}, u32[]{:S(2)}) collective-permute-start(bf16[16,4096]{1,0:T(8,128)(2,1)S(1)} %get-tuple-element.51), channel_id=1, source_target_pairs={{0,16},{1,17},{2,18},{3,19},{4,20},{5,21},{6,22},{7,23},{8,24},{9,... | collective-permute-start | bytes 393224 | tf_op jit(solution)/shard_map/ppermute | solution.py:211
  24.5 1.4 %collective-permute-start.5 = (bf16[16,4096]{1,0:T(8,128)(2,1)S(1)}, bf16[16,4096]{1,0:T(8,128)(2,1)S(1)}, u32[]{:S(2)}, u32[]{:S(2)}) collective-permute-start(bf16[16,4096]{1,0:T(8,128)(2,1)S(1)} %get-tuple-element.52), channel_id=1, source_target_pairs={{0,17},{1,16},{2,19},{3,18},{4,21},{5,20},{6,23},{7,22},{8,25},{9,... | collective-permute-start | bytes 393224 | tf_op jit(solution)/shard_map/ppermute | solution.py:211
  26.0 1.2 %shard_map.124 = (bf16[16,4096]{1,0:T(8,128)(2,1)S(1)}, bf16[16,4096]{1,0:T(8,128)(2,1)S(1)}, bf16[16,4096]{1,0:T(8,128)(2,1)S(1)}, bf16[16,4096]{1,0:T(8,128)(2...) custom-call(s32[4]{0:T(128)S(1)} %pad_add_fusion.here_ref, ...), custom_call_target="tpu_custom_call" | custom-call | flops 1000000 | bytes 1000000 | tf_op jit(solution)/shard_map/pallas_call | solution.py:177
  27.2 1.7 %collective-permute-start.6 = (bf16[16,4096]{1,0:T(8,128)(2,1)S(1)}, bf16[16,4096]{1,0:T(8,128)(2,1)S(1)}, u32[]{:S(2)}, u32[]{:S(2)}) collective-permute-start(bf16[16,4096]{1,0:T(8,128)(2,1)S(1)} %get-tuple-element.53), channel_id=1, source_target_pairs={{0,18},{1,19},{2,16},{3,17},{4,22},{5,23},{6,20},{7,21},{8,26},{9,... | collective-permute-start | bytes 393224 | tf_op jit(solution)/shard_map/ppermute | solution.py:211
  28.9 1.2 %collective-permute-start.7 = (bf16[16,4096]{1,0:T(8,128)(2,1)S(1)}, bf16[16,4096]{1,0:T(8,128)(2,1)S(1)}, u32[]{:S(2)}, u32[]{:S(2)}) collective-permute-start(bf16[16,4096]{1,0:T(8,128)(2,1)S(1)} %get-tuple-element.54), channel_id=1, source_target_pairs={{0,19},{1,18},{2,17},{3,16},{4,23},{5,22},{6,21},{7,20},{8,27},{9,... | collective-permute-start | bytes 393224 | tf_op jit(solution)/shard_map/ppermute | solution.py:211
  30.1 1.5 %collective-permute-start.10 = (bf16[16,4096]{1,0:T(8,128)(2,1)S(1)}, bf16[16,4096]{1,0:T(8,128)(2,1)S(1)}, u32[]{:S(2)}, u32[]{:S(2)}) collective-permute-start(bf16[16,4096]{1,0:T(8,128)(2,1)S(1)} %get-tuple-element.56), channel_id=1, source_target_pairs={{0,1},{1,0},{2,3},{3,2},{4,5},{5,4},{6,7},{7,6},{8,9},{9,8},{10,11... | collective-permute-start | bytes 393224 | tf_op jit(solution)/shard_map/ppermute | solution.py:211
  31.7 0.7 collective-permute-start.11
  32.4 6.4 %collective-permute-done.5.refs_5_ = bf16[16,4096]{1,0:T(8,128)(2,1)S(1)} collective-permute-done((bf16[16,4096]{1,0:T(8,128)(2,1)S(1)}, bf16[16,4096]{1,0:T(8,128)(2,1)S(1)}, u32[]{:S(2)}, u32[]{:S(2)}) %collective-permute-start.5) | collective-permute-done | bytes 131104 | tf_op jit(solution)/shard_map/ppermute | solution.py:211
  38.8 0.9 collective-permute-start.12
  39.7 0.4 collective-permute-start.13
  40.0 1.9 %collective-permute-start.14 = (bf16[16,4096]{1,0:T(8,128)(2,1)S(1)}, bf16[16,4096]{1,0:T(8,128)(2,1)S(1)}, u32[]{:S(2)}, u32[]{:S(2)}) collective-permute-start(bf16[16,4096]{1,0:T(8,128)(2,1)S(1)} %get-tuple-element.60), channel_id=1, source_target_pairs={{0,17},{1,16},{2,19},{3,18},{4,21},{5,20},{6,23},{7,22},{8,25},{9,... | collective-permute-start | bytes 393224 | tf_op jit(solution)/shard_map/ppermute | solution.py:211
  41.9 1.5 %collective-permute-start.15 = (bf16[16,4096]{1,0:T(8,128)(2,1)S(1)}, bf16[16,4096]{1,0:T(8,128)(2,1)S(1)}, u32[]{:S(2)}, u32[]{:S(2)}) collective-permute-start(bf16[16,4096]{1,0:T(8,128)(2,1)S(1)} %get-tuple-element.61), channel_id=1, source_target_pairs={{0,18},{1,19},{2,16},{3,17},{4,22},{5,23},{6,20},{7,21},{8,26},{9,... | collective-permute-start | bytes 393224 | tf_op jit(solution)/shard_map/ppermute | solution.py:211
  43.4 2.1 %collective-permute-start.16 = (bf16[16,4096]{1,0:T(8,128)(2,1)S(1)}, bf16[16,4096]{1,0:T(8,128)(2,1)S(1)}, u32[]{:S(2)}, u32[]{:S(2)}) collective-permute-start(bf16[16,4096]{1,0:T(8,128)(2,1)S(1)} %get-tuple-element.62), channel_id=1, source_target_pairs={{0,19},{1,18},{2,17},{3,16},{4,23},{5,22},{6,21},{7,20},{8,27},{9,... | collective-permute-start | bytes 393224 | tf_op jit(solution)/shard_map/ppermute | solution.py:211
  45.5 7.3 %shard_map.125 = (bf16[2,2048,512]{2,1,0:T(8,128)(2,1)S(1)}, bf16[2,2048,512]{2,1,0:T(8,128)(2,1)S(1)}, bf16[2,512,2048]{2,1,0:T(8,128)(2,1)S(1)}, bf16[2,64,204...) custom-call(bf16[2,2048,512]{2,1,0:T(8,128)(2,1)} %refs_0_.1, ...), custom_call_target="tpu_custom_call" | custom-call | tf_op jit(solution)/shard_map/pallas_call | solution.py:249
  52.9 10.5 %shard_map.126 = (bf16[16,2560]{1,0:T(8,128)(2,1)S(1)}, bf16[16,2560]{1,0:T(8,128)(2,1)S(1)}, bf16[16,2560]{1,0:T(8,128)(2,1)S(1)}, bf16[16,2560]{1,0:T(8,128)(2...) custom-call(bf16[16,4096]{1,0:T(8,128)(2,1)S(1)} %get-tuple-element., ...), custom_call_target="tpu_custom_call" | custom-call | flops 5536481280 | bytes 21626880 | tf_op jit(solution)/shard_map/pallas_call | solution.py:177
  63.4 0.9 collective-permute-start.25
  64.3 1.8 %collective-permute-start.26 = (bf16[16,2560]{1,0:T(8,128)(2,1)S(1)}, bf16[16,2560]{1,0:T(8,128)(2,1)S(1)}, u32[]{:S(2)}, u32[]{:S(2)}) collective-permute-start(bf16[16,2560]{1,0:T(8,128)(2,1)S(1)} %get-tuple-element.82), channel_id=1, source_target_pairs={{0,2},{1,3},{2,0},{3,1},{4,6},{5,7},{6,4},{7,5},{8,10},{9,11},{10,... | collective-permute-start | bytes 245768 | tf_op jit(solution)/shard_map/ppermute | solution.py:211
  66.1 0.9 collective-permute-start.27
  66.9 0.9 collective-permute-start.28
  67.8 1.4 %collective-permute-start.29 = (bf16[16,2560]{1,0:T(8,128)(2,1)S(1)}, bf16[16,2560]{1,0:T(8,128)(2,1)S(1)}, u32[]{:S(2)}, u32[]{:S(2)}) collective-permute-start(bf16[16,2560]{1,0:T(8,128)(2,1)S(1)} %get-tuple-element.85), channel_id=1, source_target_pairs={{0,17},{1,16},{2,19},{3,18},{4,21},{5,20},{6,23},{7,22},{8,25},{9,... | collective-permute-start | bytes 245768 | tf_op jit(solution)/shard_map/ppermute | solution.py:211
  69.2 1.5 %collective-permute-start.30 = (bf16[16,2560]{1,0:T(8,128)(2,1)S(1)}, bf16[16,2560]{1,0:T(8,128)(2,1)S(1)}, u32[]{:S(2)}, u32[]{:S(2)}) collective-permute-start(bf16[16,2560]{1,0:T(8,128)(2,1)S(1)} %get-tuple-element.86), channel_id=1, source_target_pairs={{0,18},{1,19},{2,16},{3,17},{4,22},{5,23},{6,20},{7,21},{8,26},{9,... | collective-permute-start | bytes 245768 | tf_op jit(solution)/shard_map/ppermute | solution.py:211
  70.7 2.1 %collective-permute-start.31 = (bf16[16,2560]{1,0:T(8,128)(2,1)S(1)}, bf16[16,2560]{1,0:T(8,128)(2,1)S(1)}, u32[]{:S(2)}, u32[]{:S(2)}) collective-permute-start(bf16[16,2560]{1,0:T(8,128)(2,1)S(1)} %get-tuple-element.87), channel_id=1, source_target_pairs={{0,19},{1,18},{2,17},{3,16},{4,23},{5,22},{6,21},{7,20},{8,27},{9,... | collective-permute-start | bytes 245768 | tf_op jit(solution)/shard_map/ppermute | solution.py:211
  72.8 0.8 collective-permute-start.17
  73.6 1.8 %collective-permute-start.18 = (bf16[16,2560]{1,0:T(8,128)(2,1)S(1)}, bf16[16,2560]{1,0:T(8,128)(2,1)S(1)}, u32[]{:S(2)}, u32[]{:S(2)}) collective-permute-start(bf16[16,2560]{1,0:T(8,128)(2,1)S(1)} %get-tuple-element.71), channel_id=1, source_target_pairs={{0,2},{1,3},{2,0},{3,1},{4,6},{5,7},{6,4},{7,5},{8,10},{9,11},{10,... | collective-permute-start | bytes 245768 | tf_op jit(solution)/shard_map/ppermute | solution.py:211
  75.4 0.9 collective-permute-start.19
  76.3 0.6 collective-permute-done.31.refs_7_
  77.0 0.2 shard_map.128
  77.2 0.1 collective-permute-start.32
  77.3 1.9 %collective-permute-start.20 = (bf16[16,2560]{1,0:T(8,128)(2,1)S(1)}, bf16[16,2560]{1,0:T(8,128)(2,1)S(1)}, u32[]{:S(2)}, u32[]{:S(2)}) collective-permute-start(bf16[16,2560]{1,0:T(8,128)(2,1)S(1)} %get-tuple-element.73), channel_id=1, source_target_pairs={{0,16},{1,17},{2,18},{3,19},{4,20},{5,21},{6,22},{7,23},{8,24},{9,... | collective-permute-start | bytes 245768 | tf_op jit(solution)/shard_map/ppermute | solution.py:211
  79.2 0.7 collective-permute-start.21
  79.9 1.5 %collective-permute-start.22 = (bf16[16,2560]{1,0:T(8,128)(2,1)S(1)}, bf16[16,2560]{1,0:T(8,128)(2,1)S(1)}, u32[]{:S(2)}, u32[]{:S(2)}) collective-permute-start(bf16[16,2560]{1,0:T(8,128)(2,1)S(1)} %get-tuple-element.75), channel_id=1, source_target_pairs={{0,18},{1,19},{2,16},{3,17},{4,22},{5,23},{6,20},{7,21},{8,26},{9,... | collective-permute-start | bytes 245768 | tf_op jit(solution)/shard_map/ppermute | solution.py:211
  81.5 1.7 %collective-permute-start.23 = (bf16[16,2560]{1,0:T(8,128)(2,1)S(1)}, bf16[16,2560]{1,0:T(8,128)(2,1)S(1)}, u32[]{:S(2)}, u32[]{:S(2)}) collective-permute-start(bf16[16,2560]{1,0:T(8,128)(2,1)S(1)} %get-tuple-element.76), channel_id=1, source_target_pairs={{0,19},{1,18},{2,17},{3,16},{4,23},{5,22},{6,21},{7,20},{8,27},{9,... | collective-permute-start | bytes 245768 | tf_op jit(solution)/shard_map/ppermute | solution.py:211
  83.2 2.5 %collective-permute-done.20.refs_4_ = bf16[16,2560]{1,0:T(8,128)(2,1)S(1)} collective-permute-done((bf16[16,2560]{1,0:T(8,128)(2,1)S(1)}, bf16[16,2560]{1,0:T(8,128)(2,1)S(1)}, u32[]{:S(2)}, u32[]{:S(2)}) %collective-permute-start.20) | collective-permute-done | bytes 81952 | tf_op jit(solution)/shard_map/ppermute | solution.py:211
  85.8 0.2 collective-permute-done.21.refs_5_
  85.9 0.6 collective-permute-done.22.refs_6_
  86.5 1.6 %collective-permute-done.23.refs_7_ = bf16[16,2560]{1,0:T(8,128)(2,1)S(1)} collective-permute-done((bf16[16,2560]{1,0:T(8,128)(2,1)S(1)}, bf16[16,2560]{1,0:T(8,128)(2,1)S(1)}, u32[]{:S(2)}, u32[]{:S(2)}) %collective-permute-start.23) | collective-permute-done | bytes 81952 | tf_op jit(solution)/shard_map/ppermute | solution.py:211
  88.1 0.2 shard_map.127
  88.5 3.1 %collective-permute-start.33 = (bf16[32,2560]{1,0:T(8,128)(2,1)S(1)}, bf16[32,2560]{1,0:T(8,128)(2,1)S(1)}, u32[]{:S(2)}, u32[]{:S(2)}) collective-permute-start(bf16[32,2560]{1,0:T(8,128)(2,1)S(1)} %shard_map.129), channel_id=1, source_target_pairs={{0,4},{1,5},{2,6},{3,7},{4,0},{5,1},{6,2},{7,3},{8,12},{9,13},{10,... | collective-permute-start | bytes 491528 | tf_op jit(solution)/shard_map/ppermute | solution.py:211
  91.6 8.4 %collective-permute-done.33.far_ref = bf16[32,2560]{1,0:T(8,128)(2,1)S(1)} collective-permute-done((bf16[32,2560]{1,0:T(8,128)(2,1)S(1)}, bf16[32,2560]{1,0:T(8,128)(2,1)S(1)}, u32[]{:S(2)}, u32[]{:S(2)}) %collective-permute-start.33) | collective-permute-done | bytes 163872 | tf_op jit(solution)/shard_map/ppermute | solution.py:211
  100.0 0.8 shard_map.130
  (32 shorter events, 0.2 us)
Async XLA Ops:
  1.7 16.4 %collective-permute-start.8 = (bf16[32,4224]{1,0:T(8,128)(2,1)S(1)}, bf16[32,4224]{1,0:T(8,128)(2,1)S(1)}, u32[]{:S(2)}, u32[]{:S(2)}) collective-permute-start(bf16[32,4224]{1,0:T(8,128)(2,1)S(1)} %shard_map.122.first_ref), channel_id=1, source_target_pairs={{0,4},{1,5},{2,6},{3,7},{4,0},{5,1},{6,2},{7,3},{8,12},{9,13},{10,... | collective-permute-start | bytes 811016 | tf_op jit(solution)/shard_map/ppermute | solution.py:211
  5.8 12.4 %collective-permute-start = (bf16[32,4224]{1,0:T(8,128)(2,1)S(1)}, bf16[32,4224]{1,0:T(8,128)(2,1)S(1)}, u32[]{:S(2)}, u32[]{:S(2)}) collective-permute-start(bf16[32,4224]{1,0:T(8,128)(2,1)S(1)} %shard_map.122.first_ref), channel_id=1, source_target_pairs={{0,8},{1,9},{2,10},{3,11},{4,12},{5,13},{6,14},{7,15},{8,0},{9,1},... | collective-permute-start | bytes 811016 | tf_op jit(solution)/shard_map/ppermute | solution.py:211
  18.1 6.4 %collective-permute-start.9 = (bf16[32,4224]{1,0:T(8,128)(2,1)S(1)}, bf16[32,4224]{1,0:T(8,128)(2,1)S(1)}, u32[]{:S(2)}, u32[]{:S(2)}) collective-permute-start(bf16[32,4224]{1,0:T(8,128)(2,1)S(1)} %collective-permute-done.8.first_ref), channel_id=1, source_target_pairs={{0,8},{1,9},{2,10},{3,11},{4,12},{5,13},{6,14},{7,15},{8,0},{9,1},... | collective-permute-start | bytes 811016 | tf_op jit(solution)/shard_map/ppermute | solution.py:211
  19.4 7.8 %collective-permute-start.1 = (bf16[16,4096]{1,0:T(8,128)(2,1)S(1)}, bf16[16,4096]{1,0:T(8,128)(2,1)S(1)}, u32[]{:S(2)}, u32[]{:S(2)}) collective-permute-start(bf16[16,4096]{1,0:T(8,128)(2,1)S(1)} %get-tuple-element.48), channel_id=1, source_target_pairs={{0,1},{1,0},{2,3},{3,2},{4,5},{5,4},{6,7},{7,6},{8,9},{9,8},{10,11... | collective-permute-start | bytes 393224 | tf_op jit(solution)/shard_map/ppermute | solution.py:211
  21.0 7.9 %collective-permute-start.2 = (bf16[16,4096]{1,0:T(8,128)(2,1)S(1)}, bf16[16,4096]{1,0:T(8,128)(2,1)S(1)}, u32[]{:S(2)}, u32[]{:S(2)}) collective-permute-start(bf16[16,4096]{1,0:T(8,128)(2,1)S(1)} %get-tuple-element.49), channel_id=1, source_target_pairs={{0,2},{1,3},{2,0},{3,1},{4,6},{5,7},{6,4},{7,5},{8,10},{9,11},{10,... | collective-permute-start | bytes 393224 | tf_op jit(solution)/shard_map/ppermute | solution.py:211
  21.7 8.4 %collective-permute-start.3 = (bf16[16,4096]{1,0:T(8,128)(2,1)S(1)}, bf16[16,4096]{1,0:T(8,128)(2,1)S(1)}, u32[]{:S(2)}, u32[]{:S(2)}) collective-permute-start(bf16[16,4096]{1,0:T(8,128)(2,1)S(1)} %get-tuple-element.50), channel_id=1, source_target_pairs={{0,3},{1,2},{2,1},{3,0},{4,7},{5,6},{6,5},{7,4},{8,11},{9,10},{10,... | collective-permute-start | bytes 393224 | tf_op jit(solution)/shard_map/ppermute | solution.py:211
  23.0 8.7 %collective-permute-start.4 = (bf16[16,4096]{1,0:T(8,128)(2,1)S(1)}, bf16[16,4096]{1,0:T(8,128)(2,1)S(1)}, u32[]{:S(2)}, u32[]{:S(2)}) collective-permute-start(bf16[16,4096]{1,0:T(8,128)(2,1)S(1)} %get-tuple-element.51), channel_id=1, source_target_pairs={{0,16},{1,17},{2,18},{3,19},{4,20},{5,21},{6,22},{7,23},{8,24},{9,... | collective-permute-start | bytes 393224 | tf_op jit(solution)/shard_map/ppermute | solution.py:211
  24.5 14.3 %collective-permute-start.5 = (bf16[16,4096]{1,0:T(8,128)(2,1)S(1)}, bf16[16,4096]{1,0:T(8,128)(2,1)S(1)}, u32[]{:S(2)}, u32[]{:S(2)}) collective-permute-start(bf16[16,4096]{1,0:T(8,128)(2,1)S(1)} %get-tuple-element.52), channel_id=1, source_target_pairs={{0,17},{1,16},{2,19},{3,18},{4,21},{5,20},{6,23},{7,22},{8,25},{9,... | collective-permute-start | bytes 393224 | tf_op jit(solution)/shard_map/ppermute | solution.py:211
  27.2 12.5 %collective-permute-start.6 = (bf16[16,4096]{1,0:T(8,128)(2,1)S(1)}, bf16[16,4096]{1,0:T(8,128)(2,1)S(1)}, u32[]{:S(2)}, u32[]{:S(2)}) collective-permute-start(bf16[16,4096]{1,0:T(8,128)(2,1)S(1)} %get-tuple-element.53), channel_id=1, source_target_pairs={{0,18},{1,19},{2,16},{3,17},{4,22},{5,23},{6,20},{7,21},{8,26},{9,... | collective-permute-start | bytes 393224 | tf_op jit(solution)/shard_map/ppermute | solution.py:211
  28.9 11.1 %collective-permute-start.7 = (bf16[16,4096]{1,0:T(8,128)(2,1)S(1)}, bf16[16,4096]{1,0:T(8,128)(2,1)S(1)}, u32[]{:S(2)}, u32[]{:S(2)}) collective-permute-start(bf16[16,4096]{1,0:T(8,128)(2,1)S(1)} %get-tuple-element.54), channel_id=1, source_target_pairs={{0,19},{1,18},{2,17},{3,16},{4,23},{5,22},{6,21},{7,20},{8,27},{9,... | collective-permute-start | bytes 393224 | tf_op jit(solution)/shard_map/ppermute | solution.py:211
  30.1 11.8 %collective-permute-start.10 = (bf16[16,4096]{1,0:T(8,128)(2,1)S(1)}, bf16[16,4096]{1,0:T(8,128)(2,1)S(1)}, u32[]{:S(2)}, u32[]{:S(2)}) collective-permute-start(bf16[16,4096]{1,0:T(8,128)(2,1)S(1)} %get-tuple-element.56), channel_id=1, source_target_pairs={{0,1},{1,0},{2,3},{3,2},{4,5},{5,4},{6,7},{7,6},{8,9},{9,8},{10,11... | collective-permute-start | bytes 393224 | tf_op jit(solution)/shard_map/ppermute | solution.py:211
  31.7 11.7 %collective-permute-start.11 = (bf16[16,4096]{1,0:T(8,128)(2,1)S(1)}, bf16[16,4096]{1,0:T(8,128)(2,1)S(1)}, u32[]{:S(2)}, u32[]{:S(2)}) collective-permute-start(bf16[16,4096]{1,0:T(8,128)(2,1)S(1)} %get-tuple-element.57), channel_id=1, source_target_pairs={{0,2},{1,3},{2,0},{3,1},{4,6},{5,7},{6,4},{7,5},{8,10},{9,11},{10,... | collective-permute-start | bytes 393224 | tf_op jit(solution)/shard_map/ppermute | solution.py:211
  38.8 14.0 %collective-permute-start.12 = (bf16[16,4096]{1,0:T(8,128)(2,1)S(1)}, bf16[16,4096]{1,0:T(8,128)(2,1)S(1)}, u32[]{:S(2)}, u32[]{:S(2)}) collective-permute-start(bf16[16,4096]{1,0:T(8,128)(2,1)S(1)} %get-tuple-element.58), channel_id=1, source_target_pairs={{0,3},{1,2},{2,1},{3,0},{4,7},{5,6},{6,5},{7,4},{8,11},{9,10},{10,... | collective-permute-start | bytes 393224 | tf_op jit(solution)/shard_map/ppermute | solution.py:211
  39.7 13.2 %collective-permute-start.13 = (bf16[16,4096]{1,0:T(8,128)(2,1)S(1)}, bf16[16,4096]{1,0:T(8,128)(2,1)S(1)}, u32[]{:S(2)}, u32[]{:S(2)}) collective-permute-start(bf16[16,4096]{1,0:T(8,128)(2,1)S(1)} %get-tuple-element.59), channel_id=1, source_target_pairs={{0,16},{1,17},{2,18},{3,19},{4,20},{5,21},{6,22},{7,23},{8,24},{9,... | collective-permute-start | bytes 393224 | tf_op jit(solution)/shard_map/ppermute | solution.py:211
  40.0 12.8 %collective-permute-start.14 = (bf16[16,4096]{1,0:T(8,128)(2,1)S(1)}, bf16[16,4096]{1,0:T(8,128)(2,1)S(1)}, u32[]{:S(2)}, u32[]{:S(2)}) collective-permute-start(bf16[16,4096]{1,0:T(8,128)(2,1)S(1)} %get-tuple-element.60), channel_id=1, source_target_pairs={{0,17},{1,16},{2,19},{3,18},{4,21},{5,20},{6,23},{7,22},{8,25},{9,... | collective-permute-start | bytes 393224 | tf_op jit(solution)/shard_map/ppermute | solution.py:211
  41.9 10.9 %collective-permute-start.15 = (bf16[16,4096]{1,0:T(8,128)(2,1)S(1)}, bf16[16,4096]{1,0:T(8,128)(2,1)S(1)}, u32[]{:S(2)}, u32[]{:S(2)}) collective-permute-start(bf16[16,4096]{1,0:T(8,128)(2,1)S(1)} %get-tuple-element.61), channel_id=1, source_target_pairs={{0,18},{1,19},{2,16},{3,17},{4,22},{5,23},{6,20},{7,21},{8,26},{9,... | collective-permute-start | bytes 393224 | tf_op jit(solution)/shard_map/ppermute | solution.py:211
  43.4 9.5 %collective-permute-start.16 = (bf16[16,4096]{1,0:T(8,128)(2,1)S(1)}, bf16[16,4096]{1,0:T(8,128)(2,1)S(1)}, u32[]{:S(2)}, u32[]{:S(2)}) collective-permute-start(bf16[16,4096]{1,0:T(8,128)(2,1)S(1)} %get-tuple-element.62), channel_id=1, source_target_pairs={{0,19},{1,18},{2,17},{3,16},{4,23},{5,22},{6,21},{7,20},{8,27},{9,... | collective-permute-start | bytes 393224 | tf_op jit(solution)/shard_map/ppermute | solution.py:211
  52.9 47.1 %copy-start = (s32[1,32]{1,0:T(1,128)S(1)}, s32[1,32]{1,0:T(1,128)}, u32[]{:S(2)}) copy-start(s32[1,32]{1,0:T(1,128)} %query_ref.1) | copy-start | bytes 388
  63.4 5.8 %collective-permute-start.25 = (bf16[16,2560]{1,0:T(8,128)(2,1)S(1)}, bf16[16,2560]{1,0:T(8,128)(2,1)S(1)}, u32[]{:S(2)}, u32[]{:S(2)}) collective-permute-start(bf16[16,2560]{1,0:T(8,128)(2,1)S(1)} %get-tuple-element.81), channel_id=1, source_target_pairs={{0,1},{1,0},{2,3},{3,2},{4,5},{5,4},{6,7},{7,6},{8,9},{9,8},{10,11... | collective-permute-start | bytes 245768 | tf_op jit(solution)/shard_map/ppermute | solution.py:211
  64.3 6.4 %collective-permute-start.26 = (bf16[16,2560]{1,0:T(8,128)(2,1)S(1)}, bf16[16,2560]{1,0:T(8,128)(2,1)S(1)}, u32[]{:S(2)}, u32[]{:S(2)}) collective-permute-start(bf16[16,2560]{1,0:T(8,128)(2,1)S(1)} %get-tuple-element.82), channel_id=1, source_target_pairs={{0,2},{1,3},{2,0},{3,1},{4,6},{5,7},{6,4},{7,5},{8,10},{9,11},{10,... | collective-permute-start | bytes 245768 | tf_op jit(solution)/shard_map/ppermute | solution.py:211
  66.1 6.7 %collective-permute-start.27 = (bf16[16,2560]{1,0:T(8,128)(2,1)S(1)}, bf16[16,2560]{1,0:T(8,128)(2,1)S(1)}, u32[]{:S(2)}, u32[]{:S(2)}) collective-permute-start(bf16[16,2560]{1,0:T(8,128)(2,1)S(1)} %get-tuple-element.83), channel_id=1, source_target_pairs={{0,3},{1,2},{2,1},{3,0},{4,7},{5,6},{6,5},{7,4},{8,11},{9,10},{10,... | collective-permute-start | bytes 245768 | tf_op jit(solution)/shard_map/ppermute | solution.py:211
  66.9 6.7 %collective-permute-start.28 = (bf16[16,2560]{1,0:T(8,128)(2,1)S(1)}, bf16[16,2560]{1,0:T(8,128)(2,1)S(1)}, u32[]{:S(2)}, u32[]{:S(2)}) collective-permute-start(bf16[16,2560]{1,0:T(8,128)(2,1)S(1)} %get-tuple-element.84), channel_id=1, source_target_pairs={{0,16},{1,17},{2,18},{3,19},{4,20},{5,21},{6,22},{7,23},{8,24},{9,... | collective-permute-start | bytes 245768 | tf_op jit(solution)/shard_map/ppermute | solution.py:211
  67.8 7.6 %collective-permute-start.29 = (bf16[16,2560]{1,0:T(8,128)(2,1)S(1)}, bf16[16,2560]{1,0:T(8,128)(2,1)S(1)}, u32[]{:S(2)}, u32[]{:S(2)}) collective-permute-start(bf16[16,2560]{1,0:T(8,128)(2,1)S(1)} %get-tuple-element.85), channel_id=1, source_target_pairs={{0,17},{1,16},{2,19},{3,18},{4,21},{5,20},{6,23},{7,22},{8,25},{9,... | collective-permute-start | bytes 245768 | tf_op jit(solution)/shard_map/ppermute | solution.py:211
  69.2 7.1 %collective-permute-start.30 = (bf16[16,2560]{1,0:T(8,128)(2,1)S(1)}, bf16[16,2560]{1,0:T(8,128)(2,1)S(1)}, u32[]{:S(2)}, u32[]{:S(2)}) collective-permute-start(bf16[16,2560]{1,0:T(8,128)(2,1)S(1)} %get-tuple-element.86), channel_id=1, source_target_pairs={{0,18},{1,19},{2,16},{3,17},{4,22},{5,23},{6,20},{7,21},{8,26},{9,... | collective-permute-start | bytes 245768 | tf_op jit(solution)/shard_map/ppermute | solution.py:211
  70.7 6.3 %collective-permute-start.31 = (bf16[16,2560]{1,0:T(8,128)(2,1)S(1)}, bf16[16,2560]{1,0:T(8,128)(2,1)S(1)}, u32[]{:S(2)}, u32[]{:S(2)}) collective-permute-start(bf16[16,2560]{1,0:T(8,128)(2,1)S(1)} %get-tuple-element.87), channel_id=1, source_target_pairs={{0,19},{1,18},{2,17},{3,16},{4,23},{5,22},{6,21},{7,20},{8,27},{9,... | collective-permute-start | bytes 245768 | tf_op jit(solution)/shard_map/ppermute | solution.py:211
  72.8 6.4 %collective-permute-start.17 = (bf16[16,2560]{1,0:T(8,128)(2,1)S(1)}, bf16[16,2560]{1,0:T(8,128)(2,1)S(1)}, u32[]{:S(2)}, u32[]{:S(2)}) collective-permute-start(bf16[16,2560]{1,0:T(8,128)(2,1)S(1)} %get-tuple-element.70), channel_id=1, source_target_pairs={{0,1},{1,0},{2,3},{3,2},{4,5},{5,4},{6,7},{7,6},{8,9},{9,8},{10,11... | collective-permute-start | bytes 245768 | tf_op jit(solution)/shard_map/ppermute | solution.py:211
  73.6 6.3 %collective-permute-start.18 = (bf16[16,2560]{1,0:T(8,128)(2,1)S(1)}, bf16[16,2560]{1,0:T(8,128)(2,1)S(1)}, u32[]{:S(2)}, u32[]{:S(2)}) collective-permute-start(bf16[16,2560]{1,0:T(8,128)(2,1)S(1)} %get-tuple-element.71), channel_id=1, source_target_pairs={{0,2},{1,3},{2,0},{3,1},{4,6},{5,7},{6,4},{7,5},{8,10},{9,11},{10,... | collective-permute-start | bytes 245768 | tf_op jit(solution)/shard_map/ppermute | solution.py:211
  75.4 6.0 %collective-permute-start.19 = (bf16[16,2560]{1,0:T(8,128)(2,1)S(1)}, bf16[16,2560]{1,0:T(8,128)(2,1)S(1)}, u32[]{:S(2)}, u32[]{:S(2)}) collective-permute-start(bf16[16,2560]{1,0:T(8,128)(2,1)S(1)} %get-tuple-element.72), channel_id=1, source_target_pairs={{0,3},{1,2},{2,1},{3,0},{4,7},{5,6},{6,5},{7,4},{8,11},{9,10},{10,... | collective-permute-start | bytes 245768 | tf_op jit(solution)/shard_map/ppermute | solution.py:211
  77.2 11.3 %collective-permute-start.32 = (bf16[32,2560]{1,0:T(8,128)(2,1)S(1)}, bf16[32,2560]{1,0:T(8,128)(2,1)S(1)}, u32[]{:S(2)}, u32[]{:S(2)}) collective-permute-start(bf16[32,2560]{1,0:T(8,128)(2,1)S(1)} %get-tuple-element.89), channel_id=1, source_target_pairs={{0,8},{1,9},{2,10},{3,11},{4,12},{5,13},{6,14},{7,15},{8,0},{9,1},... | collective-permute-start | bytes 491528 | tf_op jit(solution)/shard_map/ppermute | solution.py:211
  77.3 8.5 %collective-permute-start.20 = (bf16[16,2560]{1,0:T(8,128)(2,1)S(1)}, bf16[16,2560]{1,0:T(8,128)(2,1)S(1)}, u32[]{:S(2)}, u32[]{:S(2)}) collective-permute-start(bf16[16,2560]{1,0:T(8,128)(2,1)S(1)} %get-tuple-element.73), channel_id=1, source_target_pairs={{0,16},{1,17},{2,18},{3,19},{4,20},{5,21},{6,22},{7,23},{8,24},{9,... | collective-permute-start | bytes 245768 | tf_op jit(solution)/shard_map/ppermute | solution.py:211
  79.2 6.7 %collective-permute-start.21 = (bf16[16,2560]{1,0:T(8,128)(2,1)S(1)}, bf16[16,2560]{1,0:T(8,128)(2,1)S(1)}, u32[]{:S(2)}, u32[]{:S(2)}) collective-permute-start(bf16[16,2560]{1,0:T(8,128)(2,1)S(1)} %get-tuple-element.74), channel_id=1, source_target_pairs={{0,17},{1,16},{2,19},{3,18},{4,21},{5,20},{6,23},{7,22},{8,25},{9,... | collective-permute-start | bytes 245768 | tf_op jit(solution)/shard_map/ppermute | solution.py:211
  79.9 6.6 %collective-permute-start.22 = (bf16[16,2560]{1,0:T(8,128)(2,1)S(1)}, bf16[16,2560]{1,0:T(8,128)(2,1)S(1)}, u32[]{:S(2)}, u32[]{:S(2)}) collective-permute-start(bf16[16,2560]{1,0:T(8,128)(2,1)S(1)} %get-tuple-element.75), channel_id=1, source_target_pairs={{0,18},{1,19},{2,16},{3,17},{4,22},{5,23},{6,20},{7,21},{8,26},{9,... | collective-permute-start | bytes 245768 | tf_op jit(solution)/shard_map/ppermute | solution.py:211
  81.5 6.7 %collective-permute-start.23 = (bf16[16,2560]{1,0:T(8,128)(2,1)S(1)}, bf16[16,2560]{1,0:T(8,128)(2,1)S(1)}, u32[]{:S(2)}, u32[]{:S(2)}) collective-permute-start(bf16[16,2560]{1,0:T(8,128)(2,1)S(1)} %get-tuple-element.76), channel_id=1, source_target_pairs={{0,19},{1,18},{2,17},{3,16},{4,23},{5,22},{6,21},{7,20},{8,27},{9,... | collective-permute-start | bytes 245768 | tf_op jit(solution)/shard_map/ppermute | solution.py:211
  88.4 3.2 %collective-permute-start.24 = (bf16[32,2560]{1,0:T(8,128)(2,1)S(1)}, bf16[32,2560]{1,0:T(8,128)(2,1)S(1)}, u32[]{:S(2)}, u32[]{:S(2)}) collective-permute-start(bf16[32,2560]{1,0:T(8,128)(2,1)S(1)} %get-tuple-element.78), channel_id=1, source_target_pairs={{0,8},{1,9},{2,10},{3,11},{4,12},{5,13},{6,14},{7,15},{8,0},{9,1},... | collective-permute-start | bytes 491528 | tf_op jit(solution)/shard_map/ppermute | solution.py:211
  88.5 11.5 %collective-permute-start.33 = (bf16[32,2560]{1,0:T(8,128)(2,1)S(1)}, bf16[32,2560]{1,0:T(8,128)(2,1)S(1)}, u32[]{:S(2)}, u32[]{:S(2)}) collective-permute-start(bf16[32,2560]{1,0:T(8,128)(2,1)S(1)} %shard_map.129), channel_id=1, source_target_pairs={{0,4},{1,5},{2,6},{3,7},{4,0},{5,1},{6,2},{7,3},{8,12},{9,13},{10,... | collective-permute-start | bytes 491528 | tf_op jit(solution)/shard_map/ppermute | solution.py:211

commit v5 on v4

--- a/solution.py
+++ b/solution.py
@@ -90,72 +90,64 @@
 
 
 def expert_kernel(count, group, *refs):
-    ins, weights, outs = refs[:count], refs[count : count + 6], refs[count + 6 : 2 * count + 6]
+    ins, weights, outs = refs[:count], refs[count : count + 6], refs[count + 6 : -1]
     gate, up, down, left_proj, right_proj, stored = weights
     outer_ref = refs[-1]
     experts, width, _ = gate.shape
     rank = left_proj.shape[1]
-    piece = ins[0].shape[0]
-    rows = piece * count
-    x = jnp.concatenate([r[:, :width] for r in ins], axis=0)
-    delta = jnp.concatenate([r[:, width:] for r in ins], axis=0)
-    owner = lax.broadcasted_iota(jnp.int32, (rows, 1), 0) // group % experts
-    left = jnp.zeros((rows, rank), F32)
-    right = jnp.zeros((rows, rank), F32)
-    grad = jnp.zeros((rows, width), F32)
+    half = count // 2
+    ins = [ins[i // 2 + i % 2 * half] for i in range(count)]
+    per = LANES // rank
+    rows = count * group
+    lane = lax.broadcasted_iota(jnp.int32, (rows, LANES), 1) // rank
     for j in range(experts):
-        mine = owner == j
+        part = slice(j * group, (j + 1) * group)
+        x = jnp.concatenate([r[part, :width] for r in ins], axis=0)
+        delta = jnp.concatenate([r[part, width:] for r in ins], axis=0)
         a_gate = dot(x, gate[j])
         a_up = dot(x, up[j])
         d_hidden = dot_nt(delta, down[j])
         sig = jax.nn.sigmoid(a_gate)
         active = a_gate * sig
         hidden = (active * a_up).astype(BF16)
-        grad_up = jnp.where(mine, d_hidden * active, 0.0).astype(BF16)
-        grad_gate = jnp.where(
-            mine, d_hidden * a_up * sig * (1.0 + a_gate * (1.0 - sig)), 0.0
-        ).astype(BF16)
-        grad = grad + dot_nt(grad_gate, gate[j])
-        grad = grad + dot_nt(grad_up, up[j])
-        left = jnp.where(mine, dot_nt(delta, left_proj[j]), left)
-        right = jnp.where(mine, dot_nt(hidden, right_proj[j]), right)
-    grad = grad.astype(BF16)
-    per = LANES // rank
-    wide = jnp.concatenate([right] * per, axis=1)
-    lane = lax.broadcasted_iota(jnp.int32, (rows, LANES), 1) // rank
-    for c in range(rank // per):
-        factor = left[:, c * per : c * per + 1]
-        for k in range(1, per):
-            factor = jnp.where(lane == k, left[:, c * per + k : c * per + k + 1], factor)
-        outer = factor * wide
-        for j in range(experts):
-            outer_ref[j, :, c * LANES : (c + 1) * LANES] = jnp.where(owner == j, outer, 0.0).astype(
-                BF16
-            )
-    score = jnp.zeros((rows, stored.shape[2]), F32)
-    for j in range(experts):
-        score = score + dot(outer_ref[j], stored[j])
-    score = score.astype(BF16)
-    for i, out in enumerate(outs):
-        out[:, :width] = grad[i * piece : (i + 1) * piece]
-        out[:, width:] = score[i * piece : (i + 1) * piece]
-
-
-def part_kernel(place_ref, *refs):
-    ins, keep_ref, give_ref = refs[:-2], refs[-2], refs[-1]
-    tok = keep_ref.shape[0]
-    total = dot(place_ref[...], jnp.concatenate([r[...] for r in ins], axis=0))
-    keep_ref[...] = total[:tok]
-    give_ref[...] = total[tok:].astype(BF16)
+        grad_up = (d_hidden * active).astype(BF16)
+        grad_gate = (d_hidden * a_up * sig * (1.0 + a_gate * (1.0 - sig))).astype(BF16)
+        grad = (dot_nt(grad_gate, gate[j]) + dot_nt(grad_up, up[j])).astype(BF16)
+        left = dot_nt(delta, left_proj[j])
+        right = dot_nt(hidden, right_proj[j])
+        wide = jnp.concatenate([right] * per, axis=1)
+        for c in range(rank // per):
+            factor = left[:, c * per : c * per + 1]
+            for k in range(1, per):
+                factor = jnp.where(lane == k, left[:, c * per + k : c * per + k + 1], factor)
+            outer_ref[j, :, c * LANES : (c + 1) * LANES] = (factor * wide).astype(BF16)
+        score = dot(outer_ref[j], stored[j]).astype(BF16)
+        for i in range(count):
+            here = slice(i * group, (i + 1) * group)
+            to = slice((i % 2 * experts + j) * group, (i % 2 * experts + j + 1) * group)
+            outs[i // 2][to, :width] = grad[here]
+            outs[i // 2][to, width:] = score[here]
+
+
+def part_kernel(own_ref, guest_ref, *refs):
+    ins, own_keep_ref, guest_keep_ref, give_ref = refs[:-3], refs[-3], refs[-2], refs[-1]
+    tok = own_keep_ref.shape[0]
+    piece = ins[0].shape[0] // 2
+    own = dot(own_ref[...], jnp.concatenate([r[:piece] for r in ins], axis=0))
+    guest = dot(guest_ref[...], jnp.concatenate([r[piece:] for r in ins], axis=0))
+    own_keep_ref[...] = own[:tok]
+    guest_keep_ref[...] = guest[:tok]
+    give_ref[:tok] = guest[tok:].astype(BF16)
+    give_ref[tok:] = own[tok:].astype(BF16)
 
 
 def join_kernel(keep_ref, more_ref, out_ref):
-    out_ref[...] = (keep_ref[...] + more_ref[...].astype(F32)).astype(BF16)
+    out_ref[...] = (keep_ref[...] + more_ref[: keep_ref.shape[0]].astype(F32)).astype(BF16)
 
 
 def final_kernel(keep_ref, more_ref, far_ref, query_ref, grad_ref, score_ref):
     width = grad_ref.shape[1]
-    total = keep_ref[...] + more_ref[...].astype(F32) + far_ref[...].astype(F32)
+    total = keep_ref[...] + more_ref[keep_ref.shape[0] :].astype(F32) + far_ref[...].astype(F32)
     grad_ref[...] = total[:, :width].astype(BF16)
     wanted = lax.broadcasted_iota(jnp.int32, (score_ref.shape[0], query_ref.shape[1]), 0)
     pick = jnp.where(query_ref[...] == wanted, 1.0, 0.0)
@@ -225,10 +217,6 @@
         kernel = functools.partial(pack_kernel, top, experts, capacity, deep)
         filled = call(kernel, outs, [SMEM, VMEM, VMEM], (here, first, second), limit=12 << 20)
         return filled[:-1], filled[-1]
-
-    def part(place, pieces):
-        outs = (shape((tok, width + train), F32), shape((tok, width + train), BF16))
-        return call(part_kernel, outs, [VMEM] * (1 + chips), (place, *pieces))
 
     inputs = tuple(in_hbm(v) for v in (expert_ids.T, gate_w.T, tokens, out_grad))
     pay = call(
@@ -258,25 +246,24 @@
     size = sum(w.size for w in weights)
     outs = call(
         functools.partial(expert_kernel, 2 * chips, PAIR * capacity),
-        (shape((piece, width + train), BF16),) * (2 * chips),
+        (shape((2 * piece, width + train), BF16),) * chips,
         [VMEM] * (2 * chips + len(weights)),
         (*own_rows, *guest_rows, *held),
-        scratch=[pltpu.VMEM((experts, rows, weights[5].shape[1]), BF16)],
+        scratch=[pltpu.VMEM((experts, rows // experts, weights[5].shape[1]), BF16)],
         flops=2 * rows * size,
         moved=2 * size,
         limit=rows * (76 << 10),
     )
-    guest_back = exchange(outs[chips:])
-    early = (chips - 1) // 2
-    moved = move(outs[:chips], order[:early])
-    moved.update(move(outs[:chips], order[early:]))
-    own_back = [outs[0]] + [moved[o] for o in range(1, chips)]
-    guest_keep, guest_give = part(guest_place, guest_back)
-    more = swap(guest_give, core=1)
+    keep = shape((tok, width + train), F32)
+    own_keep, guest_keep, give = call(
+        part_kernel,
+        (keep, keep, shape((PAIR * tok, width + train), BF16)),
+        [VMEM] * (2 + chips),
+        (own_place, guest_place, *exchange(outs)),
+    )
+    more = swap(give, core=1)
     far = call(join_kernel, shape((tok, width + train), BF16), [VMEM] * 2, (guest_keep, more))
     far = swap(far, half=1)
-    own_keep, own_give = part(own_place, own_back)
-    more = swap(own_give, core=1)
     return call(
         final_kernel,
         (shape((tok, width), BF16), shape((QRY_DEV, train), F32)),

time: 101 us -> 94.8 us (0.939)
  starting transfers between devices: 44.6 us -> 34.6 us
  waiting for transfers between devices: 32.7 us -> 37.8 us
  Pallas kernels: 22.6 us -> 21.4 us
    ppermute x34 -> x26, starting transfers between devices: 44.6 us -> 34.6 us  [swap(): return lax.ppermute(value, AXES, pairs)]
    ppermute x34 -> x26, waiting for transfers between devices: 32.7 us -> 37.8 us  [swap(): return lax.ppermute(value, AXES, pairs)]
    pallas_call x8 -> x7, Pallas kernels: 15.3 us -> 14.1 us  [call(): pl.pallas_call(kernel, out_shape=outs, in_specs=in_specs, out_specs=jax.t...]
  transfers between devices with their start and end apart: 34 -> 26, of which waited for: 8 -> 6; matrix products, arithmetic and copies ran while one was open for 0% -> 0% of each run, Pallas kernels for 10% -> 10%
where the time goes in v5:
time: 94.8 us; the launch traced here: 94.7 us
  waiting for transfers between devices  37.8 us (40%)
  starting transfers between devices  34.6 us (36%)
  Pallas kernels  21.4 us (23%)
    ppermute x26, waiting for transfers between devices, swap(): return lax.ppermute(value, AXES, pairs)  37.8 us
    ppermute x26, starting transfers between devices, swap(): return lax.ppermute(value, AXES, pairs)  34.6 us
    pallas_call x7, Pallas kernels, call(): pl.pallas_call(kernel, out_shape=outs, in_specs=in_specs, out_specs=jax.t...  14.1 us
    pallas_call x1, Pallas kernels, layer(): pl.pallas_call(load_kernel, out_shape=tuple((pltpu.VMEM(w.shape, w.dtype)...  7.28 us
  transfers between devices with their start and end apart: 26, of which 6 were waited for; matrix products, arithmetic and copies ran while one was open for 0% of the time, Pallas kernels for 10%

profile of v5, /device:TPU:0, one launch (start us, length us, event | category | flops | bytes accessed | tf_op | source)
XLA Modules:
  0.0 94.7 jit_solution(15296641422292773742)
XLA Ops:
  0.6 1.0 %shard_map.122.first_ref = bf16[32,4224]{1,0:T(8,128)(2,1)S(1)} custom-call(s32[4,32]{1,0:T(4,128)} %bitcast.10, bf16[4,32]{1,0:T(4,128)(2,1)} %bitcast.11, bf16[32,2048]{1,0:T(8,128)(2,1)} %x_hbm.1, bf16[32,2048]{1,0:T(8,128)(2,1)} %g_hbm.1), custom_call_target="tpu_custom_call" | custom-call | flops 1000000 | bytes 1000000 | tf_op jit(solution)/shard_map/pallas_call | solution.py:169
  1.7 4.1 %collective-permute-start.1 = (bf16[32,4224]{1,0:T(8,128)(2,1)S(1)}, bf16[32,4224]{1,0:T(8,128)(2,1)S(1)}, u32[]{:S(2)}, u32[]{:S(2)}) collective-permute-start(bf16[32,4224]{1,0:T(8,128)(2,1)S(1)} %shard_map.122.first_ref), channel_id=1, source_target_pairs={{0,4},{1,5},{2,6},{3,7},{4,0},{5,1},{6,2},{7,3},{8,12},{9,13},{10,... | collective-permute-start | bytes 811016 | tf_op jit(solution)/shard_map/ppermute | solution.py:203
  5.8 0.0 collective-permute-start
  5.8 12.3 %collective-permute-done.1.first_ref = bf16[32,4224]{1,0:T(8,128)(2,1)S(1)} collective-permute-done((bf16[32,4224]{1,0:T(8,128)(2,1)S(1)}, bf16[32,4224]{1,0:T(8,128)(2,1)S(1)}, u32[]{:S(2)}, u32[]{:S(2)}) %collective-permute-start.1) | collective-permute-done | bytes 270368 | tf_op jit(solution)/shard_map/ppermute | solution.py:203
  18.1 0.0 collective-permute-start.2
  18.1 0.1 pad_add_fusion.here_ref
  18.2 0.0 collective-permute-done.second_ref
  18.2 1.2 %shard_map.123 = (bf16[16,4096]{1,0:T(8,128)(2,1)S(1)}, bf16[16,4096]{1,0:T(8,128)(2,1)S(1)}, bf16[16,4096]{1,0:T(8,128)(2,1)S(1)}, bf16[16,4096]{1,0:T(8,128)(2...) custom-call(s32[4]{0:T(128)S(1)} %pad_add_fusion.here_ref, ...), custom_call_target="tpu_custom_call" | custom-call | flops 1000000 | bytes 1000000 | tf_op jit(solution)/shard_map/pallas_call | solution.py:169
  19.4 1.6 %collective-permute-start.3 = (bf16[16,4096]{1,0:T(8,128)(2,1)S(1)}, bf16[16,4096]{1,0:T(8,128)(2,1)S(1)}, u32[]{:S(2)}, u32[]{:S(2)}) collective-permute-start(bf16[16,4096]{1,0:T(8,128)(2,1)S(1)} %get-tuple-element.40), channel_id=1, source_target_pairs={{0,1},{1,0},{2,3},{3,2},{4,5},{5,4},{6,7},{7,6},{8,9},{9,8},{10,11... | collective-permute-start | bytes 393224 | tf_op jit(solution)/shard_map/ppermute | solution.py:203
  21.0 0.7 collective-permute-start.4
  21.7 1.3 %collective-permute-start.5 = (bf16[16,4096]{1,0:T(8,128)(2,1)S(1)}, bf16[16,4096]{1,0:T(8,128)(2,1)S(1)}, u32[]{:S(2)}, u32[]{:S(2)}) collective-permute-start(bf16[16,4096]{1,0:T(8,128)(2,1)S(1)} %get-tuple-element.42), channel_id=1, source_target_pairs={{0,3},{1,2},{2,1},{3,0},{4,7},{5,6},{6,5},{7,4},{8,11},{9,10},{10,... | collective-permute-start | bytes 393224 | tf_op jit(solution)/shard_map/ppermute | solution.py:203
  23.0 1.6 %collective-permute-start.6 = (bf16[16,4096]{1,0:T(8,128)(2,1)S(1)}, bf16[16,4096]{1,0:T(8,128)(2,1)S(1)}, u32[]{:S(2)}, u32[]{:S(2)}) collective-permute-start(bf16[16,4096]{1,0:T(8,128)(2,1)S(1)} %get-tuple-element.43), channel_id=1, source_target_pairs={{0,16},{1,17},{2,18},{3,19},{4,20},{5,21},{6,22},{7,23},{8,24},{9,... | collective-permute-start | bytes 393224 | tf_op jit(solution)/shard_map/ppermute | solution.py:203
  24.5 0.0 collective-permute-done.2.second_ref
  24.5 1.4 %collective-permute-start.7 = (bf16[16,4096]{1,0:T(8,128)(2,1)S(1)}, bf16[16,4096]{1,0:T(8,128)(2,1)S(1)}, u32[]{:S(2)}, u32[]{:S(2)}) collective-permute-start(bf16[16,4096]{1,0:T(8,128)(2,1)S(1)} %get-tuple-element.44), channel_id=1, source_target_pairs={{0,17},{1,16},{2,19},{3,18},{4,21},{5,20},{6,23},{7,22},{8,25},{9,... | collective-permute-start | bytes 393224 | tf_op jit(solution)/shard_map/ppermute | solution.py:203
  26.0 1.2 %shard_map.124 = (bf16[16,4096]{1,0:T(8,128)(2,1)S(1)}, bf16[16,4096]{1,0:T(8,128)(2,1)S(1)}, bf16[16,4096]{1,0:T(8,128)(2,1)S(1)}, bf16[16,4096]{1,0:T(8,128)(2...) custom-call(s32[4]{0:T(128)S(1)} %pad_add_fusion.here_ref, ...), custom_call_target="tpu_custom_call" | custom-call | flops 1000000 | bytes 1000000 | tf_op jit(solution)/shard_map/pallas_call | solution.py:169
  27.2 0.0 collective-permute-done.3.refs_1_
  27.2 1.7 %collective-permute-start.8 = (bf16[16,4096]{1,0:T(8,128)(2,1)S(1)}, bf16[16,4096]{1,0:T(8,128)(2,1)S(1)}, u32[]{:S(2)}, u32[]{:S(2)}) collective-permute-start(bf16[16,4096]{1,0:T(8,128)(2,1)S(1)} %get-tuple-element.45), channel_id=1, source_target_pairs={{0,18},{1,19},{2,16},{3,17},{4,22},{5,23},{6,20},{7,21},{8,26},{9,... | collective-permute-start | bytes 393224 | tf_op jit(solution)/shard_map/ppermute | solution.py:203
  28.9 1.2 %collective-permute-start.9 = (bf16[16,4096]{1,0:T(8,128)(2,1)S(1)}, bf16[16,4096]{1,0:T(8,128)(2,1)S(1)}, u32[]{:S(2)}, u32[]{:S(2)}) collective-permute-start(bf16[16,4096]{1,0:T(8,128)(2,1)S(1)} %get-tuple-element.46), channel_id=1, source_target_pairs={{0,19},{1,18},{2,17},{3,16},{4,23},{5,22},{6,21},{7,20},{8,27},{9,... | collective-permute-start | bytes 393224 | tf_op jit(solution)/shard_map/ppermute | solution.py:203
  30.1 1.5 %collective-permute-start.10 = (bf16[16,4096]{1,0:T(8,128)(2,1)S(1)}, bf16[16,4096]{1,0:T(8,128)(2,1)S(1)}, u32[]{:S(2)}, u32[]{:S(2)}) collective-permute-start(bf16[16,4096]{1,0:T(8,128)(2,1)S(1)} %get-tuple-element.48), channel_id=1, source_target_pairs={{0,1},{1,0},{2,3},{3,2},{4,5},{5,4},{6,7},{7,6},{8,9},{9,8},{10,11... | collective-permute-start | bytes 393224 | tf_op jit(solution)/shard_map/ppermute | solution.py:203
  31.7 0.0 collective-permute-done.6.refs_4_
  31.7 0.7 collective-permute-start.11
  32.4 6.4 %collective-permute-done.7.refs_5_ = bf16[16,4096]{1,0:T(8,128)(2,1)S(1)} collective-permute-done((bf16[16,4096]{1,0:T(8,128)(2,1)S(1)}, bf16[16,4096]{1,0:T(8,128)(2,1)S(1)}, u32[]{:S(2)}, u32[]{:S(2)}) %collective-permute-start.7) | collective-permute-done | bytes 131104 | tf_op jit(solution)/shard_map/ppermute | solution.py:203
  38.8 0.9 collective-permute-start.12
  39.7 0.0 collective-permute-done.8.refs_6_
  39.7 0.4 collective-permute-start.13
  40.0 0.0 collective-permute-done.9.refs_7_
  40.0 1.9 %collective-permute-start.14 = (bf16[16,4096]{1,0:T(8,128)(2,1)S(1)}, bf16[16,4096]{1,0:T(8,128)(2,1)S(1)}, u32[]{:S(2)}, u32[]{:S(2)}) collective-permute-start(bf16[16,4096]{1,0:T(8,128)(2,1)S(1)} %get-tuple-element.52), channel_id=1, source_target_pairs={{0,17},{1,16},{2,19},{3,18},{4,21},{5,20},{6,23},{7,22},{8,25},{9,... | collective-permute-start | bytes 393224 | tf_op jit(solution)/shard_map/ppermute | solution.py:203
  41.9 0.0 collective-permute-done.10.refs_9_
  41.9 1.5 %collective-permute-start.15 = (bf16[16,4096]{1,0:T(8,128)(2,1)S(1)}, bf16[16,4096]{1,0:T(8,128)(2,1)S(1)}, u32[]{:S(2)}, u32[]{:S(2)}) collective-permute-start(bf16[16,4096]{1,0:T(8,128)(2,1)S(1)} %get-tuple-element.53), channel_id=1, source_target_pairs={{0,18},{1,19},{2,16},{3,17},{4,22},{5,23},{6,20},{7,21},{8,26},{9,... | collective-permute-start | bytes 393224 | tf_op jit(solution)/shard_map/ppermute | solution.py:203
  43.4 2.1 %collective-permute-start.16 = (bf16[16,4096]{1,0:T(8,128)(2,1)S(1)}, bf16[16,4096]{1,0:T(8,128)(2,1)S(1)}, u32[]{:S(2)}, u32[]{:S(2)}) collective-permute-start(bf16[16,4096]{1,0:T(8,128)(2,1)S(1)} %get-tuple-element.54), channel_id=1, source_target_pairs={{0,19},{1,18},{2,17},{3,16},{4,23},{5,22},{6,21},{7,20},{8,27},{9,... | collective-permute-start | bytes 393224 | tf_op jit(solution)/shard_map/ppermute | solution.py:203
  45.5 7.3 %shard_map.125 = (bf16[2,2048,512]{2,1,0:T(8,128)(2,1)S(1)}, bf16[2,2048,512]{2,1,0:T(8,128)(2,1)S(1)}, bf16[2,512,2048]{2,1,0:T(8,128)(2,1)S(1)}, bf16[2,64,204...) custom-call(bf16[2,2048,512]{2,1,0:T(8,128)(2,1)} %refs_0_.1, ...), custom_call_target="tpu_custom_call" | custom-call | tf_op jit(solution)/shard_map/pallas_call | solution.py:237
  52.9 0.0 copy-start
  52.9 9.5 %shard_map.126 = (bf16[32,2560]{1,0:T(8,128)(2,1)S(1)}, bf16[32,2560]{1,0:T(8,128)(2,1)S(1)}, bf16[32,2560]{1,0:T(8,128)(2,1)S(1)}, bf16[32,2560]{1,0:T(8,128)(2...) custom-call(bf16[16,4096]{1,0:T(8,128)(2,1)S(1)} %get-tuple-element., ...), custom_call_target="tpu_custom_call" | custom-call | flops 5536481280 | bytes 21626880 | tf_op jit(solution)/shard_map/pallas_call | solution.py:169
  62.4 0.8 collective-permute-start.17
  63.2 1.8 %collective-permute-start.18 = (bf16[32,2560]{1,0:T(8,128)(2,1)S(1)}, bf16[32,2560]{1,0:T(8,128)(2,1)S(1)}, u32[]{:S(2)}, u32[]{:S(2)}) collective-permute-start(bf16[32,2560]{1,0:T(8,128)(2,1)S(1)} %get-tuple-element.63), channel_id=1, source_target_pairs={{0,2},{1,3},{2,0},{3,1},{4,6},{5,7},{6,4},{7,5},{8,10},{9,11},{10,... | collective-permute-start | bytes 491528 | tf_op jit(solution)/shard_map/ppermute | solution.py:203
  65.0 0.9 collective-permute-start.19
  65.9 0.9 collective-permute-start.20
  66.8 1.4 %collective-permute-start.21 = (bf16[32,2560]{1,0:T(8,128)(2,1)S(1)}, bf16[32,2560]{1,0:T(8,128)(2,1)S(1)}, u32[]{:S(2)}, u32[]{:S(2)}) collective-permute-start(bf16[32,2560]{1,0:T(8,128)(2,1)S(1)} %get-tuple-element.66), channel_id=1, source_target_pairs={{0,17},{1,16},{2,19},{3,18},{4,21},{5,20},{6,23},{7,22},{8,25},{9,... | collective-permute-start | bytes 491528 | tf_op jit(solution)/shard_map/ppermute | solution.py:203
  68.2 2.8 %collective-permute-done.17.refs_1_ = bf16[32,2560]{1,0:T(8,128)(2,1)S(1)} collective-permute-done((bf16[32,2560]{1,0:T(8,128)(2,1)S(1)}, bf16[32,2560]{1,0:T(8,128)(2,1)S(1)}, u32[]{:S(2)}, u32[]{:S(2)}) %collective-permute-start.17) | collective-permute-done | bytes 163872 | tf_op jit(solution)/shard_map/ppermute | solution.py:203
  71.0 0.5 collective-permute-start.22
  71.5 2.9 %collective-permute-start.23 = (bf16[32,2560]{1,0:T(8,128)(2,1)S(1)}, bf16[32,2560]{1,0:T(8,128)(2,1)S(1)}, u32[]{:S(2)}, u32[]{:S(2)}) collective-permute-start(bf16[32,2560]{1,0:T(8,128)(2,1)S(1)} %get-tuple-element.68), channel_id=1, source_target_pairs={{0,19},{1,18},{2,17},{3,16},{4,23},{5,22},{6,21},{7,20},{8,27},{9,... | collective-permute-start | bytes 491528 | tf_op jit(solution)/shard_map/ppermute | solution.py:203
  74.4 6.6 %collective-permute-done.20.refs_4_ = bf16[32,2560]{1,0:T(8,128)(2,1)S(1)} collective-permute-done((bf16[32,2560]{1,0:T(8,128)(2,1)S(1)}, bf16[32,2560]{1,0:T(8,128)(2,1)S(1)}, u32[]{:S(2)}, u32[]{:S(2)}) %collective-permute-start.20) | collective-permute-done | bytes 163872 | tf_op jit(solution)/shard_map/ppermute | solution.py:203
  81.0 0.3 shard_map.127
  81.3 0.1 collective-permute-start.24
  81.4 1.6 %collective-permute-done.24.more_ref = bf16[64,2560]{1,0:T(8,128)(2,1)S(1)} collective-permute-done((bf16[64,2560]{1,0:T(8,128)(2,1)S(1)}, bf16[64,2560]{1,0:T(8,128)(2,1)S(1)}, u32[]{:S(2)}, u32[]{:S(2)}) %collective-permute-start.24) | collective-permute-done | bytes 327712 | tf_op jit(solution)/shard_map/ppermute | solution.py:203
  83.1 2.8 %collective-permute-start.25 = (bf16[32,2560]{1,0:T(8,128)(2,1)S(1)}, bf16[32,2560]{1,0:T(8,128)(2,1)S(1)}, u32[]{:S(2)}, u32[]{:S(2)}) collective-permute-start(bf16[32,2560]{1,0:T(8,128)(2,1)S(1)} %shard_map.128), channel_id=1, source_target_pairs={{0,4},{1,5},{2,6},{3,7},{4,0},{5,1},{6,2},{7,3},{8,12},{9,13},{10,... | collective-permute-start | bytes 491528 | tf_op jit(solution)/shard_map/ppermute | solution.py:203
  85.9 8.0 %collective-permute-done.25.far_ref = bf16[32,2560]{1,0:T(8,128)(2,1)S(1)} collective-permute-done((bf16[32,2560]{1,0:T(8,128)(2,1)S(1)}, bf16[32,2560]{1,0:T(8,128)(2,1)S(1)}, u32[]{:S(2)}, u32[]{:S(2)}) %collective-permute-start.25) | collective-permute-done | bytes 163872 | tf_op jit(solution)/shard_map/ppermute | solution.py:203
  93.9 0.8 shard_map.129
  (15 shorter events, 0.1 us)
Async XLA Ops:
  1.7 16.4 %collective-permute-start.1 = (bf16[32,4224]{1,0:T(8,128)(2,1)S(1)}, bf16[32,4224]{1,0:T(8,128)(2,1)S(1)}, u32[]{:S(2)}, u32[]{:S(2)}) collective-permute-start(bf16[32,4224]{1,0:T(8,128)(2,1)S(1)} %shard_map.122.first_ref), channel_id=1, source_target_pairs={{0,4},{1,5},{2,6},{3,7},{4,0},{5,1},{6,2},{7,3},{8,12},{9,13},{10,... | collective-permute-start | bytes 811016 | tf_op jit(solution)/shard_map/ppermute | solution.py:203
  5.8 12.4 %collective-permute-start = (bf16[32,4224]{1,0:T(8,128)(2,1)S(1)}, bf16[32,4224]{1,0:T(8,128)(2,1)S(1)}, u32[]{:S(2)}, u32[]{:S(2)}) collective-permute-start(bf16[32,4224]{1,0:T(8,128)(2,1)S(1)} %shard_map.122.first_ref), channel_id=1, source_target_pairs={{0,8},{1,9},{2,10},{3,11},{4,12},{5,13},{6,14},{7,15},{8,0},{9,1},... | collective-permute-start | bytes 811016 | tf_op jit(solution)/shard_map/ppermute | solution.py:203
  18.1 6.4 %collective-permute-start.2 = (bf16[32,4224]{1,0:T(8,128)(2,1)S(1)}, bf16[32,4224]{1,0:T(8,128)(2,1)S(1)}, u32[]{:S(2)}, u32[]{:S(2)}) collective-permute-start(bf16[32,4224]{1,0:T(8,128)(2,1)S(1)} %collective-permute-done.1.first_ref), channel_id=1, source_target_pairs={{0,8},{1,9},{2,10},{3,11},{4,12},{5,13},{6,14},{7,15},{8,0},{9,1},... | collective-permute-start | bytes 811016 | tf_op jit(solution)/shard_map/ppermute | solution.py:203
  19.4 7.8 %collective-permute-start.3 = (bf16[16,4096]{1,0:T(8,128)(2,1)S(1)}, bf16[16,4096]{1,0:T(8,128)(2,1)S(1)}, u32[]{:S(2)}, u32[]{:S(2)}) collective-permute-start(bf16[16,4096]{1,0:T(8,128)(2,1)S(1)} %get-tuple-element.40), channel_id=1, source_target_pairs={{0,1},{1,0},{2,3},{3,2},{4,5},{5,4},{6,7},{7,6},{8,9},{9,8},{10,11... | collective-permute-start | bytes 393224 | tf_op jit(solution)/shard_map/ppermute | solution.py:203
  21.0 7.9 %collective-permute-start.4 = (bf16[16,4096]{1,0:T(8,128)(2,1)S(1)}, bf16[16,4096]{1,0:T(8,128)(2,1)S(1)}, u32[]{:S(2)}, u32[]{:S(2)}) collective-permute-start(bf16[16,4096]{1,0:T(8,128)(2,1)S(1)} %get-tuple-element.41), channel_id=1, source_target_pairs={{0,2},{1,3},{2,0},{3,1},{4,6},{5,7},{6,4},{7,5},{8,10},{9,11},{10,... | collective-permute-start | bytes 393224 | tf_op jit(solution)/shard_map/ppermute | solution.py:203
  21.7 8.4 %collective-permute-start.5 = (bf16[16,4096]{1,0:T(8,128)(2,1)S(1)}, bf16[16,4096]{1,0:T(8,128)(2,1)S(1)}, u32[]{:S(2)}, u32[]{:S(2)}) collective-permute-start(bf16[16,4096]{1,0:T(8,128)(2,1)S(1)} %get-tuple-element.42), channel_id=1, source_target_pairs={{0,3},{1,2},{2,1},{3,0},{4,7},{5,6},{6,5},{7,4},{8,11},{9,10},{10,... | collective-permute-start | bytes 393224 | tf_op jit(solution)/shard_map/ppermute | solution.py:203
  23.0 8.7 %collective-permute-start.6 = (bf16[16,4096]{1,0:T(8,128)(2,1)S(1)}, bf16[16,4096]{1,0:T(8,128)(2,1)S(1)}, u32[]{:S(2)}, u32[]{:S(2)}) collective-permute-start(bf16[16,4096]{1,0:T(8,128)(2,1)S(1)} %get-tuple-element.43), channel_id=1, source_target_pairs={{0,16},{1,17},{2,18},{3,19},{4,20},{5,21},{6,22},{7,23},{8,24},{9,... | collective-permute-start | bytes 393224 | tf_op jit(solution)/shard_map/ppermute | solution.py:203
  24.5 14.3 %collective-permute-start.7 = (bf16[16,4096]{1,0:T(8,128)(2,1)S(1)}, bf16[16,4096]{1,0:T(8,128)(2,1)S(1)}, u32[]{:S(2)}, u32[]{:S(2)}) collective-permute-start(bf16[16,4096]{1,0:T(8,128)(2,1)S(1)} %get-tuple-element.44), channel_id=1, source_target_pairs={{0,17},{1,16},{2,19},{3,18},{4,21},{5,20},{6,23},{7,22},{8,25},{9,... | collective-permute-start | bytes 393224 | tf_op jit(solution)/shard_map/ppermute | solution.py:203
  27.2 12.5 %collective-permute-start.8 = (bf16[16,4096]{1,0:T(8,128)(2,1)S(1)}, bf16[16,4096]{1,0:T(8,128)(2,1)S(1)}, u32[]{:S(2)}, u32[]{:S(2)}) collective-permute-start(bf16[16,4096]{1,0:T(8,128)(2,1)S(1)} %get-tuple-element.45), channel_id=1, source_target_pairs={{0,18},{1,19},{2,16},{3,17},{4,22},{5,23},{6,20},{7,21},{8,26},{9,... | collective-permute-start | bytes 393224 | tf_op jit(solution)/shard_map/ppermute | solution.py:203
  28.9 11.1 %collective-permute-start.9 = (bf16[16,4096]{1,0:T(8,128)(2,1)S(1)}, bf16[16,4096]{1,0:T(8,128)(2,1)S(1)}, u32[]{:S(2)}, u32[]{:S(2)}) collective-permute-start(bf16[16,4096]{1,0:T(8,128)(2,1)S(1)} %get-tuple-element.46), channel_id=1, source_target_pairs={{0,19},{1,18},{2,17},{3,16},{4,23},{5,22},{6,21},{7,20},{8,27},{9,... | collective-permute-start | bytes 393224 | tf_op jit(solution)/shard_map/ppermute | solution.py:203
  30.1 11.8 %collective-permute-start.10 = (bf16[16,4096]{1,0:T(8,128)(2,1)S(1)}, bf16[16,4096]{1,0:T(8,128)(2,1)S(1)}, u32[]{:S(2)}, u32[]{:S(2)}) collective-permute-start(bf16[16,4096]{1,0:T(8,128)(2,1)S(1)} %get-tuple-element.48), channel_id=1, source_target_pairs={{0,1},{1,0},{2,3},{3,2},{4,5},{5,4},{6,7},{7,6},{8,9},{9,8},{10,11... | collective-permute-start | bytes 393224 | tf_op jit(solution)/shard_map/ppermute | solution.py:203
  31.7 11.7 %collective-permute-start.11 = (bf16[16,4096]{1,0:T(8,128)(2,1)S(1)}, bf16[16,4096]{1,0:T(8,128)(2,1)S(1)}, u32[]{:S(2)}, u32[]{:S(2)}) collective-permute-start(bf16[16,4096]{1,0:T(8,128)(2,1)S(1)} %get-tuple-element.49), channel_id=1, source_target_pairs={{0,2},{1,3},{2,0},{3,1},{4,6},{5,7},{6,4},{7,5},{8,10},{9,11},{10,... | collective-permute-start | bytes 393224 | tf_op jit(solution)/shard_map/ppermute | solution.py:203
  38.8 14.0 %collective-permute-start.12 = (bf16[16,4096]{1,0:T(8,128)(2,1)S(1)}, bf16[16,4096]{1,0:T(8,128)(2,1)S(1)}, u32[]{:S(2)}, u32[]{:S(2)}) collective-permute-start(bf16[16,4096]{1,0:T(8,128)(2,1)S(1)} %get-tuple-element.50), channel_id=1, source_target_pairs={{0,3},{1,2},{2,1},{3,0},{4,7},{5,6},{6,5},{7,4},{8,11},{9,10},{10,... | collective-permute-start | bytes 393224 | tf_op jit(solution)/shard_map/ppermute | solution.py:203
  39.7 13.2 %collective-permute-start.13 = (bf16[16,4096]{1,0:T(8,128)(2,1)S(1)}, bf16[16,4096]{1,0:T(8,128)(2,1)S(1)}, u32[]{:S(2)}, u32[]{:S(2)}) collective-permute-start(bf16[16,4096]{1,0:T(8,128)(2,1)S(1)} %get-tuple-element.51), channel_id=1, source_target_pairs={{0,16},{1,17},{2,18},{3,19},{4,20},{5,21},{6,22},{7,23},{8,24},{9,... | collective-permute-start | bytes 393224 | tf_op jit(solution)/shard_map/ppermute | solution.py:203
  40.0 12.8 %collective-permute-start.14 = (bf16[16,4096]{1,0:T(8,128)(2,1)S(1)}, bf16[16,4096]{1,0:T(8,128)(2,1)S(1)}, u32[]{:S(2)}, u32[]{:S(2)}) collective-permute-start(bf16[16,4096]{1,0:T(8,128)(2,1)S(1)} %get-tuple-element.52), channel_id=1, source_target_pairs={{0,17},{1,16},{2,19},{3,18},{4,21},{5,20},{6,23},{7,22},{8,25},{9,... | collective-permute-start | bytes 393224 | tf_op jit(solution)/shard_map/ppermute | solution.py:203
  41.9 10.9 %collective-permute-start.15 = (bf16[16,4096]{1,0:T(8,128)(2,1)S(1)}, bf16[16,4096]{1,0:T(8,128)(2,1)S(1)}, u32[]{:S(2)}, u32[]{:S(2)}) collective-permute-start(bf16[16,4096]{1,0:T(8,128)(2,1)S(1)} %get-tuple-element.53), channel_id=1, source_target_pairs={{0,18},{1,19},{2,16},{3,17},{4,22},{5,23},{6,20},{7,21},{8,26},{9,... | collective-permute-start | bytes 393224 | tf_op jit(solution)/shard_map/ppermute | solution.py:203
  43.4 9.5 %collective-permute-start.16 = (bf16[16,4096]{1,0:T(8,128)(2,1)S(1)}, bf16[16,4096]{1,0:T(8,128)(2,1)S(1)}, u32[]{:S(2)}, u32[]{:S(2)}) collective-permute-start(bf16[16,4096]{1,0:T(8,128)(2,1)S(1)} %get-tuple-element.54), channel_id=1, source_target_pairs={{0,19},{1,18},{2,17},{3,16},{4,23},{5,22},{6,21},{7,20},{8,27},{9,... | collective-permute-start | bytes 393224 | tf_op jit(solution)/shard_map/ppermute | solution.py:203
  52.9 41.0 %copy-start = (s32[1,32]{1,0:T(1,128)S(1)}, s32[1,32]{1,0:T(1,128)}, u32[]{:S(2)}) copy-start(s32[1,32]{1,0:T(1,128)} %query_ref.1) | copy-start | bytes 388
  62.4 8.6 %collective-permute-start.17 = (bf16[32,2560]{1,0:T(8,128)(2,1)S(1)}, bf16[32,2560]{1,0:T(8,128)(2,1)S(1)}, u32[]{:S(2)}, u32[]{:S(2)}) collective-permute-start(bf16[32,2560]{1,0:T(8,128)(2,1)S(1)} %get-tuple-element.62), channel_id=1, source_target_pairs={{0,1},{1,0},{2,3},{3,2},{4,5},{5,4},{6,7},{7,6},{8,9},{9,8},{10,11... | collective-permute-start | bytes 491528 | tf_op jit(solution)/shard_map/ppermute | solution.py:203
  63.2 8.3 %collective-permute-start.18 = (bf16[32,2560]{1,0:T(8,128)(2,1)S(1)}, bf16[32,2560]{1,0:T(8,128)(2,1)S(1)}, u32[]{:S(2)}, u32[]{:S(2)}) collective-permute-start(bf16[32,2560]{1,0:T(8,128)(2,1)S(1)} %get-tuple-element.63), channel_id=1, source_target_pairs={{0,2},{1,3},{2,0},{3,1},{4,6},{5,7},{6,4},{7,5},{8,10},{9,11},{10,... | collective-permute-start | bytes 491528 | tf_op jit(solution)/shard_map/ppermute | solution.py:203
  65.0 9.4 %collective-permute-start.19 = (bf16[32,2560]{1,0:T(8,128)(2,1)S(1)}, bf16[32,2560]{1,0:T(8,128)(2,1)S(1)}, u32[]{:S(2)}, u32[]{:S(2)}) collective-permute-start(bf16[32,2560]{1,0:T(8,128)(2,1)S(1)} %get-tuple-element.64), channel_id=1, source_target_pairs={{0,3},{1,2},{2,1},{3,0},{4,7},{5,6},{6,5},{7,4},{8,11},{9,10},{10,... | collective-permute-start | bytes 491528 | tf_op jit(solution)/shard_map/ppermute | solution.py:203
  65.9 15.1 %collective-permute-start.20 = (bf16[32,2560]{1,0:T(8,128)(2,1)S(1)}, bf16[32,2560]{1,0:T(8,128)(2,1)S(1)}, u32[]{:S(2)}, u32[]{:S(2)}) collective-permute-start(bf16[32,2560]{1,0:T(8,128)(2,1)S(1)} %get-tuple-element.65), channel_id=1, source_target_pairs={{0,16},{1,17},{2,18},{3,19},{4,20},{5,21},{6,22},{7,23},{8,24},{9,... | collective-permute-start | bytes 491528 | tf_op jit(solution)/shard_map/ppermute | solution.py:203
  66.8 14.2 %collective-permute-start.21 = (bf16[32,2560]{1,0:T(8,128)(2,1)S(1)}, bf16[32,2560]{1,0:T(8,128)(2,1)S(1)}, u32[]{:S(2)}, u32[]{:S(2)}) collective-permute-start(bf16[32,2560]{1,0:T(8,128)(2,1)S(1)} %get-tuple-element.66), channel_id=1, source_target_pairs={{0,17},{1,16},{2,19},{3,18},{4,21},{5,20},{6,23},{7,22},{8,25},{9,... | collective-permute-start | bytes 491528 | tf_op jit(solution)/shard_map/ppermute | solution.py:203
  71.0 10.0 %collective-permute-start.22 = (bf16[32,2560]{1,0:T(8,128)(2,1)S(1)}, bf16[32,2560]{1,0:T(8,128)(2,1)S(1)}, u32[]{:S(2)}, u32[]{:S(2)}) collective-permute-start(bf16[32,2560]{1,0:T(8,128)(2,1)S(1)} %get-tuple-element.67), channel_id=1, source_target_pairs={{0,18},{1,19},{2,16},{3,17},{4,22},{5,23},{6,20},{7,21},{8,26},{9,... | collective-permute-start | bytes 491528 | tf_op jit(solution)/shard_map/ppermute | solution.py:203
  71.5 9.5 %collective-permute-start.23 = (bf16[32,2560]{1,0:T(8,128)(2,1)S(1)}, bf16[32,2560]{1,0:T(8,128)(2,1)S(1)}, u32[]{:S(2)}, u32[]{:S(2)}) collective-permute-start(bf16[32,2560]{1,0:T(8,128)(2,1)S(1)} %get-tuple-element.68), channel_id=1, source_target_pairs={{0,19},{1,18},{2,17},{3,16},{4,23},{5,22},{6,21},{7,20},{8,27},{9,... | collective-permute-start | bytes 491528 | tf_op jit(solution)/shard_map/ppermute | solution.py:203
  81.3 1.7 %collective-permute-start.24 = (bf16[64,2560]{1,0:T(8,128)(2,1)S(1)}, bf16[64,2560]{1,0:T(8,128)(2,1)S(1)}, u32[]{:S(2)}, u32[]{:S(2)}) collective-permute-start(bf16[64,2560]{1,0:T(8,128)(2,1)S(1)} %get-tuple-element.70), channel_id=1, source_target_pairs={{0,8},{1,9},{2,10},{3,11},{4,12},{5,13},{6,14},{7,15},{8,0},{9,1},... | collective-permute-start | bytes 983048 | tf_op jit(solution)/shard_map/ppermute | solution.py:203
  83.1 10.8 %collective-permute-start.25 = (bf16[32,2560]{1,0:T(8,128)(2,1)S(1)}, bf16[32,2560]{1,0:T(8,128)(2,1)S(1)}, u32[]{:S(2)}, u32[]{:S(2)}) collective-permute-start(bf16[32,2560]{1,0:T(8,128)(2,1)S(1)} %shard_map.128), channel_id=1, source_target_pairs={{0,4},{1,5},{2,6},{3,7},{4,0},{5,1},{6,2},{7,3},{8,12},{9,13},{10,... | collective-permute-start | bytes 491528 | tf_op jit(solution)/shard_map/ppermute | solution.py:203

commit v6 on v5

--- a/solution.py
+++ b/solution.py
@@ -25,27 +25,35 @@
     return lax.dot_general(a, b, NT, preferred_element_type=F32)
 
 
-def pay_kernel(ids_hbm, w_hbm, x_hbm, g_hbm, pay_ref, ids_ref, w_ref, x_ref, g_ref, sem):
+def pay_kernel(
+    ids_hbm, w_hbm, query_hbm, x_hbm, g_hbm, pay_ref, ids_ref, w_ref, query_ref, x_ref, g_ref, sem
+):
     top, tok = ids_ref.shape
     width = x_ref.shape[1]
-    pairs = ((ids_hbm, ids_ref), (w_hbm, w_ref), (x_hbm, x_ref), (g_hbm, g_ref))
+    pairs = (
+        (ids_hbm, ids_ref),
+        (w_hbm, w_ref),
+        (query_hbm, query_ref),
+        (x_hbm, x_ref),
+        (g_hbm, g_ref),
+    )
     copies = [pltpu.make_async_copy(a, b, sem.at[i]) for i, (a, b) in enumerate(pairs)]
     for copy in copies:
         copy.start()
-    copies[0].wait()
-    copies[1].wait()
-    flat = jnp.concatenate([ids_ref[...].astype(F32), w_ref[...].astype(F32)], axis=0)
-    flat = jnp.concatenate([flat, jnp.zeros((LANES - 2 * top, tok), F32)], axis=0)
+    for copy in copies[:3]:
+        copy.wait()
+    parts = [ids_ref[...].astype(F32), w_ref[...].astype(F32), query_ref[...].astype(F32)]
+    flat = jnp.concatenate(parts + [jnp.zeros((LANES - 2 * top - 1, tok), F32)], axis=0)
     flat = jnp.concatenate([flat, jnp.zeros((LANES, LANES - tok), F32)], axis=1)
     pay_ref[:, 2 * width :] = flat.T[:tok, :].astype(BF16)
-    copies[2].wait()
+    copies[3].wait()
     pay_ref[:, :width] = x_ref[...]
-    copies[3].wait()
+    copies[4].wait()
     pay_ref[:, width : 2 * width] = g_ref[...]
 
 
 def pack_kernel(top, experts, capacity, deep, here_ref, first_ref, second_ref, *outs):
-    place_ref, sends = outs[-1], outs[:-1]
+    place_ref, tally_ref, sends = outs[-2], outs[-1], outs[:-2]
     tok = first_ref.shape[0]
     width = sends[0].shape[1] // 2
     piece = sends[0].shape[0]
@@ -70,6 +78,12 @@
     earlier = dot(jnp.where(col < row, 1.0, 0.0).astype(BF16), named.astype(BF16))
     place = jnp.where(earlier == (slot % capacity).astype(F32), named, 0.0)
     place_ref[...] = place.astype(BF16)
+    asked = lax.broadcasted_iota(jnp.int32, (PAIR * tok, LANES), 1)
+    whose = lax.broadcasted_iota(jnp.int32, (PAIR * tok, LANES), 0) // tok
+    query = meta[:, 2 * top : 2 * top + 1] + (whose * QRY_DEV).astype(F32)
+    asked = jnp.where(query == asked.astype(F32), 1.0, 0.0)
+    tally = dot(asked.T[: PAIR * QRY_DEV].astype(BF16), place.astype(BF16))
+    tally_ref[...] = tally.astype(BF16)
     pick = place.T.astype(BF16)
     scale = jnp.sum((place * weight).T, axis=1, keepdims=True)
     x = dot(pick, both[:, :width]).astype(BF16)
@@ -100,60 +114,95 @@
     per = LANES // rank
     rows = count * group
     lane = lax.broadcasted_iota(jnp.int32, (rows, LANES), 1) // rank
-    for j in range(experts):
+
+    def front(j):
         part = slice(j * group, (j + 1) * group)
         x = jnp.concatenate([r[part, :width] for r in ins], axis=0)
         delta = jnp.concatenate([r[part, width:] for r in ins], axis=0)
-        a_gate = dot(x, gate[j])
-        a_up = dot(x, up[j])
-        d_hidden = dot_nt(delta, down[j])
+        left = dot_nt(delta, left_proj[j])
+        return dot(x, gate[j]), dot(x, up[j]), dot_nt(delta, down[j]), left
+
+    def middle(j, a_gate, a_up, d_hidden, left):
         sig = jax.nn.sigmoid(a_gate)
         active = a_gate * sig
         hidden = (active * a_up).astype(BF16)
+        right = dot_nt(hidden, right_proj[j])
         grad_up = (d_hidden * active).astype(BF16)
         grad_gate = (d_hidden * a_up * sig * (1.0 + a_gate * (1.0 - sig))).astype(BF16)
-        grad = (dot_nt(grad_gate, gate[j]) + dot_nt(grad_up, up[j])).astype(BF16)
-        left = dot_nt(delta, left_proj[j])
-        right = dot_nt(hidden, right_proj[j])
+        return grad_gate, grad_up, left, right
+
+    def outers(j, left, right):
         wide = jnp.concatenate([right] * per, axis=1)
         for c in range(rank // per):
             factor = left[:, c * per : c * per + 1]
             for k in range(1, per):
                 factor = jnp.where(lane == k, left[:, c * per + k : c * per + k + 1], factor)
             outer_ref[j, :, c * LANES : (c + 1) * LANES] = (factor * wide).astype(BF16)
-        score = dot(outer_ref[j], stored[j]).astype(BF16)
+
+    def put(j, value, columns):
+        value = value.astype(BF16)
         for i in range(count):
-            here = slice(i * group, (i + 1) * group)
             to = slice((i % 2 * experts + j) * group, (i % 2 * experts + j + 1) * group)
-            outs[i // 2][to, :width] = grad[here]
-            outs[i // 2][to, width:] = score[here]
-
-
-def part_kernel(own_ref, guest_ref, *refs):
+            outs[i // 2][to, columns] = value[i * group : (i + 1) * group]
+
+    def grads(j, grad_gate, grad_up):
+        put(j, dot_nt(grad_gate, gate[j]) + dot_nt(grad_up, up[j]), slice(0, width))
+
+    def scores(j):
+        put(j, dot(outer_ref[j], stored[j]), slice(width, width + stored.shape[2]))
+
+    every = range(experts)
+    second = []
+    for j in every:
+        second.append(middle(j, *front(j)))
+    for j in every:
+        outers(j, *second[j][2:])
+        grads(j, *second[j][:2])
+        scores(j)
+
+
+def part_kernel(own_ref, own_tally_ref, guest_ref, guest_tally_ref, *refs):
     ins, own_keep_ref, guest_keep_ref, give_ref = refs[:-3], refs[-3], refs[-2], refs[-1]
-    tok = own_keep_ref.shape[0]
+    tok, span = own_keep_ref.shape
+    width = span - LANES
     piece = ins[0].shape[0] // 2
-    own = dot(own_ref[...], jnp.concatenate([r[:piece] for r in ins], axis=0))
-    guest = dot(guest_ref[...], jnp.concatenate([r[piece:] for r in ins], axis=0))
-    own_keep_ref[...] = own[:tok]
-    guest_keep_ref[...] = guest[:tok]
-    give_ref[:tok] = guest[tok:].astype(BF16)
-    give_ref[tok:] = own[tok:].astype(BF16)
+
+    def token_sums(place_ref, tally_ref, part):
+        grads = jnp.concatenate([r[part, :width] for r in ins], axis=0)
+        scores = jnp.concatenate([r[part, width:] for r in ins], axis=0)
+        total, tally = dot(place_ref[...], grads), dot(tally_ref[...], scores)
+
+        def fold(block):
+            rows = tally[block * QRY_DEV : (block + 1) * QRY_DEV]
+            return jnp.concatenate(
+                [rows[:, i : i + LANES] for i in range(0, rows.shape[1], LANES)], axis=0
+            )
+
+        return total, fold
+
+    own, own_fold = token_sums(own_ref, own_tally_ref, slice(0, piece))
+    guest, guest_fold = token_sums(guest_ref, guest_tally_ref, slice(piece, 2 * piece))
+    own_keep_ref[:, :width] = own[:tok]
+    own_keep_ref[:, width:] = own_fold(0)
+    guest_keep_ref[:, :width] = guest[:tok]
+    guest_keep_ref[:, width:] = guest_fold(0)
+    give_ref[:tok, :width] = guest[tok:].astype(BF16)
+    give_ref[:tok, width:] = guest_fold(1).astype(BF16)
+    give_ref[tok:, :width] = own[tok:].astype(BF16)
+    give_ref[tok:, width:] = own_fold(1).astype(BF16)
 
 
 def join_kernel(keep_ref, more_ref, out_ref):
     out_ref[...] = (keep_ref[...] + more_ref[: keep_ref.shape[0]].astype(F32)).astype(BF16)
 
 
-def final_kernel(keep_ref, more_ref, far_ref, query_ref, grad_ref, score_ref):
-    width = grad_ref.shape[1]
-    total = keep_ref[...] + more_ref[keep_ref.shape[0] :].astype(F32) + far_ref[...].astype(F32)
+def final_kernel(keep_ref, more_ref, far_ref, grad_ref, score_ref):
+    tok, width = grad_ref.shape
+    total = keep_ref[...] + more_ref[tok:].astype(F32) + far_ref[...].astype(F32)
     grad_ref[...] = total[:, :width].astype(BF16)
-    wanted = lax.broadcasted_iota(jnp.int32, (score_ref.shape[0], query_ref.shape[1]), 0)
-    pick = jnp.where(query_ref[...] == wanted, 1.0, 0.0)
-    score_ref[...] = jnp.dot(
-        pick, total[:, width:], precision=lax.Precision.HIGHEST, preferred_element_type=F32
-    )
+    for i in range(tok // QRY_DEV):
+        part = total[i * QRY_DEV : (i + 1) * QRY_DEV, width:]
+        score_ref[:, i * LANES : (i + 1) * LANES] = part
 
 
 VMEM = pl.BlockSpec(memory_space=pltpu.VMEM)
@@ -214,15 +263,16 @@
     def pack(first, second):
         outs = (shape((piece, 2 * width), BF16),) * chips
         outs += (shape((PAIR * tok, piece * chips), BF16),)
+        outs += (shape((PAIR * QRY_DEV, piece * chips), BF16),)
         kernel = functools.partial(pack_kernel, top, experts, capacity, deep)
         filled = call(kernel, outs, [SMEM, VMEM, VMEM], (here, first, second), limit=12 << 20)
-        return filled[:-1], filled[-1]
-
-    inputs = tuple(in_hbm(v) for v in (expert_ids.T, gate_w.T, tokens, out_grad))
+        return filled[:-2], filled[-2:]
+
+    inputs = tuple(in_hbm(v) for v in (expert_ids.T, gate_w.T, query_ids, tokens, out_grad))
     pay = call(
         pay_kernel,
         shape((tok, 2 * width + LANES), BF16),
-        [HBM] * 4,
+        [HBM] * len(inputs),
         inputs,
         scratch=[pltpu.VMEM(v.shape, v.dtype) for v in inputs]
         + [pltpu.SemaphoreType.DMA((len(inputs),))],
@@ -254,21 +304,22 @@
         moved=2 * size,
         limit=rows * (76 << 10),
     )
-    keep = shape((tok, width + train), F32)
+    assert QRY_DEV * train == tok * LANES
+    keep = shape((tok, width + LANES), F32)
     own_keep, guest_keep, give = call(
         part_kernel,
-        (keep, keep, shape((PAIR * tok, width + train), BF16)),
-        [VMEM] * (2 + chips),
-        (own_place, guest_place, *exchange(outs)),
+        (keep, keep, shape((PAIR * tok, width + LANES), BF16)),
+        [VMEM] * (4 + chips),
+        (*own_place, *guest_place, *exchange(outs)),
     )
     more = swap(give, core=1)
-    far = call(join_kernel, shape((tok, width + train), BF16), [VMEM] * 2, (guest_keep, more))
+    far = call(join_kernel, shape((tok, width + LANES), BF16), [VMEM] * 2, (guest_keep, more))
     far = swap(far, half=1)
     return call(
         final_kernel,
         (shape((tok, width), BF16), shape((QRY_DEV, train), F32)),
-        [VMEM] * 4,
-        (own_keep, more, far, query_ids),
+        [VMEM] * 3,
+        (own_keep, more, far),
     )
 
 

time: 94.8 us -> 90.8 us (0.958)
  Pallas kernels: 21.4 us -> 18.5 us
  waiting for transfers between devices: 37.8 us -> 36.6 us
    pallas_call x7, Pallas kernels: 14.1 us -> 11.2 us  [call(): pl.pallas_call(kernel, out_shape=outs, in_specs=in_specs, out_specs=jax.t...]
    ppermute x26, waiting for transfers between devices: 37.8 us -> 36.6 us  [swap(): return lax.ppermute(value, AXES, pairs)]
  transfers between devices with their start and end apart: 26 -> 26, of which waited for: 6 -> 6; matrix products, arithmetic and copies ran while one was open for 0% -> 0% of each run, Pallas kernels for 10% -> 11%
where the time goes in v6:
time: 90.8 us; the launch traced here: 90.6 us
  waiting for transfers between devices  36.6 us (40%)
  starting transfers between devices  34.7 us (38%)
  Pallas kernels  18.5 us (20%)
    ppermute x26, waiting for transfers between devices, swap(): return lax.ppermute(value, AXES, pairs)  36.6 us
    ppermute x26, starting transfers between devices, swap(): return lax.ppermute(value, AXES, pairs)  34.7 us
    pallas_call x7, Pallas kernels, call(): pl.pallas_call(kernel, out_shape=outs, in_specs=in_specs, out_specs=jax.t...  11.2 us
    pallas_call x1, Pallas kernels, layer(): pl.pallas_call(load_kernel, out_shape=tuple((pltpu.VMEM(w.shape, w.dtype)...  7.28 us
  transfers between devices with their start and end apart: 26, of which 6 were waited for; matrix products, arithmetic and copies ran while one was open for 0% of the time, Pallas kernels for 11%

profile of v6, /device:TPU:0, one launch (start us, length us, event | category | flops | bytes accessed | tf_op | source)
XLA Modules:
  0.0 90.6 jit_solution(16220793013720474558)
XLA Ops:
  0.6 1.1 %shard_map.122.first_ref = bf16[32,4224]{1,0:T(8,128)(2,1)S(1)} custom-call(s32[4,32]{1,0:T(4,128)} %bitcast.10, bf16[4,32]{1,0:T(4,128)(2,1)} %bitcast.11, s32[1,32]{1,0:T(1,128)} %query_hbm.1, bf16[32,2048]{1,0:T(8,128)(2,1)} %x_hbm.1, bf16[32,2048]{1,0:T(8,128)(2,1)} %g_hbm.1), custom_call_target="tpu_custom_call" | custom-call | flops 1000000 | bytes 1000000 | tf_op jit(solution)/shard_map/pallas_call | solution.py:218
  1.7 4.1 %collective-permute-start.1 = (bf16[32,4224]{1,0:T(8,128)(2,1)S(1)}, bf16[32,4224]{1,0:T(8,128)(2,1)S(1)}, u32[]{:S(2)}, u32[]{:S(2)}) collective-permute-start(bf16[32,4224]{1,0:T(8,128)(2,1)S(1)} %shard_map.122.first_ref), channel_id=1, source_target_pairs={{0,4},{1,5},{2,6},{3,7},{4,0},{5,1},{6,2},{7,3},{8,12},{9,13},{10,... | collective-permute-start | bytes 811016 | tf_op jit(solution)/shard_map/ppermute | solution.py:252
  5.8 12.3 %collective-permute-done.1.first_ref = bf16[32,4224]{1,0:T(8,128)(2,1)S(1)} collective-permute-done((bf16[32,4224]{1,0:T(8,128)(2,1)S(1)}, bf16[32,4224]{1,0:T(8,128)(2,1)S(1)}, u32[]{:S(2)}, u32[]{:S(2)}) %collective-permute-start.1) | collective-permute-done | bytes 270368 | tf_op jit(solution)/shard_map/ppermute | solution.py:252
  18.1 0.0 collective-permute-start.2
  18.1 0.1 pad_add_fusion.here_ref
  18.2 0.0 collective-permute-done.second_ref
  18.2 1.2 %shard_map.123 = (bf16[16,4096]{1,0:T(8,128)(2,1)S(1)}, bf16[16,4096]{1,0:T(8,128)(2,1)S(1)}, bf16[16,4096]{1,0:T(8,128)(2,1)S(1)}, bf16[16,4096]{1,0:T(8,128)(2...) custom-call(s32[4]{0:T(128)S(1)} %pad_add_fusion.here_ref, ...), custom_call_target="tpu_custom_call" | custom-call | flops 1000000 | bytes 1000000 | tf_op jit(solution)/shard_map/pallas_call | solution.py:218
  19.4 1.6 %collective-permute-start.3 = (bf16[16,4096]{1,0:T(8,128)(2,1)S(1)}, bf16[16,4096]{1,0:T(8,128)(2,1)S(1)}, u32[]{:S(2)}, u32[]{:S(2)}) collective-permute-start(bf16[16,4096]{1,0:T(8,128)(2,1)S(1)} %get-tuple-element.44), channel_id=1, source_target_pairs={{0,1},{1,0},{2,3},{3,2},{4,5},{5,4},{6,7},{7,6},{8,9},{9,8},{10,11... | collective-permute-start | bytes 393224 | tf_op jit(solution)/shard_map/ppermute | solution.py:252
  21.0 0.7 collective-permute-start.4
  21.7 1.3 %collective-permute-start.5 = (bf16[16,4096]{1,0:T(8,128)(2,1)S(1)}, bf16[16,4096]{1,0:T(8,128)(2,1)S(1)}, u32[]{:S(2)}, u32[]{:S(2)}) collective-permute-start(bf16[16,4096]{1,0:T(8,128)(2,1)S(1)} %get-tuple-element.46), channel_id=1, source_target_pairs={{0,3},{1,2},{2,1},{3,0},{4,7},{5,6},{6,5},{7,4},{8,11},{9,10},{10,... | collective-permute-start | bytes 393224 | tf_op jit(solution)/shard_map/ppermute | solution.py:252
  23.0 1.6 %collective-permute-start.6 = (bf16[16,4096]{1,0:T(8,128)(2,1)S(1)}, bf16[16,4096]{1,0:T(8,128)(2,1)S(1)}, u32[]{:S(2)}, u32[]{:S(2)}) collective-permute-start(bf16[16,4096]{1,0:T(8,128)(2,1)S(1)} %get-tuple-element.47), channel_id=1, source_target_pairs={{0,16},{1,17},{2,18},{3,19},{4,20},{5,21},{6,22},{7,23},{8,24},{9,... | collective-permute-start | bytes 393224 | tf_op jit(solution)/shard_map/ppermute | solution.py:252
  24.6 0.0 collective-permute-done.2.second_ref
  24.6 1.4 %collective-permute-start.7 = (bf16[16,4096]{1,0:T(8,128)(2,1)S(1)}, bf16[16,4096]{1,0:T(8,128)(2,1)S(1)}, u32[]{:S(2)}, u32[]{:S(2)}) collective-permute-start(bf16[16,4096]{1,0:T(8,128)(2,1)S(1)} %get-tuple-element.48), channel_id=1, source_target_pairs={{0,17},{1,16},{2,19},{3,18},{4,21},{5,20},{6,23},{7,22},{8,25},{9,... | collective-permute-start | bytes 393224 | tf_op jit(solution)/shard_map/ppermute | solution.py:252
  26.0 1.2 %shard_map.124 = (bf16[16,4096]{1,0:T(8,128)(2,1)S(1)}, bf16[16,4096]{1,0:T(8,128)(2,1)S(1)}, bf16[16,4096]{1,0:T(8,128)(2,1)S(1)}, bf16[16,4096]{1,0:T(8,128)(2...) custom-call(s32[4]{0:T(128)S(1)} %pad_add_fusion.here_ref, ...), custom_call_target="tpu_custom_call" | custom-call | flops 1000000 | bytes 1000000 | tf_op jit(solution)/shard_map/pallas_call | solution.py:218
  27.2 0.0 collective-permute-done.3.refs_1_
  27.3 1.7 %collective-permute-start.8 = (bf16[16,4096]{1,0:T(8,128)(2,1)S(1)}, bf16[16,4096]{1,0:T(8,128)(2,1)S(1)}, u32[]{:S(2)}, u32[]{:S(2)}) collective-permute-start(bf16[16,4096]{1,0:T(8,128)(2,1)S(1)} %get-tuple-element.49), channel_id=1, source_target_pairs={{0,18},{1,19},{2,16},{3,17},{4,22},{5,23},{6,20},{7,21},{8,26},{9,... | collective-permute-start | bytes 393224 | tf_op jit(solution)/shard_map/ppermute | solution.py:252
  29.0 1.2 %collective-permute-start.9 = (bf16[16,4096]{1,0:T(8,128)(2,1)S(1)}, bf16[16,4096]{1,0:T(8,128)(2,1)S(1)}, u32[]{:S(2)}, u32[]{:S(2)}) collective-permute-start(bf16[16,4096]{1,0:T(8,128)(2,1)S(1)} %get-tuple-element.50), channel_id=1, source_target_pairs={{0,19},{1,18},{2,17},{3,16},{4,23},{5,22},{6,21},{7,20},{8,27},{9,... | collective-permute-start | bytes 393224 | tf_op jit(solution)/shard_map/ppermute | solution.py:252
  30.2 0.0 collective-permute-done.5.refs_3_
  30.2 1.6 %collective-permute-start.10 = (bf16[16,4096]{1,0:T(8,128)(2,1)S(1)}, bf16[16,4096]{1,0:T(8,128)(2,1)S(1)}, u32[]{:S(2)}, u32[]{:S(2)}) collective-permute-start(bf16[16,4096]{1,0:T(8,128)(2,1)S(1)} %get-tuple-element.52), channel_id=1, source_target_pairs={{0,1},{1,0},{2,3},{3,2},{4,5},{5,4},{6,7},{7,6},{8,9},{9,8},{10,11... | collective-permute-start | bytes 393224 | tf_op jit(solution)/shard_map/ppermute | solution.py:252
  31.7 0.7 collective-permute-start.11
  32.4 6.4 %collective-permute-done.7.refs_5_ = bf16[16,4096]{1,0:T(8,128)(2,1)S(1)} collective-permute-done((bf16[16,4096]{1,0:T(8,128)(2,1)S(1)}, bf16[16,4096]{1,0:T(8,128)(2,1)S(1)}, u32[]{:S(2)}, u32[]{:S(2)}) %collective-permute-start.7) | collective-permute-done | bytes 131104 | tf_op jit(solution)/shard_map/ppermute | solution.py:252
  38.8 0.9 collective-permute-start.12
  39.7 0.0 collective-permute-done.8.refs_6_
  39.7 0.3 collective-permute-start.13
  40.0 2.0 %collective-permute-start.14 = (bf16[16,4096]{1,0:T(8,128)(2,1)S(1)}, bf16[16,4096]{1,0:T(8,128)(2,1)S(1)}, u32[]{:S(2)}, u32[]{:S(2)}) collective-permute-start(bf16[16,4096]{1,0:T(8,128)(2,1)S(1)} %get-tuple-element.56), channel_id=1, source_target_pairs={{0,17},{1,16},{2,19},{3,18},{4,21},{5,20},{6,23},{7,22},{8,25},{9,... | collective-permute-start | bytes 393224 | tf_op jit(solution)/shard_map/ppermute | solution.py:252
  42.0 0.0 collective-permute-done.10.refs_9_
  42.0 1.4 %collective-permute-start.15 = (bf16[16,4096]{1,0:T(8,128)(2,1)S(1)}, bf16[16,4096]{1,0:T(8,128)(2,1)S(1)}, u32[]{:S(2)}, u32[]{:S(2)}) collective-permute-start(bf16[16,4096]{1,0:T(8,128)(2,1)S(1)} %get-tuple-element.57), channel_id=1, source_target_pairs={{0,18},{1,19},{2,16},{3,17},{4,22},{5,23},{6,20},{7,21},{8,26},{9,... | collective-permute-start | bytes 393224 | tf_op jit(solution)/shard_map/ppermute | solution.py:252
  43.4 0.0 collective-permute-done.11.refs_10_
  43.4 2.2 %collective-permute-start.16 = (bf16[16,4096]{1,0:T(8,128)(2,1)S(1)}, bf16[16,4096]{1,0:T(8,128)(2,1)S(1)}, u32[]{:S(2)}, u32[]{:S(2)}) collective-permute-start(bf16[16,4096]{1,0:T(8,128)(2,1)S(1)} %get-tuple-element.58), channel_id=1, source_target_pairs={{0,19},{1,18},{2,17},{3,16},{4,23},{5,22},{6,21},{7,20},{8,27},{9,... | collective-permute-start | bytes 393224 | tf_op jit(solution)/shard_map/ppermute | solution.py:252
  45.6 7.3 %shard_map.125 = (bf16[2,2048,512]{2,1,0:T(8,128)(2,1)S(1)}, bf16[2,2048,512]{2,1,0:T(8,128)(2,1)S(1)}, bf16[2,512,2048]{2,1,0:T(8,128)(2,1)S(1)}, bf16[2,64,204...) custom-call(bf16[2,2048,512]{2,1,0:T(8,128)(2,1)} %refs_0_.1, ...), custom_call_target="tpu_custom_call" | custom-call | tf_op jit(solution)/shard_map/pallas_call | solution.py:287
  52.9 0.0 collective-permute-done.12.refs_11_
  52.9 0.0 collective-permute-done.15.refs_14_
  52.9 6.6 %shard_map.126 = (bf16[32,2560]{1,0:T(8,128)(2,1)S(1)}, bf16[32,2560]{1,0:T(8,128)(2,1)S(1)}, bf16[32,2560]{1,0:T(8,128)(2,1)S(1)}, bf16[32,2560]{1,0:T(8,128)(2...) custom-call(bf16[16,4096]{1,0:T(8,128)(2,1)S(1)} %get-tuple-element., ...), custom_call_target="tpu_custom_call" | custom-call | flops 5536481280 | bytes 21626880 | tf_op jit(solution)/shard_map/pallas_call | solution.py:218
  59.5 0.9 collective-permute-start.17
  60.4 1.7 %collective-permute-start.18 = (bf16[32,2560]{1,0:T(8,128)(2,1)S(1)}, bf16[32,2560]{1,0:T(8,128)(2,1)S(1)}, u32[]{:S(2)}, u32[]{:S(2)}) collective-permute-start(bf16[32,2560]{1,0:T(8,128)(2,1)S(1)} %get-tuple-element.67), channel_id=1, source_target_pairs={{0,2},{1,3},{2,0},{3,1},{4,6},{5,7},{6,4},{7,5},{8,10},{9,11},{10,... | collective-permute-start | bytes 491528 | tf_op jit(solution)/shard_map/ppermute | solution.py:252
  62.2 0.9 %collective-permute-start.19 = (bf16[32,2560]{1,0:T(8,128)(2,1)S(1)}, bf16[32,2560]{1,0:T(8,128)(2,1)S(1)}, u32[]{:S(2)}, u32[]{:S(2)}) collective-permute-start(bf16[32,2560]{1,0:T(8,128)(2,1)S(1)} %get-tuple-element.68), channel_id=1, source_target_pairs={{0,3},{1,2},{2,1},{3,0},{4,7},{5,6},{6,5},{7,4},{8,11},{9,10},{10,... | collective-permute-start | bytes 491528 | tf_op jit(solution)/shard_map/ppermute | solution.py:252
  63.1 0.9 collective-permute-start.20
  64.0 1.4 %collective-permute-start.21 = (bf16[32,2560]{1,0:T(8,128)(2,1)S(1)}, bf16[32,2560]{1,0:T(8,128)(2,1)S(1)}, u32[]{:S(2)}, u32[]{:S(2)}) collective-permute-start(bf16[32,2560]{1,0:T(8,128)(2,1)S(1)} %get-tuple-element.70), channel_id=1, source_target_pairs={{0,17},{1,16},{2,19},{3,18},{4,21},{5,20},{6,23},{7,22},{8,25},{9,... | collective-permute-start | bytes 491528 | tf_op jit(solution)/shard_map/ppermute | solution.py:252
  65.4 2.7 %collective-permute-done.17.refs_1_ = bf16[32,2560]{1,0:T(8,128)(2,1)S(1)} collective-permute-done((bf16[32,2560]{1,0:T(8,128)(2,1)S(1)}, bf16[32,2560]{1,0:T(8,128)(2,1)S(1)}, u32[]{:S(2)}, u32[]{:S(2)}) %collective-permute-start.17) | collective-permute-done | bytes 163872 | tf_op jit(solution)/shard_map/ppermute | solution.py:252
  68.1 0.6 collective-permute-start.22
  68.7 2.8 %collective-permute-start.23 = (bf16[32,2560]{1,0:T(8,128)(2,1)S(1)}, bf16[32,2560]{1,0:T(8,128)(2,1)S(1)}, u32[]{:S(2)}, u32[]{:S(2)}) collective-permute-start(bf16[32,2560]{1,0:T(8,128)(2,1)S(1)} %get-tuple-element.72), channel_id=1, source_target_pairs={{0,19},{1,18},{2,17},{3,16},{4,23},{5,22},{6,21},{7,20},{8,27},{9,... | collective-permute-start | bytes 491528 | tf_op jit(solution)/shard_map/ppermute | solution.py:252
  71.5 6.7 %collective-permute-done.20.refs_4_ = bf16[32,2560]{1,0:T(8,128)(2,1)S(1)} collective-permute-done((bf16[32,2560]{1,0:T(8,128)(2,1)S(1)}, bf16[32,2560]{1,0:T(8,128)(2,1)S(1)}, u32[]{:S(2)}, u32[]{:S(2)}) %collective-permute-start.20) | collective-permute-done | bytes 163872 | tf_op jit(solution)/shard_map/ppermute | solution.py:252
  78.2 0.3 shard_map.127
  78.5 0.1 collective-permute-start.24
  78.6 1.5 %collective-permute-done.24.more_ref = bf16[64,2176]{1,0:T(8,128)(2,1)S(1)} collective-permute-done((bf16[64,2176]{1,0:T(8,128)(2,1)S(1)}, bf16[64,2176]{1,0:T(8,128)(2,1)S(1)}, u32[]{:S(2)}, u32[]{:S(2)}) %collective-permute-start.24) | collective-permute-done | bytes 278560 | tf_op jit(solution)/shard_map/ppermute | solution.py:252
  80.2 2.8 %collective-permute-start.25 = (bf16[32,2176]{1,0:T(8,128)(2,1)S(1)}, bf16[32,2176]{1,0:T(8,128)(2,1)S(1)}, u32[]{:S(2)}, u32[]{:S(2)}) collective-permute-start(bf16[32,2176]{1,0:T(8,128)(2,1)S(1)} %shard_map.128), channel_id=1, source_target_pairs={{0,4},{1,5},{2,6},{3,7},{4,0},{5,1},{6,2},{7,3},{8,12},{9,13},{10,... | collective-permute-start | bytes 417800 | tf_op jit(solution)/shard_map/ppermute | solution.py:252
  82.9 7.0 %collective-permute-done.25.far_ref = bf16[32,2176]{1,0:T(8,128)(2,1)S(1)} collective-permute-done((bf16[32,2176]{1,0:T(8,128)(2,1)S(1)}, bf16[32,2176]{1,0:T(8,128)(2,1)S(1)}, u32[]{:S(2)}, u32[]{:S(2)}) %collective-permute-start.25) | collective-permute-done | bytes 139296 | tf_op jit(solution)/shard_map/ppermute | solution.py:252
  89.9 0.7 shard_map.129
  (13 shorter events, 0.1 us)
Async XLA Ops:
  1.7 16.4 %collective-permute-start.1 = (bf16[32,4224]{1,0:T(8,128)(2,1)S(1)}, bf16[32,4224]{1,0:T(8,128)(2,1)S(1)}, u32[]{:S(2)}, u32[]{:S(2)}) collective-permute-start(bf16[32,4224]{1,0:T(8,128)(2,1)S(1)} %shard_map.122.first_ref), channel_id=1, source_target_pairs={{0,4},{1,5},{2,6},{3,7},{4,0},{5,1},{6,2},{7,3},{8,12},{9,13},{10,... | collective-permute-start | bytes 811016 | tf_op jit(solution)/shard_map/ppermute | solution.py:252
  5.8 12.4 %collective-permute-start = (bf16[32,4224]{1,0:T(8,128)(2,1)S(1)}, bf16[32,4224]{1,0:T(8,128)(2,1)S(1)}, u32[]{:S(2)}, u32[]{:S(2)}) collective-permute-start(bf16[32,4224]{1,0:T(8,128)(2,1)S(1)} %shard_map.122.first_ref), channel_id=1, source_target_pairs={{0,8},{1,9},{2,10},{3,11},{4,12},{5,13},{6,14},{7,15},{8,0},{9,1},... | collective-permute-start | bytes 811016 | tf_op jit(solution)/shard_map/ppermute | solution.py:252
  18.1 6.5 %collective-permute-start.2 = (bf16[32,4224]{1,0:T(8,128)(2,1)S(1)}, bf16[32,4224]{1,0:T(8,128)(2,1)S(1)}, u32[]{:S(2)}, u32[]{:S(2)}) collective-permute-start(bf16[32,4224]{1,0:T(8,128)(2,1)S(1)} %collective-permute-done.1.first_ref), channel_id=1, source_target_pairs={{0,8},{1,9},{2,10},{3,11},{4,12},{5,13},{6,14},{7,15},{8,0},{9,1},... | collective-permute-start | bytes 811016 | tf_op jit(solution)/shard_map/ppermute | solution.py:252
  19.4 7.8 %collective-permute-start.3 = (bf16[16,4096]{1,0:T(8,128)(2,1)S(1)}, bf16[16,4096]{1,0:T(8,128)(2,1)S(1)}, u32[]{:S(2)}, u32[]{:S(2)}) collective-permute-start(bf16[16,4096]{1,0:T(8,128)(2,1)S(1)} %get-tuple-element.44), channel_id=1, source_target_pairs={{0,1},{1,0},{2,3},{3,2},{4,5},{5,4},{6,7},{7,6},{8,9},{9,8},{10,11... | collective-permute-start | bytes 393224 | tf_op jit(solution)/shard_map/ppermute | solution.py:252
  21.0 7.9 %collective-permute-start.4 = (bf16[16,4096]{1,0:T(8,128)(2,1)S(1)}, bf16[16,4096]{1,0:T(8,128)(2,1)S(1)}, u32[]{:S(2)}, u32[]{:S(2)}) collective-permute-start(bf16[16,4096]{1,0:T(8,128)(2,1)S(1)} %get-tuple-element.45), channel_id=1, source_target_pairs={{0,2},{1,3},{2,0},{3,1},{4,6},{5,7},{6,4},{7,5},{8,10},{9,11},{10,... | collective-permute-start | bytes 393224 | tf_op jit(solution)/shard_map/ppermute | solution.py:252
  21.7 8.4 %collective-permute-start.5 = (bf16[16,4096]{1,0:T(8,128)(2,1)S(1)}, bf16[16,4096]{1,0:T(8,128)(2,1)S(1)}, u32[]{:S(2)}, u32[]{:S(2)}) collective-permute-start(bf16[16,4096]{1,0:T(8,128)(2,1)S(1)} %get-tuple-element.46), channel_id=1, source_target_pairs={{0,3},{1,2},{2,1},{3,0},{4,7},{5,6},{6,5},{7,4},{8,11},{9,10},{10,... | collective-permute-start | bytes 393224 | tf_op jit(solution)/shard_map/ppermute | solution.py:252
  23.0 8.7 %collective-permute-start.6 = (bf16[16,4096]{1,0:T(8,128)(2,1)S(1)}, bf16[16,4096]{1,0:T(8,128)(2,1)S(1)}, u32[]{:S(2)}, u32[]{:S(2)}) collective-permute-start(bf16[16,4096]{1,0:T(8,128)(2,1)S(1)} %get-tuple-element.47), channel_id=1, source_target_pairs={{0,16},{1,17},{2,18},{3,19},{4,20},{5,21},{6,22},{7,23},{8,24},{9,... | collective-permute-start | bytes 393224 | tf_op jit(solution)/shard_map/ppermute | solution.py:252
  24.6 14.2 %collective-permute-start.7 = (bf16[16,4096]{1,0:T(8,128)(2,1)S(1)}, bf16[16,4096]{1,0:T(8,128)(2,1)S(1)}, u32[]{:S(2)}, u32[]{:S(2)}) collective-permute-start(bf16[16,4096]{1,0:T(8,128)(2,1)S(1)} %get-tuple-element.48), channel_id=1, source_target_pairs={{0,17},{1,16},{2,19},{3,18},{4,21},{5,20},{6,23},{7,22},{8,25},{9,... | collective-permute-start | bytes 393224 | tf_op jit(solution)/shard_map/ppermute | solution.py:252
  27.3 12.5 %collective-permute-start.8 = (bf16[16,4096]{1,0:T(8,128)(2,1)S(1)}, bf16[16,4096]{1,0:T(8,128)(2,1)S(1)}, u32[]{:S(2)}, u32[]{:S(2)}) collective-permute-start(bf16[16,4096]{1,0:T(8,128)(2,1)S(1)} %get-tuple-element.49), channel_id=1, source_target_pairs={{0,18},{1,19},{2,16},{3,17},{4,22},{5,23},{6,20},{7,21},{8,26},{9,... | collective-permute-start | bytes 393224 | tf_op jit(solution)/shard_map/ppermute | solution.py:252
  29.0 11.1 %collective-permute-start.9 = (bf16[16,4096]{1,0:T(8,128)(2,1)S(1)}, bf16[16,4096]{1,0:T(8,128)(2,1)S(1)}, u32[]{:S(2)}, u32[]{:S(2)}) collective-permute-start(bf16[16,4096]{1,0:T(8,128)(2,1)S(1)} %get-tuple-element.50), channel_id=1, source_target_pairs={{0,19},{1,18},{2,17},{3,16},{4,23},{5,22},{6,21},{7,20},{8,27},{9,... | collective-permute-start | bytes 393224 | tf_op jit(solution)/shard_map/ppermute | solution.py:252
  30.2 11.9 %collective-permute-start.10 = (bf16[16,4096]{1,0:T(8,128)(2,1)S(1)}, bf16[16,4096]{1,0:T(8,128)(2,1)S(1)}, u32[]{:S(2)}, u32[]{:S(2)}) collective-permute-start(bf16[16,4096]{1,0:T(8,128)(2,1)S(1)} %get-tuple-element.52), channel_id=1, source_target_pairs={{0,1},{1,0},{2,3},{3,2},{4,5},{5,4},{6,7},{7,6},{8,9},{9,8},{10,11... | collective-permute-start | bytes 393224 | tf_op jit(solution)/shard_map/ppermute | solution.py:252
  31.7 11.7 %collective-permute-start.11 = (bf16[16,4096]{1,0:T(8,128)(2,1)S(1)}, bf16[16,4096]{1,0:T(8,128)(2,1)S(1)}, u32[]{:S(2)}, u32[]{:S(2)}) collective-permute-start(bf16[16,4096]{1,0:T(8,128)(2,1)S(1)} %get-tuple-element.53), channel_id=1, source_target_pairs={{0,2},{1,3},{2,0},{3,1},{4,6},{5,7},{6,4},{7,5},{8,10},{9,11},{10,... | collective-permute-start | bytes 393224 | tf_op jit(solution)/shard_map/ppermute | solution.py:252
  38.8 14.1 %collective-permute-start.12 = (bf16[16,4096]{1,0:T(8,128)(2,1)S(1)}, bf16[16,4096]{1,0:T(8,128)(2,1)S(1)}, u32[]{:S(2)}, u32[]{:S(2)}) collective-permute-start(bf16[16,4096]{1,0:T(8,128)(2,1)S(1)} %get-tuple-element.54), channel_id=1, source_target_pairs={{0,3},{1,2},{2,1},{3,0},{4,7},{5,6},{6,5},{7,4},{8,11},{9,10},{10,... | collective-permute-start | bytes 393224 | tf_op jit(solution)/shard_map/ppermute | solution.py:252
  39.7 13.2 %collective-permute-start.13 = (bf16[16,4096]{1,0:T(8,128)(2,1)S(1)}, bf16[16,4096]{1,0:T(8,128)(2,1)S(1)}, u32[]{:S(2)}, u32[]{:S(2)}) collective-permute-start(bf16[16,4096]{1,0:T(8,128)(2,1)S(1)} %get-tuple-element.55), channel_id=1, source_target_pairs={{0,16},{1,17},{2,18},{3,19},{4,20},{5,21},{6,22},{7,23},{8,24},{9,... | collective-permute-start | bytes 393224 | tf_op jit(solution)/shard_map/ppermute | solution.py:252
  40.0 12.9 %collective-permute-start.14 = (bf16[16,4096]{1,0:T(8,128)(2,1)S(1)}, bf16[16,4096]{1,0:T(8,128)(2,1)S(1)}, u32[]{:S(2)}, u32[]{:S(2)}) collective-permute-start(bf16[16,4096]{1,0:T(8,128)(2,1)S(1)} %get-tuple-element.56), channel_id=1, source_target_pairs={{0,17},{1,16},{2,19},{3,18},{4,21},{5,20},{6,23},{7,22},{8,25},{9,... | collective-permute-start | bytes 393224 | tf_op jit(solution)/shard_map/ppermute | solution.py:252
  42.0 10.9 %collective-permute-start.15 = (bf16[16,4096]{1,0:T(8,128)(2,1)S(1)}, bf16[16,4096]{1,0:T(8,128)(2,1)S(1)}, u32[]{:S(2)}, u32[]{:S(2)}) collective-permute-start(bf16[16,4096]{1,0:T(8,128)(2,1)S(1)} %get-tuple-element.57), channel_id=1, source_target_pairs={{0,18},{1,19},{2,16},{3,17},{4,22},{5,23},{6,20},{7,21},{8,26},{9,... | collective-permute-start | bytes 393224 | tf_op jit(solution)/shard_map/ppermute | solution.py:252
  43.4 9.5 %collective-permute-start.16 = (bf16[16,4096]{1,0:T(8,128)(2,1)S(1)}, bf16[16,4096]{1,0:T(8,128)(2,1)S(1)}, u32[]{:S(2)}, u32[]{:S(2)}) collective-permute-start(bf16[16,4096]{1,0:T(8,128)(2,1)S(1)} %get-tuple-element.58), channel_id=1, source_target_pairs={{0,19},{1,18},{2,17},{3,16},{4,23},{5,22},{6,21},{7,20},{8,27},{9,... | collective-permute-start | bytes 393224 | tf_op jit(solution)/shard_map/ppermute | solution.py:252
  59.5 8.6 %collective-permute-start.17 = (bf16[32,2560]{1,0:T(8,128)(2,1)S(1)}, bf16[32,2560]{1,0:T(8,128)(2,1)S(1)}, u32[]{:S(2)}, u32[]{:S(2)}) collective-permute-start(bf16[32,2560]{1,0:T(8,128)(2,1)S(1)} %get-tuple-element.66), channel_id=1, source_target_pairs={{0,1},{1,0},{2,3},{3,2},{4,5},{5,4},{6,7},{7,6},{8,9},{9,8},{10,11... | collective-permute-start | bytes 491528 | tf_op jit(solution)/shard_map/ppermute | solution.py:252
  60.4 8.3 %collective-permute-start.18 = (bf16[32,2560]{1,0:T(8,128)(2,1)S(1)}, bf16[32,2560]{1,0:T(8,128)(2,1)S(1)}, u32[]{:S(2)}, u32[]{:S(2)}) collective-permute-start(bf16[32,2560]{1,0:T(8,128)(2,1)S(1)} %get-tuple-element.67), channel_id=1, source_target_pairs={{0,2},{1,3},{2,0},{3,1},{4,6},{5,7},{6,4},{7,5},{8,10},{9,11},{10,... | collective-permute-start | bytes 491528 | tf_op jit(solution)/shard_map/ppermute | solution.py:252
  62.2 9.3 %collective-permute-start.19 = (bf16[32,2560]{1,0:T(8,128)(2,1)S(1)}, bf16[32,2560]{1,0:T(8,128)(2,1)S(1)}, u32[]{:S(2)}, u32[]{:S(2)}) collective-permute-start(bf16[32,2560]{1,0:T(8,128)(2,1)S(1)} %get-tuple-element.68), channel_id=1, source_target_pairs={{0,3},{1,2},{2,1},{3,0},{4,7},{5,6},{6,5},{7,4},{8,11},{9,10},{10,... | collective-permute-start | bytes 491528 | tf_op jit(solution)/shard_map/ppermute | solution.py:252
  63.1 15.1 %collective-permute-start.20 = (bf16[32,2560]{1,0:T(8,128)(2,1)S(1)}, bf16[32,2560]{1,0:T(8,128)(2,1)S(1)}, u32[]{:S(2)}, u32[]{:S(2)}) collective-permute-start(bf16[32,2560]{1,0:T(8,128)(2,1)S(1)} %get-tuple-element.69), channel_id=1, source_target_pairs={{0,16},{1,17},{2,18},{3,19},{4,20},{5,21},{6,22},{7,23},{8,24},{9,... | collective-permute-start | bytes 491528 | tf_op jit(solution)/shard_map/ppermute | solution.py:252
  64.0 14.2 %collective-permute-start.21 = (bf16[32,2560]{1,0:T(8,128)(2,1)S(1)}, bf16[32,2560]{1,0:T(8,128)(2,1)S(1)}, u32[]{:S(2)}, u32[]{:S(2)}) collective-permute-start(bf16[32,2560]{1,0:T(8,128)(2,1)S(1)} %get-tuple-element.70), channel_id=1, source_target_pairs={{0,17},{1,16},{2,19},{3,18},{4,21},{5,20},{6,23},{7,22},{8,25},{9,... | collective-permute-start | bytes 491528 | tf_op jit(solution)/shard_map/ppermute | solution.py:252
  68.1 10.1 %collective-permute-start.22 = (bf16[32,2560]{1,0:T(8,128)(2,1)S(1)}, bf16[32,2560]{1,0:T(8,128)(2,1)S(1)}, u32[]{:S(2)}, u32[]{:S(2)}) collective-permute-start(bf16[32,2560]{1,0:T(8,128)(2,1)S(1)} %get-tuple-element.71), channel_id=1, source_target_pairs={{0,18},{1,19},{2,16},{3,17},{4,22},{5,23},{6,20},{7,21},{8,26},{9,... | collective-permute-start | bytes 491528 | tf_op jit(solution)/shard_map/ppermute | solution.py:252
  68.7 9.5 %collective-permute-start.23 = (bf16[32,2560]{1,0:T(8,128)(2,1)S(1)}, bf16[32,2560]{1,0:T(8,128)(2,1)S(1)}, u32[]{:S(2)}, u32[]{:S(2)}) collective-permute-start(bf16[32,2560]{1,0:T(8,128)(2,1)S(1)} %get-tuple-element.72), channel_id=1, source_target_pairs={{0,19},{1,18},{2,17},{3,16},{4,23},{5,22},{6,21},{7,20},{8,27},{9,... | collective-permute-start | bytes 491528 | tf_op jit(solution)/shard_map/ppermute | solution.py:252
  78.5 1.6 %collective-permute-start.24 = (bf16[64,2176]{1,0:T(8,128)(2,1)S(1)}, bf16[64,2176]{1,0:T(8,128)(2,1)S(1)}, u32[]{:S(2)}, u32[]{:S(2)}) collective-permute-start(bf16[64,2176]{1,0:T(8,128)(2,1)S(1)} %get-tuple-element.74), channel_id=1, source_target_pairs={{0,8},{1,9},{2,10},{3,11},{4,12},{5,13},{6,14},{7,15},{8,0},{9,1},... | collective-permute-start | bytes 835592 | tf_op jit(solution)/shard_map/ppermute | solution.py:252
  80.2 9.7 %collective-permute-start.25 = (bf16[32,2176]{1,0:T(8,128)(2,1)S(1)}, bf16[32,2176]{1,0:T(8,128)(2,1)S(1)}, u32[]{:S(2)}, u32[]{:S(2)}) collective-permute-start(bf16[32,2176]{1,0:T(8,128)(2,1)S(1)} %shard_map.128), channel_id=1, source_target_pairs={{0,4},{1,5},{2,6},{3,7},{4,0},{5,1},{6,2},{7,3},{8,12},{9,13},{10,... | collective-permute-start | bytes 417800 | tf_op jit(solution)/shard_map/ppermute | solution.py:252

commit v7 on v6

--- a/solution.py
+++ b/solution.py
@@ -52,7 +52,7 @@
     pay_ref[:, width : 2 * width] = g_ref[...]
 
 
-def pack_kernel(top, experts, capacity, deep, here_ref, first_ref, second_ref, *outs):
+def pack_kernel(top, experts, capacity, deep, first_ref, second_ref, *outs):
     place_ref, tally_ref, sends = outs[-2], outs[-1], outs[:-2]
     tok = first_ref.shape[0]
     width = sends[0].shape[1] // 2
@@ -63,8 +63,9 @@
     slot = lax.broadcasted_iota(jnp.int32, shape, 1)
     block = lax.broadcasted_iota(jnp.int32, shape, 0) // tok
     chip = slot // piece
-    to_row, to_deep = here_ref[0] ^ (chip // deep), here_ref[3] ^ (chip % deep)
-    device = ((to_row * PAIR + here_ref[1]) * PAIR + here_ref[2]) * deep + to_deep
+    here = [lax.axis_index(a) for a in AXES]
+    to_row, to_deep = here[0] ^ (chip // deep), here[3] ^ (chip % deep)
+    device = ((to_row * PAIR + here[1]) * PAIR + here[2]) * deep + to_deep
     expert = (device * experts + slot // (PAIR * capacity) % experts).astype(F32)
     meant = jnp.where(slot // capacity % PAIR == block, 1.0, 0.0)
     named = jnp.zeros(shape, F32)
@@ -103,14 +104,15 @@
         copy.wait()
 
 
-def expert_kernel(count, group, *refs):
-    ins, weights, outs = refs[:count], refs[count : count + 6], refs[count + 6 : -1]
+def expert_kernel(count, group, deep, *refs):
+    ins, weights = refs[:count], refs[count : count + 6]
+    own_ref, outs, stage_ref = refs[count + 6], refs[count + 7 : -2], refs[-2]
+    me = lax.axis_index("row") * deep + lax.axis_index("deep")
     gate, up, down, left_proj, right_proj, stored = weights
     outer_ref = refs[-1]
     experts, width, _ = gate.shape
     rank = left_proj.shape[1]
     half = count // 2
-    ins = [ins[i // 2 + i % 2 * half] for i in range(count)]
     per = LANES // rank
     rows = count * group
     lane = lax.broadcasted_iota(jnp.int32, (rows, LANES), 1) // rank
@@ -141,9 +143,11 @@
 
     def put(j, value, columns):
         value = value.astype(BF16)
-        for i in range(count):
-            to = slice((i % 2 * experts + j) * group, (i % 2 * experts + j + 1) * group)
-            outs[i // 2][to, columns] = value[i * group : (i + 1) * group]
+        part = slice(j * group, (j + 1) * group)
+        for i in range(half):
+            stage_ref[i, part, columns] = value[i * group : (i + 1) * group]
+        for i in range(half):
+            outs[i][part, columns] = value[(half + i) * group : (half + i + 1) * group]
 
     def grads(j, grad_gate, grad_up):
         put(j, dot_nt(grad_gate, gate[j]) + dot_nt(grad_up, up[j]), slice(0, width))
@@ -159,46 +163,44 @@
         outers(j, *second[j][2:])
         grads(j, *second[j][:2])
         scores(j)
-
-
-def part_kernel(own_ref, own_tally_ref, guest_ref, guest_tally_ref, *refs):
-    ins, own_keep_ref, guest_keep_ref, give_ref = refs[:-3], refs[-3], refs[-2], refs[-1]
-    tok, span = own_keep_ref.shape
+    for i in range(half):
+        own_ref[i ^ me] = stage_ref[i]
+
+
+def token_sums(place_ref, tally_ref, ins, keep_ref, give_ref):
+    tok, span = keep_ref.shape
     width = span - LANES
-    piece = ins[0].shape[0] // 2
-
-    def token_sums(place_ref, tally_ref, part):
-        grads = jnp.concatenate([r[part, :width] for r in ins], axis=0)
-        scores = jnp.concatenate([r[part, width:] for r in ins], axis=0)
-        total, tally = dot(place_ref[...], grads), dot(tally_ref[...], scores)
-
-        def fold(block):
-            rows = tally[block * QRY_DEV : (block + 1) * QRY_DEV]
-            return jnp.concatenate(
-                [rows[:, i : i + LANES] for i in range(0, rows.shape[1], LANES)], axis=0
-            )
-
-        return total, fold
-
-    own, own_fold = token_sums(own_ref, own_tally_ref, slice(0, piece))
-    guest, guest_fold = token_sums(guest_ref, guest_tally_ref, slice(piece, 2 * piece))
-    own_keep_ref[:, :width] = own[:tok]
-    own_keep_ref[:, width:] = own_fold(0)
-    guest_keep_ref[:, :width] = guest[:tok]
-    guest_keep_ref[:, width:] = guest_fold(0)
-    give_ref[:tok, :width] = guest[tok:].astype(BF16)
-    give_ref[:tok, width:] = guest_fold(1).astype(BF16)
-    give_ref[tok:, :width] = own[tok:].astype(BF16)
-    give_ref[tok:, width:] = own_fold(1).astype(BF16)
+    rows = jnp.concatenate(ins, axis=0)
+    total, tally = dot(place_ref[...], rows[:, :width]), dot(tally_ref[...], rows[:, width:])
+
+    def fold(block):
+        part = tally[block * QRY_DEV : (block + 1) * QRY_DEV]
+        pieces = [part[:, i : i + LANES] for i in range(0, part.shape[1], LANES)]
+        return jnp.concatenate(pieces, axis=0)
+
+    keep_ref[:, :width] = total[:tok]
+    keep_ref[:, width:] = fold(0)
+    give_ref[:, :width] = total[tok:].astype(BF16)
+    give_ref[:, width:] = fold(1).astype(BF16)
+
+
+def guest_part_kernel(place_ref, tally_ref, *refs):
+    token_sums(place_ref, tally_ref, [r[...] for r in refs[:-2]], *refs[-2:])
+
+
+def own_part_kernel(deep, place_ref, tally_ref, rows_ref, keep_ref, give_ref):
+    me = lax.axis_index("row") * deep + lax.axis_index("deep")
+    ins = [rows_ref[i ^ me] for i in range(rows_ref.shape[0])]
+    token_sums(place_ref, tally_ref, ins, keep_ref, give_ref)
 
 
 def join_kernel(keep_ref, more_ref, out_ref):
-    out_ref[...] = (keep_ref[...] + more_ref[: keep_ref.shape[0]].astype(F32)).astype(BF16)
+    out_ref[...] = (keep_ref[...] + more_ref[...].astype(F32)).astype(BF16)
 
 
 def final_kernel(keep_ref, more_ref, far_ref, grad_ref, score_ref):
     tok, width = grad_ref.shape
-    total = keep_ref[...] + more_ref[tok:].astype(F32) + far_ref[...].astype(F32)
+    total = keep_ref[...] + more_ref[...].astype(F32) + far_ref[...].astype(F32)
     grad_ref[...] = total[:, :width].astype(BF16)
     for i in range(tok // QRY_DEV):
         part = total[i * QRY_DEV : (i + 1) * QRY_DEV, width:]
@@ -206,7 +208,6 @@
 
 
 VMEM = pl.BlockSpec(memory_space=pltpu.VMEM)
-SMEM = pl.BlockSpec(memory_space=pltpu.SMEM)
 HBM = pl.BlockSpec(memory_space=pltpu.HBM)
 
 
@@ -237,7 +238,6 @@
     chips = row_size * deep
     capacity = 2 * tok // (experts * PAIR * deep)
     piece = experts * PAIR * capacity
-    here = jnp.stack([lax.axis_index(a) for a in AXES]).astype(jnp.int32)
     shape = jax.ShapeDtypeStruct
 
     def swap(value, row=0, core=0, half=0, far=0):
@@ -265,7 +265,7 @@
         outs += (shape((PAIR * tok, piece * chips), BF16),)
         outs += (shape((PAIR * QRY_DEV, piece * chips), BF16),)
         kernel = functools.partial(pack_kernel, top, experts, capacity, deep)
-        filled = call(kernel, outs, [SMEM, VMEM, VMEM], (here, first, second), limit=12 << 20)
+        filled = call(kernel, outs, [VMEM, VMEM], (first, second), limit=12 << 20)
         return filled[:-2], filled[-2:]
 
     inputs = tuple(in_hbm(v) for v in (expert_ids.T, gate_w.T, query_ids, tokens, out_grad))
@@ -295,26 +295,36 @@
     rows = 2 * chips * piece
     size = sum(w.size for w in weights)
     outs = call(
-        functools.partial(expert_kernel, 2 * chips, PAIR * capacity),
-        (shape((2 * piece, width + train), BF16),) * chips,
+        functools.partial(expert_kernel, 2 * chips, PAIR * capacity, deep),
+        (shape((chips, piece, width + train), BF16),)
+        + (shape((piece, width + train), BF16),) * chips,
         [VMEM] * (2 * chips + len(weights)),
         (*own_rows, *guest_rows, *held),
-        scratch=[pltpu.VMEM((experts, rows // experts, weights[5].shape[1]), BF16)],
+        scratch=[
+            pltpu.VMEM((chips, piece, width + train), BF16),
+            pltpu.VMEM((experts, rows // experts, weights[5].shape[1]), BF16),
+        ],
         flops=2 * rows * size,
         moved=2 * size,
         limit=rows * (76 << 10),
     )
     assert QRY_DEV * train == tok * LANES
-    keep = shape((tok, width + LANES), F32)
-    own_keep, guest_keep, give = call(
-        part_kernel,
-        (keep, keep, shape((PAIR * tok, width + LANES), BF16)),
-        [VMEM] * (4 + chips),
-        (*own_place, *guest_place, *exchange(outs)),
-    )
-    more = swap(give, core=1)
-    far = call(join_kernel, shape((tok, width + LANES), BF16), [VMEM] * 2, (guest_keep, more))
+    guest_back = exchange(outs[1:])
+    own_back = lax.all_to_all(outs[0], ("row", "deep"), 0, 0, tiled=True)
+    sums = (shape((tok, width + LANES), F32), shape((tok, width + LANES), BF16))
+    guest_keep, guest_give = call(
+        guest_part_kernel, sums, [VMEM] * (2 + chips), (*guest_place, *guest_back)
+    )
+    more = swap(guest_give, core=1)
+    far = call(join_kernel, sums[1], [VMEM] * 2, (guest_keep, more))
     far = swap(far, half=1)
+    own_keep, own_give = call(
+        functools.partial(own_part_kernel, deep),
+        sums,
+        [VMEM] * 3,
+        (*own_place, own_back),
+    )
+    more = swap(own_give, core=1)
     return call(
         final_kernel,
         (shape((tok, width), BF16), shape((QRY_DEV, train), F32)),

time: 90.8 us -> 95.6 us (1.053)
  starting transfers between devices: 34.7 us -> 40.3 us
    all_to_all x0 -> x1, starting transfers between devices: none -> 5.06 us  [layer(): own_back = lax.all_to_all(outs[0], ('row', 'deep'), 0, 0, tiled=True)]
    ppermute x26 -> x27, waiting for transfers between devices: 36.6 us -> 35.9 us  [swap(): return lax.ppermute(value, AXES, pairs)]
    ppermute x26 -> x27, starting transfers between devices: 34.7 us -> 35.2 us  [swap(): return lax.ppermute(value, AXES, pairs)]
    pallas_call x7 -> x8, Pallas kernels: 11.2 us -> 11.1 us  [call(): pl.pallas_call(kernel, out_shape=outs, in_specs=in_specs, out_specs=jax.t...]
  transfers between devices with their start and end apart: 26 -> 28, of which waited for: 6 -> 9; matrix products, arithmetic and copies ran while one was open for 0% -> 0% of each run, Pallas kernels for 11% -> 10%
where the time goes in v7:
time: 95.6 us; the launch traced here: 95.4 us
  starting transfers between devices  40.3 us (42%)
  waiting for transfers between devices  35.9 us (38%)
  Pallas kernels  18.4 us (19%)
    ppermute x27, waiting for transfers between devices, swap(): return lax.ppermute(value, AXES, pairs)  35.9 us
    ppermute x27, starting transfers between devices, swap(): return lax.ppermute(value, AXES, pairs)  35.2 us
    pallas_call x8, Pallas kernels, call(): pl.pallas_call(kernel, out_shape=outs, in_specs=in_specs, out_specs=jax.t...  11.1 us
    pallas_call x1, Pallas kernels, layer(): pl.pallas_call(load_kernel, out_shape=tuple((pltpu.VMEM(w.shape, w.dtype)...  7.29 us
    all_to_all x1, starting transfers between devices, layer(): own_back = lax.all_to_all(outs[0], ('row', 'deep'), 0, 0, tiled=True)  5.06 us
  transfers between devices with their start and end apart: 28, of which 9 were waited for; matrix products, arithmetic and copies ran while one was open for 0% of the time, Pallas kernels for 10%

profile of v7, /device:TPU:0, one launch (start us, length us, event | category | flops | bytes accessed | tf_op | source)
XLA Modules:
  0.0 95.4 jit_solution(15917050214210835984)
XLA Ops:
  0.6 1.1 %shard_map.122.first_ref = bf16[32,4224]{1,0:T(8,128)(2,1)S(1)} custom-call(s32[4,32]{1,0:T(4,128)} %bitcast.6, bf16[4,32]{1,0:T(4,128)(2,1)} %bitcast.7, s32[1,32]{1,0:T(1,128)} %query_hbm.1, bf16[32,2048]{1,0:T(8,128)(2,1)} %x_hbm.1, bf16[32,2048]{1,0:T(8,128)(2,1)} %g_hbm.1), custom_call_target="tpu_custom_call" | custom-call | flops 1000000 | bytes 1000000 | tf_op jit(solution)/shard_map/pallas_call | solution.py:219
  1.7 4.1 %collective-permute-start.8 = (bf16[32,4224]{1,0:T(8,128)(2,1)S(1)}, bf16[32,4224]{1,0:T(8,128)(2,1)S(1)}, u32[]{:S(2)}, u32[]{:S(2)}) collective-permute-start(bf16[32,4224]{1,0:T(8,128)(2,1)S(1)} %shard_map.122.first_ref), channel_id=1, source_target_pairs={{0,4},{1,5},{2,6},{3,7},{4,0},{5,1},{6,2},{7,3},{8,12},{9,13},{10,... | collective-permute-start | bytes 811016 | tf_op jit(solution)/shard_map/ppermute | solution.py:252
  5.8 12.3 %collective-permute-done.8.first_ref = bf16[32,4224]{1,0:T(8,128)(2,1)S(1)} collective-permute-done((bf16[32,4224]{1,0:T(8,128)(2,1)S(1)}, bf16[32,4224]{1,0:T(8,128)(2,1)S(1)}, u32[]{:S(2)}, u32[]{:S(2)}) %collective-permute-start.8) | collective-permute-done | bytes 270368 | tf_op jit(solution)/shard_map/ppermute | solution.py:252
  18.1 0.0 collective-permute-start.9
  18.1 0.0 collective-permute-done.second_ref
  18.1 0.7 shard_map.123
  18.8 1.6 %collective-permute-start.1 = (bf16[16,4096]{1,0:T(8,128)(2,1)S(1)}, bf16[16,4096]{1,0:T(8,128)(2,1)S(1)}, u32[]{:S(2)}, u32[]{:S(2)}) collective-permute-start(bf16[16,4096]{1,0:T(8,128)(2,1)S(1)} %get-tuple-element.44), channel_id=1, source_target_pairs={{0,1},{1,0},{2,3},{3,2},{4,5},{5,4},{6,7},{7,6},{8,9},{9,8},{10,11... | collective-permute-start | bytes 393224 | tf_op jit(solution)/shard_map/ppermute | solution.py:252
  20.4 0.7 collective-permute-start.2
  21.1 1.3 %collective-permute-start.3 = (bf16[16,4096]{1,0:T(8,128)(2,1)S(1)}, bf16[16,4096]{1,0:T(8,128)(2,1)S(1)}, u32[]{:S(2)}, u32[]{:S(2)}) collective-permute-start(bf16[16,4096]{1,0:T(8,128)(2,1)S(1)} %get-tuple-element.46), channel_id=1, source_target_pairs={{0,3},{1,2},{2,1},{3,0},{4,7},{5,6},{6,5},{7,4},{8,11},{9,10},{10,... | collective-permute-start | bytes 393224 | tf_op jit(solution)/shard_map/ppermute | solution.py:252
  22.4 1.6 %collective-permute-start.4 = (bf16[16,4096]{1,0:T(8,128)(2,1)S(1)}, bf16[16,4096]{1,0:T(8,128)(2,1)S(1)}, u32[]{:S(2)}, u32[]{:S(2)}) collective-permute-start(bf16[16,4096]{1,0:T(8,128)(2,1)S(1)} %get-tuple-element.47), channel_id=1, source_target_pairs={{0,16},{1,17},{2,18},{3,19},{4,20},{5,21},{6,22},{7,23},{8,24},{9,... | collective-permute-start | bytes 393224 | tf_op jit(solution)/shard_map/ppermute | solution.py:252
  23.9 0.0 collective-permute-done.9.second_ref
  23.9 1.4 %collective-permute-start.5 = (bf16[16,4096]{1,0:T(8,128)(2,1)S(1)}, bf16[16,4096]{1,0:T(8,128)(2,1)S(1)}, u32[]{:S(2)}, u32[]{:S(2)}) collective-permute-start(bf16[16,4096]{1,0:T(8,128)(2,1)S(1)} %get-tuple-element.48), channel_id=1, source_target_pairs={{0,17},{1,16},{2,19},{3,18},{4,21},{5,20},{6,23},{7,22},{8,25},{9,... | collective-permute-start | bytes 393224 | tf_op jit(solution)/shard_map/ppermute | solution.py:252
  25.4 0.7 shard_map.124
  26.1 1.7 %collective-permute-start.6 = (bf16[16,4096]{1,0:T(8,128)(2,1)S(1)}, bf16[16,4096]{1,0:T(8,128)(2,1)S(1)}, u32[]{:S(2)}, u32[]{:S(2)}) collective-permute-start(bf16[16,4096]{1,0:T(8,128)(2,1)S(1)} %get-tuple-element.49), channel_id=1, source_target_pairs={{0,18},{1,19},{2,16},{3,17},{4,22},{5,23},{6,20},{7,21},{8,26},{9,... | collective-permute-start | bytes 393224 | tf_op jit(solution)/shard_map/ppermute | solution.py:252
  27.8 0.0 collective-permute-done.2.refs_2_
  27.8 1.2 %collective-permute-start.7 = (bf16[16,4096]{1,0:T(8,128)(2,1)S(1)}, bf16[16,4096]{1,0:T(8,128)(2,1)S(1)}, u32[]{:S(2)}, u32[]{:S(2)}) collective-permute-start(bf16[16,4096]{1,0:T(8,128)(2,1)S(1)} %get-tuple-element.50), channel_id=1, source_target_pairs={{0,19},{1,18},{2,17},{3,16},{4,23},{5,22},{6,21},{7,20},{8,27},{9,... | collective-permute-start | bytes 393224 | tf_op jit(solution)/shard_map/ppermute | solution.py:252
  29.0 0.0 collective-permute-done.3.refs_3_
  29.0 1.5 %collective-permute-start.10 = (bf16[16,4096]{1,0:T(8,128)(2,1)S(1)}, bf16[16,4096]{1,0:T(8,128)(2,1)S(1)}, u32[]{:S(2)}, u32[]{:S(2)}) collective-permute-start(bf16[16,4096]{1,0:T(8,128)(2,1)S(1)} %get-tuple-element.52), channel_id=1, source_target_pairs={{0,1},{1,0},{2,3},{3,2},{4,5},{5,4},{6,7},{7,6},{8,9},{9,8},{10,11... | collective-permute-start | bytes 393224 | tf_op jit(solution)/shard_map/ppermute | solution.py:252
  30.6 0.0 collective-permute-done.4.refs_4_
  30.6 0.7 collective-permute-start.11
  31.2 6.0 %collective-permute-done.5.refs_5_ = bf16[16,4096]{1,0:T(8,128)(2,1)S(1)} collective-permute-done((bf16[16,4096]{1,0:T(8,128)(2,1)S(1)}, bf16[16,4096]{1,0:T(8,128)(2,1)S(1)}, u32[]{:S(2)}, u32[]{:S(2)}) %collective-permute-start.5) | collective-permute-done | bytes 131104 | tf_op jit(solution)/shard_map/ppermute | solution.py:252
  37.3 1.2 %collective-permute-start.12 = (bf16[16,4096]{1,0:T(8,128)(2,1)S(1)}, bf16[16,4096]{1,0:T(8,128)(2,1)S(1)}, u32[]{:S(2)}, u32[]{:S(2)}) collective-permute-start(bf16[16,4096]{1,0:T(8,128)(2,1)S(1)} %get-tuple-element.54), channel_id=1, source_target_pairs={{0,3},{1,2},{2,1},{3,0},{4,7},{5,6},{6,5},{7,4},{8,11},{9,10},{10,... | collective-permute-start | bytes 393224 | tf_op jit(solution)/shard_map/ppermute | solution.py:252
  38.4 1.5 %collective-permute-start.13 = (bf16[16,4096]{1,0:T(8,128)(2,1)S(1)}, bf16[16,4096]{1,0:T(8,128)(2,1)S(1)}, u32[]{:S(2)}, u32[]{:S(2)}) collective-permute-start(bf16[16,4096]{1,0:T(8,128)(2,1)S(1)} %get-tuple-element.55), channel_id=1, source_target_pairs={{0,16},{1,17},{2,18},{3,19},{4,20},{5,21},{6,22},{7,23},{8,24},{9,... | collective-permute-start | bytes 393224 | tf_op jit(solution)/shard_map/ppermute | solution.py:252
  40.0 1.3 %collective-permute-start.14 = (bf16[16,4096]{1,0:T(8,128)(2,1)S(1)}, bf16[16,4096]{1,0:T(8,128)(2,1)S(1)}, u32[]{:S(2)}, u32[]{:S(2)}) collective-permute-start(bf16[16,4096]{1,0:T(8,128)(2,1)S(1)} %get-tuple-element.56), channel_id=1, source_target_pairs={{0,17},{1,16},{2,19},{3,18},{4,21},{5,20},{6,23},{7,22},{8,25},{9,... | collective-permute-start | bytes 393224 | tf_op jit(solution)/shard_map/ppermute | solution.py:252
  41.2 0.2 collective-permute-done.10.refs_9_
  41.4 2.9 %collective-permute-start.15 = (bf16[16,4096]{1,0:T(8,128)(2,1)S(1)}, bf16[16,4096]{1,0:T(8,128)(2,1)S(1)}, u32[]{:S(2)}, u32[]{:S(2)}) collective-permute-start(bf16[16,4096]{1,0:T(8,128)(2,1)S(1)} %get-tuple-element.57), channel_id=1, source_target_pairs={{0,18},{1,19},{2,16},{3,17},{4,22},{5,23},{6,20},{7,21},{8,26},{9,... | collective-permute-start | bytes 393224 | tf_op jit(solution)/shard_map/ppermute | solution.py:252
  44.4 7.3 %shard_map.125 = (bf16[2,2048,512]{2,1,0:T(8,128)(2,1)S(1)}, bf16[2,2048,512]{2,1,0:T(8,128)(2,1)S(1)}, bf16[2,512,2048]{2,1,0:T(8,128)(2,1)S(1)}, bf16[2,64,204...) custom-call(bf16[2,2048,512]{2,1,0:T(8,128)(2,1)} %refs_0_.1, ...), custom_call_target="tpu_custom_call" | custom-call | tf_op jit(solution)/shard_map/pallas_call | solution.py:287
  51.7 0.1 collective-permute-done.13.refs_12_
  51.8 7.5 %shard_map.126 = (bf16[8,16,2560]{2,1,0:T(8,128)(2,1)}, bf16[16,2560]{1,0:T(8,128)(2,1)S(1)}, bf16[16,2560]{1,0:T(8,128)(2,1)S(1)}, bf16[16,2560]{1,0:T(8,128)(2...) custom-call(bf16[16,4096]{1,0:T(8,128)(2,1)S(1)} %get-tuple-element., ...), custom_call_target="tpu_custom_call" | custom-call | flops 5536481280 | bytes 21626880 | tf_op jit(solution)/shard_map/pallas_call | solution.py:219
  59.2 5.1 %all-to-all-start = ((bf16[8,16,2560]{2,1,0:T(8,128)(2,1)}), bf16[8,16,2560]{2,1,0:T(8,128)(2,1)S(1)}, u32[]{:S(2)}, u32[]{:S(2)}) async-start(bf16[8,16,2560]{2,1,0:T(8,128)(2,1)} %get-tuple-element.65), calls=%async_computation | async-start | bytes 1310720 | tf_op jit(solution)/shard_map/all_to_all | solution.py:313
  64.3 2.0 %collective-permute-start.18 = (bf16[16,2560]{1,0:T(8,128)(2,1)S(1)}, bf16[16,2560]{1,0:T(8,128)(2,1)S(1)}, u32[]{:S(2)}, u32[]{:S(2)}) collective-permute-start(bf16[16,2560]{1,0:T(8,128)(2,1)S(1)} %get-tuple-element.71), channel_id=1, source_target_pairs={{0,1},{1,0},{2,3},{3,2},{4,5},{5,4},{6,7},{7,6},{8,9},{9,8},{10,11... | collective-permute-start | bytes 245768 | tf_op jit(solution)/shard_map/ppermute | solution.py:252
  66.3 1.5 %collective-permute-start.19 = (bf16[16,2560]{1,0:T(8,128)(2,1)S(1)}, bf16[16,2560]{1,0:T(8,128)(2,1)S(1)}, u32[]{:S(2)}, u32[]{:S(2)}) collective-permute-start(bf16[16,2560]{1,0:T(8,128)(2,1)S(1)} %get-tuple-element.72), channel_id=1, source_target_pairs={{0,2},{1,3},{2,0},{3,1},{4,6},{5,7},{6,4},{7,5},{8,10},{9,11},{10,... | collective-permute-start | bytes 245768 | tf_op jit(solution)/shard_map/ppermute | solution.py:252
  67.8 0.0 collective-permute-start.20
  67.8 2.0 %collective-permute-start.21 = (bf16[16,2560]{1,0:T(8,128)(2,1)S(1)}, bf16[16,2560]{1,0:T(8,128)(2,1)S(1)}, u32[]{:S(2)}, u32[]{:S(2)}) collective-permute-start(bf16[16,2560]{1,0:T(8,128)(2,1)S(1)} %get-tuple-element.74), channel_id=1, source_target_pairs={{0,16},{1,17},{2,18},{3,19},{4,20},{5,21},{6,22},{7,23},{8,24},{9,... | collective-permute-start | bytes 245768 | tf_op jit(solution)/shard_map/ppermute | solution.py:252
  69.8 1.5 %collective-permute-start.22 = (bf16[16,2560]{1,0:T(8,128)(2,1)S(1)}, bf16[16,2560]{1,0:T(8,128)(2,1)S(1)}, u32[]{:S(2)}, u32[]{:S(2)}) collective-permute-start(bf16[16,2560]{1,0:T(8,128)(2,1)S(1)} %get-tuple-element.75), channel_id=1, source_target_pairs={{0,17},{1,16},{2,19},{3,18},{4,21},{5,20},{6,23},{7,22},{8,25},{9,... | collective-permute-start | bytes 245768 | tf_op jit(solution)/shard_map/ppermute | solution.py:252
  71.3 3.4 %collective-permute-done.18.refs_1_ = bf16[16,2560]{1,0:T(8,128)(2,1)S(1)} collective-permute-done((bf16[16,2560]{1,0:T(8,128)(2,1)S(1)}, bf16[16,2560]{1,0:T(8,128)(2,1)S(1)}, u32[]{:S(2)}, u32[]{:S(2)}) %collective-permute-start.18) | collective-permute-done | bytes 81952 | tf_op jit(solution)/shard_map/ppermute | solution.py:252
  74.7 2.6 %collective-permute-start.23 = (bf16[16,2560]{1,0:T(8,128)(2,1)S(1)}, bf16[16,2560]{1,0:T(8,128)(2,1)S(1)}, u32[]{:S(2)}, u32[]{:S(2)}) collective-permute-start(bf16[16,2560]{1,0:T(8,128)(2,1)S(1)} %get-tuple-element.76), channel_id=1, source_target_pairs={{0,18},{1,19},{2,16},{3,17},{4,22},{5,23},{6,20},{7,21},{8,26},{9,... | collective-permute-start | bytes 245768 | tf_op jit(solution)/shard_map/ppermute | solution.py:252
  77.2 0.1 collective-permute-start.24
  77.4 2.6 %collective-permute-done.23.refs_6_ = bf16[16,2560]{1,0:T(8,128)(2,1)S(1)} collective-permute-done((bf16[16,2560]{1,0:T(8,128)(2,1)S(1)}, bf16[16,2560]{1,0:T(8,128)(2,1)S(1)}, u32[]{:S(2)}, u32[]{:S(2)}) %collective-permute-start.23) | collective-permute-done | bytes 81952 | tf_op jit(solution)/shard_map/ppermute | solution.py:252
  80.0 3.5 %collective-permute-done.24.refs_7_ = bf16[16,2560]{1,0:T(8,128)(2,1)S(1)} collective-permute-done((bf16[16,2560]{1,0:T(8,128)(2,1)S(1)}, bf16[16,2560]{1,0:T(8,128)(2,1)S(1)}, u32[]{:S(2)}, u32[]{:S(2)}) %collective-permute-start.24) | collective-permute-done | bytes 81952 | tf_op jit(solution)/shard_map/ppermute | solution.py:252
  83.5 0.2 shard_map.128
  83.7 0.1 collective-permute-start.25
  83.8 1.3 %collective-permute-done.25.more_ref = bf16[32,2176]{1,0:T(8,128)(2,1)S(1)} collective-permute-done((bf16[32,2176]{1,0:T(8,128)(2,1)S(1)}, bf16[32,2176]{1,0:T(8,128)(2,1)S(1)}, u32[]{:S(2)}, u32[]{:S(2)}) %collective-permute-start.25) | collective-permute-done | bytes 139296 | tf_op jit(solution)/shard_map/ppermute | solution.py:252
  85.2 2.7 %collective-permute-start.26 = (bf16[32,2176]{1,0:T(8,128)(2,1)S(1)}, bf16[32,2176]{1,0:T(8,128)(2,1)S(1)}, u32[]{:S(2)}, u32[]{:S(2)}) collective-permute-start(bf16[32,2176]{1,0:T(8,128)(2,1)S(1)} %shard_map.129), channel_id=1, source_target_pairs={{0,4},{1,5},{2,6},{3,7},{4,0},{5,1},{6,2},{7,3},{8,12},{9,13},{10,... | collective-permute-start | bytes 417800 | tf_op jit(solution)/shard_map/ppermute | solution.py:252
  87.8 0.2 shard_map.127
  88.1 0.1 collective-permute-start.17
  88.1 6.5 %collective-permute-done.26.far_ref = bf16[32,2176]{1,0:T(8,128)(2,1)S(1)} collective-permute-done((bf16[32,2176]{1,0:T(8,128)(2,1)S(1)}, bf16[32,2176]{1,0:T(8,128)(2,1)S(1)}, u32[]{:S(2)}, u32[]{:S(2)}) %collective-permute-start.26) | collective-permute-done | bytes 139296 | tf_op jit(solution)/shard_map/ppermute | solution.py:252
  94.7 0.7 shard_map.130
  (17 shorter events, 0.1 us)
Async XLA Ops:
  1.7 16.4 %collective-permute-start.8 = (bf16[32,4224]{1,0:T(8,128)(2,1)S(1)}, bf16[32,4224]{1,0:T(8,128)(2,1)S(1)}, u32[]{:S(2)}, u32[]{:S(2)}) collective-permute-start(bf16[32,4224]{1,0:T(8,128)(2,1)S(1)} %shard_map.122.first_ref), channel_id=1, source_target_pairs={{0,4},{1,5},{2,6},{3,7},{4,0},{5,1},{6,2},{7,3},{8,12},{9,13},{10,... | collective-permute-start | bytes 811016 | tf_op jit(solution)/shard_map/ppermute | solution.py:252
  5.8 12.3 %collective-permute-start = (bf16[32,4224]{1,0:T(8,128)(2,1)S(1)}, bf16[32,4224]{1,0:T(8,128)(2,1)S(1)}, u32[]{:S(2)}, u32[]{:S(2)}) collective-permute-start(bf16[32,4224]{1,0:T(8,128)(2,1)S(1)} %shard_map.122.first_ref), channel_id=1, source_target_pairs={{0,8},{1,9},{2,10},{3,11},{4,12},{5,13},{6,14},{7,15},{8,0},{9,1},... | collective-permute-start | bytes 811016 | tf_op jit(solution)/shard_map/ppermute | solution.py:252
  18.1 5.8 %collective-permute-start.9 = (bf16[32,4224]{1,0:T(8,128)(2,1)S(1)}, bf16[32,4224]{1,0:T(8,128)(2,1)S(1)}, u32[]{:S(2)}, u32[]{:S(2)}) collective-permute-start(bf16[32,4224]{1,0:T(8,128)(2,1)S(1)} %collective-permute-done.8.first_ref), channel_id=1, source_target_pairs={{0,8},{1,9},{2,10},{3,11},{4,12},{5,13},{6,14},{7,15},{8,0},{9,1},... | collective-permute-start | bytes 811016 | tf_op jit(solution)/shard_map/ppermute | solution.py:252
  18.8 7.3 %collective-permute-start.1 = (bf16[16,4096]{1,0:T(8,128)(2,1)S(1)}, bf16[16,4096]{1,0:T(8,128)(2,1)S(1)}, u32[]{:S(2)}, u32[]{:S(2)}) collective-permute-start(bf16[16,4096]{1,0:T(8,128)(2,1)S(1)} %get-tuple-element.44), channel_id=1, source_target_pairs={{0,1},{1,0},{2,3},{3,2},{4,5},{5,4},{6,7},{7,6},{8,9},{9,8},{10,11... | collective-permute-start | bytes 393224 | tf_op jit(solution)/shard_map/ppermute | solution.py:252
  20.4 7.4 %collective-permute-start.2 = (bf16[16,4096]{1,0:T(8,128)(2,1)S(1)}, bf16[16,4096]{1,0:T(8,128)(2,1)S(1)}, u32[]{:S(2)}, u32[]{:S(2)}) collective-permute-start(bf16[16,4096]{1,0:T(8,128)(2,1)S(1)} %get-tuple-element.45), channel_id=1, source_target_pairs={{0,2},{1,3},{2,0},{3,1},{4,6},{5,7},{6,4},{7,5},{8,10},{9,11},{10,... | collective-permute-start | bytes 393224 | tf_op jit(solution)/shard_map/ppermute | solution.py:252
  21.1 7.9 %collective-permute-start.3 = (bf16[16,4096]{1,0:T(8,128)(2,1)S(1)}, bf16[16,4096]{1,0:T(8,128)(2,1)S(1)}, u32[]{:S(2)}, u32[]{:S(2)}) collective-permute-start(bf16[16,4096]{1,0:T(8,128)(2,1)S(1)} %get-tuple-element.46), channel_id=1, source_target_pairs={{0,3},{1,2},{2,1},{3,0},{4,7},{5,6},{6,5},{7,4},{8,11},{9,10},{10,... | collective-permute-start | bytes 393224 | tf_op jit(solution)/shard_map/ppermute | solution.py:252
  22.4 8.2 %collective-permute-start.4 = (bf16[16,4096]{1,0:T(8,128)(2,1)S(1)}, bf16[16,4096]{1,0:T(8,128)(2,1)S(1)}, u32[]{:S(2)}, u32[]{:S(2)}) collective-permute-start(bf16[16,4096]{1,0:T(8,128)(2,1)S(1)} %get-tuple-element.47), channel_id=1, source_target_pairs={{0,16},{1,17},{2,18},{3,19},{4,20},{5,21},{6,22},{7,23},{8,24},{9,... | collective-permute-start | bytes 393224 | tf_op jit(solution)/shard_map/ppermute | solution.py:252
  23.9 13.3 %collective-permute-start.5 = (bf16[16,4096]{1,0:T(8,128)(2,1)S(1)}, bf16[16,4096]{1,0:T(8,128)(2,1)S(1)}, u32[]{:S(2)}, u32[]{:S(2)}) collective-permute-start(bf16[16,4096]{1,0:T(8,128)(2,1)S(1)} %get-tuple-element.48), channel_id=1, source_target_pairs={{0,17},{1,16},{2,19},{3,18},{4,21},{5,20},{6,23},{7,22},{8,25},{9,... | collective-permute-start | bytes 393224 | tf_op jit(solution)/shard_map/ppermute | solution.py:252
  26.1 12.3 %collective-permute-start.6 = (bf16[16,4096]{1,0:T(8,128)(2,1)S(1)}, bf16[16,4096]{1,0:T(8,128)(2,1)S(1)}, u32[]{:S(2)}, u32[]{:S(2)}) collective-permute-start(bf16[16,4096]{1,0:T(8,128)(2,1)S(1)} %get-tuple-element.49), channel_id=1, source_target_pairs={{0,18},{1,19},{2,16},{3,17},{4,22},{5,23},{6,20},{7,21},{8,26},{9,... | collective-permute-start | bytes 393224 | tf_op jit(solution)/shard_map/ppermute | solution.py:252
  27.8 12.2 %collective-permute-start.7 = (bf16[16,4096]{1,0:T(8,128)(2,1)S(1)}, bf16[16,4096]{1,0:T(8,128)(2,1)S(1)}, u32[]{:S(2)}, u32[]{:S(2)}) collective-permute-start(bf16[16,4096]{1,0:T(8,128)(2,1)S(1)} %get-tuple-element.50), channel_id=1, source_target_pairs={{0,19},{1,18},{2,17},{3,16},{4,23},{5,22},{6,21},{7,20},{8,27},{9,... | collective-permute-start | bytes 393224 | tf_op jit(solution)/shard_map/ppermute | solution.py:252
  29.0 12.4 %collective-permute-start.10 = (bf16[16,4096]{1,0:T(8,128)(2,1)S(1)}, bf16[16,4096]{1,0:T(8,128)(2,1)S(1)}, u32[]{:S(2)}, u32[]{:S(2)}) collective-permute-start(bf16[16,4096]{1,0:T(8,128)(2,1)S(1)} %get-tuple-element.52), channel_id=1, source_target_pairs={{0,1},{1,0},{2,3},{3,2},{4,5},{5,4},{6,7},{7,6},{8,9},{9,8},{10,11... | collective-permute-start | bytes 393224 | tf_op jit(solution)/shard_map/ppermute | solution.py:252
  30.6 13.8 %collective-permute-start.11 = (bf16[16,4096]{1,0:T(8,128)(2,1)S(1)}, bf16[16,4096]{1,0:T(8,128)(2,1)S(1)}, u32[]{:S(2)}, u32[]{:S(2)}) collective-permute-start(bf16[16,4096]{1,0:T(8,128)(2,1)S(1)} %get-tuple-element.53), channel_id=1, source_target_pairs={{0,2},{1,3},{2,0},{3,1},{4,6},{5,7},{6,4},{7,5},{8,10},{9,11},{10,... | collective-permute-start | bytes 393224 | tf_op jit(solution)/shard_map/ppermute | solution.py:252
  37.3 14.4 %collective-permute-start.12 = (bf16[16,4096]{1,0:T(8,128)(2,1)S(1)}, bf16[16,4096]{1,0:T(8,128)(2,1)S(1)}, u32[]{:S(2)}, u32[]{:S(2)}) collective-permute-start(bf16[16,4096]{1,0:T(8,128)(2,1)S(1)} %get-tuple-element.54), channel_id=1, source_target_pairs={{0,3},{1,2},{2,1},{3,0},{4,7},{5,6},{6,5},{7,4},{8,11},{9,10},{10,... | collective-permute-start | bytes 393224 | tf_op jit(solution)/shard_map/ppermute | solution.py:252
  38.4 13.3 %collective-permute-start.13 = (bf16[16,4096]{1,0:T(8,128)(2,1)S(1)}, bf16[16,4096]{1,0:T(8,128)(2,1)S(1)}, u32[]{:S(2)}, u32[]{:S(2)}) collective-permute-start(bf16[16,4096]{1,0:T(8,128)(2,1)S(1)} %get-tuple-element.55), channel_id=1, source_target_pairs={{0,16},{1,17},{2,18},{3,19},{4,20},{5,21},{6,22},{7,23},{8,24},{9,... | collective-permute-start | bytes 393224 | tf_op jit(solution)/shard_map/ppermute | solution.py:252
  40.0 11.8 %collective-permute-start.14 = (bf16[16,4096]{1,0:T(8,128)(2,1)S(1)}, bf16[16,4096]{1,0:T(8,128)(2,1)S(1)}, u32[]{:S(2)}, u32[]{:S(2)}) collective-permute-start(bf16[16,4096]{1,0:T(8,128)(2,1)S(1)} %get-tuple-element.56), channel_id=1, source_target_pairs={{0,17},{1,16},{2,19},{3,18},{4,21},{5,20},{6,23},{7,22},{8,25},{9,... | collective-permute-start | bytes 393224 | tf_op jit(solution)/shard_map/ppermute | solution.py:252
  41.4 10.3 %collective-permute-start.15 = (bf16[16,4096]{1,0:T(8,128)(2,1)S(1)}, bf16[16,4096]{1,0:T(8,128)(2,1)S(1)}, u32[]{:S(2)}, u32[]{:S(2)}) collective-permute-start(bf16[16,4096]{1,0:T(8,128)(2,1)S(1)} %get-tuple-element.57), channel_id=1, source_target_pairs={{0,18},{1,19},{2,16},{3,17},{4,22},{5,23},{6,20},{7,21},{8,26},{9,... | collective-permute-start | bytes 393224 | tf_op jit(solution)/shard_map/ppermute | solution.py:252
  44.4 7.4 %collective-permute-start.16 = (bf16[16,4096]{1,0:T(8,128)(2,1)S(1)}, bf16[16,4096]{1,0:T(8,128)(2,1)S(1)}, u32[]{:S(2)}, u32[]{:S(2)}) collective-permute-start(bf16[16,4096]{1,0:T(8,128)(2,1)S(1)} %get-tuple-element.58), channel_id=1, source_target_pairs={{0,19},{1,18},{2,17},{3,16},{4,23},{5,22},{6,21},{7,20},{8,27},{9,... | collective-permute-start | bytes 393224 | tf_op jit(solution)/shard_map/ppermute | solution.py:252
  59.2 28.6 %all-to-all-start = ((bf16[8,16,2560]{2,1,0:T(8,128)(2,1)}), bf16[8,16,2560]{2,1,0:T(8,128)(2,1)S(1)}, u32[]{:S(2)}, u32[]{:S(2)}) async-start(bf16[8,16,2560]{2,1,0:T(8,128)(2,1)} %get-tuple-element.65), calls=%async_computation | async-start | bytes 1310720 | tf_op jit(solution)/shard_map/all_to_all | solution.py:313
  64.3 10.3 %collective-permute-start.18 = (bf16[16,2560]{1,0:T(8,128)(2,1)S(1)}, bf16[16,2560]{1,0:T(8,128)(2,1)S(1)}, u32[]{:S(2)}, u32[]{:S(2)}) collective-permute-start(bf16[16,2560]{1,0:T(8,128)(2,1)S(1)} %get-tuple-element.71), channel_id=1, source_target_pairs={{0,1},{1,0},{2,3},{3,2},{4,5},{5,4},{6,7},{7,6},{8,9},{9,8},{10,11... | collective-permute-start | bytes 245768 | tf_op jit(solution)/shard_map/ppermute | solution.py:252
  66.3 10.9 %collective-permute-start.19 = (bf16[16,2560]{1,0:T(8,128)(2,1)S(1)}, bf16[16,2560]{1,0:T(8,128)(2,1)S(1)}, u32[]{:S(2)}, u32[]{:S(2)}) collective-permute-start(bf16[16,2560]{1,0:T(8,128)(2,1)S(1)} %get-tuple-element.72), channel_id=1, source_target_pairs={{0,2},{1,3},{2,0},{3,1},{4,6},{5,7},{6,4},{7,5},{8,10},{9,11},{10,... | collective-permute-start | bytes 245768 | tf_op jit(solution)/shard_map/ppermute | solution.py:252
  67.8 9.6 %collective-permute-start.20 = (bf16[16,2560]{1,0:T(8,128)(2,1)S(1)}, bf16[16,2560]{1,0:T(8,128)(2,1)S(1)}, u32[]{:S(2)}, u32[]{:S(2)}) collective-permute-start(bf16[16,2560]{1,0:T(8,128)(2,1)S(1)} %get-tuple-element.73), channel_id=1, source_target_pairs={{0,3},{1,2},{2,1},{3,0},{4,7},{5,6},{6,5},{7,4},{8,11},{9,10},{10,... | collective-permute-start | bytes 245768 | tf_op jit(solution)/shard_map/ppermute | solution.py:252
  67.8 9.5 %collective-permute-start.21 = (bf16[16,2560]{1,0:T(8,128)(2,1)S(1)}, bf16[16,2560]{1,0:T(8,128)(2,1)S(1)}, u32[]{:S(2)}, u32[]{:S(2)}) collective-permute-start(bf16[16,2560]{1,0:T(8,128)(2,1)S(1)} %get-tuple-element.74), channel_id=1, source_target_pairs={{0,16},{1,17},{2,18},{3,19},{4,20},{5,21},{6,22},{7,23},{8,24},{9,... | collective-permute-start | bytes 245768 | tf_op jit(solution)/shard_map/ppermute | solution.py:252
  69.8 7.5 %collective-permute-start.22 = (bf16[16,2560]{1,0:T(8,128)(2,1)S(1)}, bf16[16,2560]{1,0:T(8,128)(2,1)S(1)}, u32[]{:S(2)}, u32[]{:S(2)}) collective-permute-start(bf16[16,2560]{1,0:T(8,128)(2,1)S(1)} %get-tuple-element.75), channel_id=1, source_target_pairs={{0,17},{1,16},{2,19},{3,18},{4,21},{5,20},{6,23},{7,22},{8,25},{9,... | collective-permute-start | bytes 245768 | tf_op jit(solution)/shard_map/ppermute | solution.py:252
  74.7 5.3 %collective-permute-start.23 = (bf16[16,2560]{1,0:T(8,128)(2,1)S(1)}, bf16[16,2560]{1,0:T(8,128)(2,1)S(1)}, u32[]{:S(2)}, u32[]{:S(2)}) collective-permute-start(bf16[16,2560]{1,0:T(8,128)(2,1)S(1)} %get-tuple-element.76), channel_id=1, source_target_pairs={{0,18},{1,19},{2,16},{3,17},{4,22},{5,23},{6,20},{7,21},{8,26},{9,... | collective-permute-start | bytes 245768 | tf_op jit(solution)/shard_map/ppermute | solution.py:252
  77.2 6.2 %collective-permute-start.24 = (bf16[16,2560]{1,0:T(8,128)(2,1)S(1)}, bf16[16,2560]{1,0:T(8,128)(2,1)S(1)}, u32[]{:S(2)}, u32[]{:S(2)}) collective-permute-start(bf16[16,2560]{1,0:T(8,128)(2,1)S(1)} %get-tuple-element.77), channel_id=1, source_target_pairs={{0,19},{1,18},{2,17},{3,16},{4,23},{5,22},{6,21},{7,20},{8,27},{9,... | collective-permute-start | bytes 245768 | tf_op jit(solution)/shard_map/ppermute | solution.py:252
  83.7 1.4 %collective-permute-start.25 = (bf16[32,2176]{1,0:T(8,128)(2,1)S(1)}, bf16[32,2176]{1,0:T(8,128)(2,1)S(1)}, u32[]{:S(2)}, u32[]{:S(2)}) collective-permute-start(bf16[32,2176]{1,0:T(8,128)(2,1)S(1)} %get-tuple-element.79), channel_id=1, source_target_pairs={{0,8},{1,9},{2,10},{3,11},{4,12},{5,13},{6,14},{7,15},{8,0},{9,1},... | collective-permute-start | bytes 417800 | tf_op jit(solution)/shard_map/ppermute | solution.py:252
  85.2 9.5 %collective-permute-start.26 = (bf16[32,2176]{1,0:T(8,128)(2,1)S(1)}, bf16[32,2176]{1,0:T(8,128)(2,1)S(1)}, u32[]{:S(2)}, u32[]{:S(2)}) collective-permute-start(bf16[32,2176]{1,0:T(8,128)(2,1)S(1)} %shard_map.129), channel_id=1, source_target_pairs={{0,4},{1,5},{2,6},{3,7},{4,0},{5,1},{6,2},{7,3},{8,12},{9,13},{10,... | collective-permute-start | bytes 417800 | tf_op jit(solution)/shard_map/ppermute | solution.py:252
  88.1 6.6 %collective-permute-start.17 = (bf16[32,2176]{1,0:T(8,128)(2,1)S(1)}, bf16[32,2176]{1,0:T(8,128)(2,1)S(1)}, u32[]{:S(2)}, u32[]{:S(2)}) collective-permute-start(bf16[32,2176]{1,0:T(8,128)(2,1)S(1)} %get-tuple-element.67), channel_id=1, source_target_pairs={{0,8},{1,9},{2,10},{3,11},{4,12},{5,13},{6,14},{7,15},{8,0},{9,1},... | collective-permute-start | bytes 417800 | tf_op jit(solution)/shard_map/ppermute | solution.py:252

commit v8 on v7

--- a/solution.py
+++ b/solution.py
@@ -26,16 +26,16 @@
 
 
 def pay_kernel(
-    ids_hbm, w_hbm, query_hbm, x_hbm, g_hbm, pay_ref, ids_ref, w_ref, query_ref, x_ref, g_ref, sem
+    ids_hbm, w_hbm, query_hbm, x_hbm, g_hbm, pay_ref, ids_ref, w_ref, query_ref, sem
 ):
     top, tok = ids_ref.shape
-    width = x_ref.shape[1]
+    width = x_hbm.shape[1]
     pairs = (
         (ids_hbm, ids_ref),
         (w_hbm, w_ref),
         (query_hbm, query_ref),
-        (x_hbm, x_ref),
-        (g_hbm, g_ref),
+        (x_hbm, pay_ref.at[:, :width]),
+        (g_hbm, pay_ref.at[:, width : 2 * width]),
     )
     copies = [pltpu.make_async_copy(a, b, sem.at[i]) for i, (a, b) in enumerate(pairs)]
     for copy in copies:
@@ -46,10 +46,8 @@
     flat = jnp.concatenate(parts + [jnp.zeros((LANES - 2 * top - 1, tok), F32)], axis=0)
     flat = jnp.concatenate([flat, jnp.zeros((LANES, LANES - tok), F32)], axis=1)
     pay_ref[:, 2 * width :] = flat.T[:tok, :].astype(BF16)
-    copies[3].wait()
-    pay_ref[:, :width] = x_ref[...]
-    copies[4].wait()
-    pay_ref[:, width : 2 * width] = g_ref[...]
+    for copy in copies[3:]:
+        copy.wait()
 
 
 def pack_kernel(top, experts, capacity, deep, first_ref, second_ref, *outs):
@@ -106,10 +104,11 @@
 
 def expert_kernel(count, group, deep, *refs):
     ins, weights = refs[:count], refs[count : count + 6]
-    own_ref, outs, stage_ref = refs[count + 6], refs[count + 7 : -2], refs[-2]
+    own_ref, outs, stage_ref = refs[count + 6], refs[count + 7 : -3], refs[-3]
+    sem = refs[-1]
     me = lax.axis_index("row") * deep + lax.axis_index("deep")
     gate, up, down, left_proj, right_proj, stored = weights
-    outer_ref = refs[-1]
+    outer_ref = refs[-2]
     experts, width, _ = gate.shape
     rank = left_proj.shape[1]
     half = count // 2
@@ -155,6 +154,14 @@
     def scores(j):
         put(j, dot(outer_ref[j], stored[j]), slice(width, width + stored.shape[2]))
 
+    def send(step, columns):
+        copies = []
+        for i in range(half):
+            source, target = stage_ref.at[i, :, columns], own_ref.at[i ^ me, :, columns]
+            copies.append(pltpu.make_async_copy(source, target, sem.at[step, i]))
+            copies[-1].start()
+        return copies
+
     every = range(experts)
     second = []
     for j in every:
@@ -162,9 +169,12 @@
     for j in every:
         outers(j, *second[j][2:])
         grads(j, *second[j][:2])
+        if j == experts - 1:
+            copies = send(0, slice(0, width))
         scores(j)
-    for i in range(half):
-        own_ref[i ^ me] = stage_ref[i]
+    copies += send(1, slice(width, width + stored.shape[2]))
+    for copy in copies:
+        copy.wait()
 
 
 def token_sums(place_ref, tally_ref, ins, keep_ref, give_ref):
@@ -215,12 +225,12 @@
     return pltpu.with_memory_space_constraint(value, pltpu.HBM)
 
 
-def call(kernel, outs, in_specs, args, scratch=(), flops=1_000_000, moved=1_000_000, limit=8 << 20):
+def call(kernel, outs, in_specs, args, scratch=(), flops=1_000_000, moved=1_000_000, limit=8 << 20, out_specs=None):
     return pl.pallas_call(
         kernel,
         out_shape=outs,
         in_specs=in_specs,
-        out_specs=jax.tree.map(lambda _: VMEM, outs),
+        out_specs=out_specs or jax.tree.map(lambda _: VMEM, outs),
         scratch_shapes=scratch,
         compiler_params=pltpu.CompilerParams(vmem_limit_bytes=limit),
         cost_estimate=pl.CostEstimate(flops=flops, bytes_accessed=moved, transcendentals=0),
@@ -274,7 +284,7 @@
         shape((tok, 2 * width + LANES), BF16),
         [HBM] * len(inputs),
         inputs,
-        scratch=[pltpu.VMEM(v.shape, v.dtype) for v in inputs]
+        scratch=[pltpu.VMEM(v.shape, v.dtype) for v in inputs[:3]]
         + [pltpu.SemaphoreType.DMA((len(inputs),))],
     )
     guest = swap(pay, half=1)
@@ -303,7 +313,9 @@
         scratch=[
             pltpu.VMEM((chips, piece, width + train), BF16),
             pltpu.VMEM((experts, rows // experts, weights[5].shape[1]), BF16),
+            pltpu.SemaphoreType.DMA((2, chips)),
         ],
+        out_specs=(HBM,) + (VMEM,) * chips,
         flops=2 * rows * size,
         moved=2 * size,
         limit=rows * (76 << 10),

time: 95.6 us -> 95.5 us (level)
  no operation moved by 1% of the time
where the time goes in v8:
time: 95.5 us; the launch traced here: 95.3 us
  starting transfers between devices  40.3 us (42%)
  waiting for transfers between devices  35.9 us (38%)
  Pallas kernels  18.4 us (19%)
    ppermute x27, waiting for transfers between devices, swap(): return lax.ppermute(value, AXES, pairs)  35.9 us
    ppermute x27, starting transfers between devices, swap(): return lax.ppermute(value, AXES, pairs)  35.2 us
    pallas_call x8, Pallas kernels, call(): pl.pallas_call(kernel, out_shape=outs, in_specs=in_specs, out_specs=out_s...  11.1 us
    pallas_call x1, Pallas kernels, layer(): pl.pallas_call(load_kernel, out_shape=tuple((pltpu.VMEM(w.shape, w.dtype)...  7.29 us
    all_to_all x1, starting transfers between devices, layer(): own_back = lax.all_to_all(outs[0], ('row', 'deep'), 0, 0, tiled=True)  5.07 us
  transfers between devices with their start and end apart: 28, of which 9 were waited for; matrix products, arithmetic and copies ran while one was open for 0% of the time, Pallas kernels for 10%

profile of v8, /device:TPU:0, one launch (start us, length us, event | category | flops | bytes accessed | tf_op | source)
XLA Modules:
  0.0 95.3 jit_solution(6234391084948982775)
XLA Ops:
  0.6 1.1 %shard_map.122.first_ref = bf16[32,4224]{1,0:T(8,128)(2,1)S(1)} custom-call(s32[4,32]{1,0:T(4,128)} %bitcast.6, bf16[4,32]{1,0:T(4,128)(2,1)} %bitcast.7, s32[1,32]{1,0:T(1,128)} %query_hbm.1, bf16[32,2048]{1,0:T(8,128)(2,1)} %x_hbm.1, bf16[32,2048]{1,0:T(8,128)(2,1)} %g_hbm.1), custom_call_target="tpu_custom_call" | custom-call | flops 1000000 | bytes 1000000 | tf_op jit(solution)/shard_map/pallas_call | solution.py:229
  1.7 4.1 %collective-permute-start.8 = (bf16[32,4224]{1,0:T(8,128)(2,1)S(1)}, bf16[32,4224]{1,0:T(8,128)(2,1)S(1)}, u32[]{:S(2)}, u32[]{:S(2)}) collective-permute-start(bf16[32,4224]{1,0:T(8,128)(2,1)S(1)} %shard_map.122.first_ref), channel_id=1, source_target_pairs={{0,4},{1,5},{2,6},{3,7},{4,0},{5,1},{6,2},{7,3},{8,12},{9,13},{10,... | collective-permute-start | bytes 811016 | tf_op jit(solution)/shard_map/ppermute | solution.py:262
  5.8 12.3 %collective-permute-done.8.first_ref = bf16[32,4224]{1,0:T(8,128)(2,1)S(1)} collective-permute-done((bf16[32,4224]{1,0:T(8,128)(2,1)S(1)}, bf16[32,4224]{1,0:T(8,128)(2,1)S(1)}, u32[]{:S(2)}, u32[]{:S(2)}) %collective-permute-start.8) | collective-permute-done | bytes 270368 | tf_op jit(solution)/shard_map/ppermute | solution.py:262
  18.1 0.0 collective-permute-start.9
  18.1 0.0 collective-permute-done.second_ref
  18.1 0.7 shard_map.123
  18.8 1.6 %collective-permute-start.1 = (bf16[16,4096]{1,0:T(8,128)(2,1)S(1)}, bf16[16,4096]{1,0:T(8,128)(2,1)S(1)}, u32[]{:S(2)}, u32[]{:S(2)}) collective-permute-start(bf16[16,4096]{1,0:T(8,128)(2,1)S(1)} %get-tuple-element.44), channel_id=1, source_target_pairs={{0,1},{1,0},{2,3},{3,2},{4,5},{5,4},{6,7},{7,6},{8,9},{9,8},{10,11... | collective-permute-start | bytes 393224 | tf_op jit(solution)/shard_map/ppermute | solution.py:262
  20.4 0.7 collective-permute-start.2
  21.1 1.3 %collective-permute-start.3 = (bf16[16,4096]{1,0:T(8,128)(2,1)S(1)}, bf16[16,4096]{1,0:T(8,128)(2,1)S(1)}, u32[]{:S(2)}, u32[]{:S(2)}) collective-permute-start(bf16[16,4096]{1,0:T(8,128)(2,1)S(1)} %get-tuple-element.46), channel_id=1, source_target_pairs={{0,3},{1,2},{2,1},{3,0},{4,7},{5,6},{6,5},{7,4},{8,11},{9,10},{10,... | collective-permute-start | bytes 393224 | tf_op jit(solution)/shard_map/ppermute | solution.py:262
  22.4 1.6 %collective-permute-start.4 = (bf16[16,4096]{1,0:T(8,128)(2,1)S(1)}, bf16[16,4096]{1,0:T(8,128)(2,1)S(1)}, u32[]{:S(2)}, u32[]{:S(2)}) collective-permute-start(bf16[16,4096]{1,0:T(8,128)(2,1)S(1)} %get-tuple-element.47), channel_id=1, source_target_pairs={{0,16},{1,17},{2,18},{3,19},{4,20},{5,21},{6,22},{7,23},{8,24},{9,... | collective-permute-start | bytes 393224 | tf_op jit(solution)/shard_map/ppermute | solution.py:262
  23.9 0.0 collective-permute-done.9.second_ref
  23.9 1.4 %collective-permute-start.5 = (bf16[16,4096]{1,0:T(8,128)(2,1)S(1)}, bf16[16,4096]{1,0:T(8,128)(2,1)S(1)}, u32[]{:S(2)}, u32[]{:S(2)}) collective-permute-start(bf16[16,4096]{1,0:T(8,128)(2,1)S(1)} %get-tuple-element.48), channel_id=1, source_target_pairs={{0,17},{1,16},{2,19},{3,18},{4,21},{5,20},{6,23},{7,22},{8,25},{9,... | collective-permute-start | bytes 393224 | tf_op jit(solution)/shard_map/ppermute | solution.py:262
  25.4 0.7 shard_map.124
  26.1 1.7 %collective-permute-start.6 = (bf16[16,4096]{1,0:T(8,128)(2,1)S(1)}, bf16[16,4096]{1,0:T(8,128)(2,1)S(1)}, u32[]{:S(2)}, u32[]{:S(2)}) collective-permute-start(bf16[16,4096]{1,0:T(8,128)(2,1)S(1)} %get-tuple-element.49), channel_id=1, source_target_pairs={{0,18},{1,19},{2,16},{3,17},{4,22},{5,23},{6,20},{7,21},{8,26},{9,... | collective-permute-start | bytes 393224 | tf_op jit(solution)/shard_map/ppermute | solution.py:262
  27.8 0.0 collective-permute-done.2.refs_2_
  27.8 1.2 %collective-permute-start.7 = (bf16[16,4096]{1,0:T(8,128)(2,1)S(1)}, bf16[16,4096]{1,0:T(8,128)(2,1)S(1)}, u32[]{:S(2)}, u32[]{:S(2)}) collective-permute-start(bf16[16,4096]{1,0:T(8,128)(2,1)S(1)} %get-tuple-element.50), channel_id=1, source_target_pairs={{0,19},{1,18},{2,17},{3,16},{4,23},{5,22},{6,21},{7,20},{8,27},{9,... | collective-permute-start | bytes 393224 | tf_op jit(solution)/shard_map/ppermute | solution.py:262
  29.0 0.0 collective-permute-done.3.refs_3_
  29.0 1.5 %collective-permute-start.10 = (bf16[16,4096]{1,0:T(8,128)(2,1)S(1)}, bf16[16,4096]{1,0:T(8,128)(2,1)S(1)}, u32[]{:S(2)}, u32[]{:S(2)}) collective-permute-start(bf16[16,4096]{1,0:T(8,128)(2,1)S(1)} %get-tuple-element.52), channel_id=1, source_target_pairs={{0,1},{1,0},{2,3},{3,2},{4,5},{5,4},{6,7},{7,6},{8,9},{9,8},{10,11... | collective-permute-start | bytes 393224 | tf_op jit(solution)/shard_map/ppermute | solution.py:262
  30.5 0.0 collective-permute-done.4.refs_4_
  30.5 0.7 collective-permute-start.11
  31.2 6.0 %collective-permute-done.5.refs_5_ = bf16[16,4096]{1,0:T(8,128)(2,1)S(1)} collective-permute-done((bf16[16,4096]{1,0:T(8,128)(2,1)S(1)}, bf16[16,4096]{1,0:T(8,128)(2,1)S(1)}, u32[]{:S(2)}, u32[]{:S(2)}) %collective-permute-start.5) | collective-permute-done | bytes 131104 | tf_op jit(solution)/shard_map/ppermute | solution.py:262
  37.3 1.2 %collective-permute-start.12 = (bf16[16,4096]{1,0:T(8,128)(2,1)S(1)}, bf16[16,4096]{1,0:T(8,128)(2,1)S(1)}, u32[]{:S(2)}, u32[]{:S(2)}) collective-permute-start(bf16[16,4096]{1,0:T(8,128)(2,1)S(1)} %get-tuple-element.54), channel_id=1, source_target_pairs={{0,3},{1,2},{2,1},{3,0},{4,7},{5,6},{6,5},{7,4},{8,11},{9,10},{10,... | collective-permute-start | bytes 393224 | tf_op jit(solution)/shard_map/ppermute | solution.py:262
  38.4 1.5 %collective-permute-start.13 = (bf16[16,4096]{1,0:T(8,128)(2,1)S(1)}, bf16[16,4096]{1,0:T(8,128)(2,1)S(1)}, u32[]{:S(2)}, u32[]{:S(2)}) collective-permute-start(bf16[16,4096]{1,0:T(8,128)(2,1)S(1)} %get-tuple-element.55), channel_id=1, source_target_pairs={{0,16},{1,17},{2,18},{3,19},{4,20},{5,21},{6,22},{7,23},{8,24},{9,... | collective-permute-start | bytes 393224 | tf_op jit(solution)/shard_map/ppermute | solution.py:262
  40.0 1.3 %collective-permute-start.14 = (bf16[16,4096]{1,0:T(8,128)(2,1)S(1)}, bf16[16,4096]{1,0:T(8,128)(2,1)S(1)}, u32[]{:S(2)}, u32[]{:S(2)}) collective-permute-start(bf16[16,4096]{1,0:T(8,128)(2,1)S(1)} %get-tuple-element.56), channel_id=1, source_target_pairs={{0,17},{1,16},{2,19},{3,18},{4,21},{5,20},{6,23},{7,22},{8,25},{9,... | collective-permute-start | bytes 393224 | tf_op jit(solution)/shard_map/ppermute | solution.py:262
  41.2 0.2 collective-permute-done.10.refs_9_
  41.4 2.9 %collective-permute-start.15 = (bf16[16,4096]{1,0:T(8,128)(2,1)S(1)}, bf16[16,4096]{1,0:T(8,128)(2,1)S(1)}, u32[]{:S(2)}, u32[]{:S(2)}) collective-permute-start(bf16[16,4096]{1,0:T(8,128)(2,1)S(1)} %get-tuple-element.57), channel_id=1, source_target_pairs={{0,18},{1,19},{2,16},{3,17},{4,22},{5,23},{6,20},{7,21},{8,26},{9,... | collective-permute-start | bytes 393224 | tf_op jit(solution)/shard_map/ppermute | solution.py:262
  44.4 7.3 %shard_map.125 = (bf16[2,2048,512]{2,1,0:T(8,128)(2,1)S(1)}, bf16[2,2048,512]{2,1,0:T(8,128)(2,1)S(1)}, bf16[2,512,2048]{2,1,0:T(8,128)(2,1)S(1)}, bf16[2,64,204...) custom-call(bf16[2,2048,512]{2,1,0:T(8,128)(2,1)} %refs_0_.1, ...), custom_call_target="tpu_custom_call" | custom-call | tf_op jit(solution)/shard_map/pallas_call | solution.py:297
  51.7 0.1 collective-permute-done.13.refs_12_
  51.8 7.5 %shard_map.126 = (bf16[8,16,2560]{2,1,0:T(8,128)(2,1)}, bf16[16,2560]{1,0:T(8,128)(2,1)S(1)}, bf16[16,2560]{1,0:T(8,128)(2,1)S(1)}, bf16[16,2560]{1,0:T(8,128)(2...) custom-call(bf16[16,4096]{1,0:T(8,128)(2,1)S(1)} %get-tuple-element., ...), custom_call_target="tpu_custom_call" | custom-call | flops 5536481280 | bytes 21626880 | tf_op jit(solution)/shard_map/pallas_call | solution.py:229
  59.2 5.1 %all-to-all-start = ((bf16[8,16,2560]{2,1,0:T(8,128)(2,1)}), bf16[8,16,2560]{2,1,0:T(8,128)(2,1)S(1)}, u32[]{:S(2)}, u32[]{:S(2)}) async-start(bf16[8,16,2560]{2,1,0:T(8,128)(2,1)} %get-tuple-element.65), calls=%async_computation | async-start | bytes 1310720 | tf_op jit(solution)/shard_map/all_to_all | solution.py:325
  64.3 2.0 %collective-permute-start.18 = (bf16[16,2560]{1,0:T(8,128)(2,1)S(1)}, bf16[16,2560]{1,0:T(8,128)(2,1)S(1)}, u32[]{:S(2)}, u32[]{:S(2)}) collective-permute-start(bf16[16,2560]{1,0:T(8,128)(2,1)S(1)} %get-tuple-element.71), channel_id=1, source_target_pairs={{0,1},{1,0},{2,3},{3,2},{4,5},{5,4},{6,7},{7,6},{8,9},{9,8},{10,11... | collective-permute-start | bytes 245768 | tf_op jit(solution)/shard_map/ppermute | solution.py:262
  66.3 1.5 %collective-permute-start.19 = (bf16[16,2560]{1,0:T(8,128)(2,1)S(1)}, bf16[16,2560]{1,0:T(8,128)(2,1)S(1)}, u32[]{:S(2)}, u32[]{:S(2)}) collective-permute-start(bf16[16,2560]{1,0:T(8,128)(2,1)S(1)} %get-tuple-element.72), channel_id=1, source_target_pairs={{0,2},{1,3},{2,0},{3,1},{4,6},{5,7},{6,4},{7,5},{8,10},{9,11},{10,... | collective-permute-start | bytes 245768 | tf_op jit(solution)/shard_map/ppermute | solution.py:262
  67.8 0.0 collective-permute-start.20
  67.8 2.0 %collective-permute-start.21 = (bf16[16,2560]{1,0:T(8,128)(2,1)S(1)}, bf16[16,2560]{1,0:T(8,128)(2,1)S(1)}, u32[]{:S(2)}, u32[]{:S(2)}) collective-permute-start(bf16[16,2560]{1,0:T(8,128)(2,1)S(1)} %get-tuple-element.74), channel_id=1, source_target_pairs={{0,16},{1,17},{2,18},{3,19},{4,20},{5,21},{6,22},{7,23},{8,24},{9,... | collective-permute-start | bytes 245768 | tf_op jit(solution)/shard_map/ppermute | solution.py:262
  69.8 1.5 %collective-permute-start.22 = (bf16[16,2560]{1,0:T(8,128)(2,1)S(1)}, bf16[16,2560]{1,0:T(8,128)(2,1)S(1)}, u32[]{:S(2)}, u32[]{:S(2)}) collective-permute-start(bf16[16,2560]{1,0:T(8,128)(2,1)S(1)} %get-tuple-element.75), channel_id=1, source_target_pairs={{0,17},{1,16},{2,19},{3,18},{4,21},{5,20},{6,23},{7,22},{8,25},{9,... | collective-permute-start | bytes 245768 | tf_op jit(solution)/shard_map/ppermute | solution.py:262
  71.3 3.4 %collective-permute-done.18.refs_1_ = bf16[16,2560]{1,0:T(8,128)(2,1)S(1)} collective-permute-done((bf16[16,2560]{1,0:T(8,128)(2,1)S(1)}, bf16[16,2560]{1,0:T(8,128)(2,1)S(1)}, u32[]{:S(2)}, u32[]{:S(2)}) %collective-permute-start.18) | collective-permute-done | bytes 81952 | tf_op jit(solution)/shard_map/ppermute | solution.py:262
  74.6 2.6 %collective-permute-start.23 = (bf16[16,2560]{1,0:T(8,128)(2,1)S(1)}, bf16[16,2560]{1,0:T(8,128)(2,1)S(1)}, u32[]{:S(2)}, u32[]{:S(2)}) collective-permute-start(bf16[16,2560]{1,0:T(8,128)(2,1)S(1)} %get-tuple-element.76), channel_id=1, source_target_pairs={{0,18},{1,19},{2,16},{3,17},{4,22},{5,23},{6,20},{7,21},{8,26},{9,... | collective-permute-start | bytes 245768 | tf_op jit(solution)/shard_map/ppermute | solution.py:262
  77.2 0.1 collective-permute-start.24
  77.4 2.6 %collective-permute-done.23.refs_6_ = bf16[16,2560]{1,0:T(8,128)(2,1)S(1)} collective-permute-done((bf16[16,2560]{1,0:T(8,128)(2,1)S(1)}, bf16[16,2560]{1,0:T(8,128)(2,1)S(1)}, u32[]{:S(2)}, u32[]{:S(2)}) %collective-permute-start.23) | collective-permute-done | bytes 81952 | tf_op jit(solution)/shard_map/ppermute | solution.py:262
  80.0 3.5 %collective-permute-done.24.refs_7_ = bf16[16,2560]{1,0:T(8,128)(2,1)S(1)} collective-permute-done((bf16[16,2560]{1,0:T(8,128)(2,1)S(1)}, bf16[16,2560]{1,0:T(8,128)(2,1)S(1)}, u32[]{:S(2)}, u32[]{:S(2)}) %collective-permute-start.24) | collective-permute-done | bytes 81952 | tf_op jit(solution)/shard_map/ppermute | solution.py:262
  83.4 0.2 shard_map.128
  83.7 0.1 collective-permute-start.25
  83.7 1.3 %collective-permute-done.25.more_ref = bf16[32,2176]{1,0:T(8,128)(2,1)S(1)} collective-permute-done((bf16[32,2176]{1,0:T(8,128)(2,1)S(1)}, bf16[32,2176]{1,0:T(8,128)(2,1)S(1)}, u32[]{:S(2)}, u32[]{:S(2)}) %collective-permute-start.25) | collective-permute-done | bytes 139296 | tf_op jit(solution)/shard_map/ppermute | solution.py:262
  85.1 2.7 %collective-permute-start.26 = (bf16[32,2176]{1,0:T(8,128)(2,1)S(1)}, bf16[32,2176]{1,0:T(8,128)(2,1)S(1)}, u32[]{:S(2)}, u32[]{:S(2)}) collective-permute-start(bf16[32,2176]{1,0:T(8,128)(2,1)S(1)} %shard_map.129), channel_id=1, source_target_pairs={{0,4},{1,5},{2,6},{3,7},{4,0},{5,1},{6,2},{7,3},{8,12},{9,13},{10,... | collective-permute-start | bytes 417800 | tf_op jit(solution)/shard_map/ppermute | solution.py:262
  87.8 0.2 shard_map.127
  88.1 0.1 collective-permute-start.17
  88.1 6.5 %collective-permute-done.26.far_ref = bf16[32,2176]{1,0:T(8,128)(2,1)S(1)} collective-permute-done((bf16[32,2176]{1,0:T(8,128)(2,1)S(1)}, bf16[32,2176]{1,0:T(8,128)(2,1)S(1)}, u32[]{:S(2)}, u32[]{:S(2)}) %collective-permute-start.26) | collective-permute-done | bytes 139296 | tf_op jit(solution)/shard_map/ppermute | solution.py:262
  94.6 0.7 shard_map.130
  (17 shorter events, 0.1 us)
Async XLA Ops:
  1.7 16.4 %collective-permute-start.8 = (bf16[32,4224]{1,0:T(8,128)(2,1)S(1)}, bf16[32,4224]{1,0:T(8,128)(2,1)S(1)}, u32[]{:S(2)}, u32[]{:S(2)}) collective-permute-start(bf16[32,4224]{1,0:T(8,128)(2,1)S(1)} %shard_map.122.first_ref), channel_id=1, source_target_pairs={{0,4},{1,5},{2,6},{3,7},{4,0},{5,1},{6,2},{7,3},{8,12},{9,13},{10,... | collective-permute-start | bytes 811016 | tf_op jit(solution)/shard_map/ppermute | solution.py:262
  5.8 12.3 %collective-permute-start = (bf16[32,4224]{1,0:T(8,128)(2,1)S(1)}, bf16[32,4224]{1,0:T(8,128)(2,1)S(1)}, u32[]{:S(2)}, u32[]{:S(2)}) collective-permute-start(bf16[32,4224]{1,0:T(8,128)(2,1)S(1)} %shard_map.122.first_ref), channel_id=1, source_target_pairs={{0,8},{1,9},{2,10},{3,11},{4,12},{5,13},{6,14},{7,15},{8,0},{9,1},... | collective-permute-start | bytes 811016 | tf_op jit(solution)/shard_map/ppermute | solution.py:262
  18.1 5.8 %collective-permute-start.9 = (bf16[32,4224]{1,0:T(8,128)(2,1)S(1)}, bf16[32,4224]{1,0:T(8,128)(2,1)S(1)}, u32[]{:S(2)}, u32[]{:S(2)}) collective-permute-start(bf16[32,4224]{1,0:T(8,128)(2,1)S(1)} %collective-permute-done.8.first_ref), channel_id=1, source_target_pairs={{0,8},{1,9},{2,10},{3,11},{4,12},{5,13},{6,14},{7,15},{8,0},{9,1},... | collective-permute-start | bytes 811016 | tf_op jit(solution)/shard_map/ppermute | solution.py:262
  18.8 7.3 %collective-permute-start.1 = (bf16[16,4096]{1,0:T(8,128)(2,1)S(1)}, bf16[16,4096]{1,0:T(8,128)(2,1)S(1)}, u32[]{:S(2)}, u32[]{:S(2)}) collective-permute-start(bf16[16,4096]{1,0:T(8,128)(2,1)S(1)} %get-tuple-element.44), channel_id=1, source_target_pairs={{0,1},{1,0},{2,3},{3,2},{4,5},{5,4},{6,7},{7,6},{8,9},{9,8},{10,11... | collective-permute-start | bytes 393224 | tf_op jit(solution)/shard_map/ppermute | solution.py:262
  20.4 7.4 %collective-permute-start.2 = (bf16[16,4096]{1,0:T(8,128)(2,1)S(1)}, bf16[16,4096]{1,0:T(8,128)(2,1)S(1)}, u32[]{:S(2)}, u32[]{:S(2)}) collective-permute-start(bf16[16,4096]{1,0:T(8,128)(2,1)S(1)} %get-tuple-element.45), channel_id=1, source_target_pairs={{0,2},{1,3},{2,0},{3,1},{4,6},{5,7},{6,4},{7,5},{8,10},{9,11},{10,... | collective-permute-start | bytes 393224 | tf_op jit(solution)/shard_map/ppermute | solution.py:262
  21.1 7.9 %collective-permute-start.3 = (bf16[16,4096]{1,0:T(8,128)(2,1)S(1)}, bf16[16,4096]{1,0:T(8,128)(2,1)S(1)}, u32[]{:S(2)}, u32[]{:S(2)}) collective-permute-start(bf16[16,4096]{1,0:T(8,128)(2,1)S(1)} %get-tuple-element.46), channel_id=1, source_target_pairs={{0,3},{1,2},{2,1},{3,0},{4,7},{5,6},{6,5},{7,4},{8,11},{9,10},{10,... | collective-permute-start | bytes 393224 | tf_op jit(solution)/shard_map/ppermute | solution.py:262
  22.4 8.2 %collective-permute-start.4 = (bf16[16,4096]{1,0:T(8,128)(2,1)S(1)}, bf16[16,4096]{1,0:T(8,128)(2,1)S(1)}, u32[]{:S(2)}, u32[]{:S(2)}) collective-permute-start(bf16[16,4096]{1,0:T(8,128)(2,1)S(1)} %get-tuple-element.47), channel_id=1, source_target_pairs={{0,16},{1,17},{2,18},{3,19},{4,20},{5,21},{6,22},{7,23},{8,24},{9,... | collective-permute-start | bytes 393224 | tf_op jit(solution)/shard_map/ppermute | solution.py:262
  23.9 13.3 %collective-permute-start.5 = (bf16[16,4096]{1,0:T(8,128)(2,1)S(1)}, bf16[16,4096]{1,0:T(8,128)(2,1)S(1)}, u32[]{:S(2)}, u32[]{:S(2)}) collective-permute-start(bf16[16,4096]{1,0:T(8,128)(2,1)S(1)} %get-tuple-element.48), channel_id=1, source_target_pairs={{0,17},{1,16},{2,19},{3,18},{4,21},{5,20},{6,23},{7,22},{8,25},{9,... | collective-permute-start | bytes 393224 | tf_op jit(solution)/shard_map/ppermute | solution.py:262
  26.1 12.3 %collective-permute-start.6 = (bf16[16,4096]{1,0:T(8,128)(2,1)S(1)}, bf16[16,4096]{1,0:T(8,128)(2,1)S(1)}, u32[]{:S(2)}, u32[]{:S(2)}) collective-permute-start(bf16[16,4096]{1,0:T(8,128)(2,1)S(1)} %get-tuple-element.49), channel_id=1, source_target_pairs={{0,18},{1,19},{2,16},{3,17},{4,22},{5,23},{6,20},{7,21},{8,26},{9,... | collective-permute-start | bytes 393224 | tf_op jit(solution)/shard_map/ppermute | solution.py:262
  27.8 12.2 %collective-permute-start.7 = (bf16[16,4096]{1,0:T(8,128)(2,1)S(1)}, bf16[16,4096]{1,0:T(8,128)(2,1)S(1)}, u32[]{:S(2)}, u32[]{:S(2)}) collective-permute-start(bf16[16,4096]{1,0:T(8,128)(2,1)S(1)} %get-tuple-element.50), channel_id=1, source_target_pairs={{0,19},{1,18},{2,17},{3,16},{4,23},{5,22},{6,21},{7,20},{8,27},{9,... | collective-permute-start | bytes 393224 | tf_op jit(solution)/shard_map/ppermute | solution.py:262
  29.0 12.4 %collective-permute-start.10 = (bf16[16,4096]{1,0:T(8,128)(2,1)S(1)}, bf16[16,4096]{1,0:T(8,128)(2,1)S(1)}, u32[]{:S(2)}, u32[]{:S(2)}) collective-permute-start(bf16[16,4096]{1,0:T(8,128)(2,1)S(1)} %get-tuple-element.52), channel_id=1, source_target_pairs={{0,1},{1,0},{2,3},{3,2},{4,5},{5,4},{6,7},{7,6},{8,9},{9,8},{10,11... | collective-permute-start | bytes 393224 | tf_op jit(solution)/shard_map/ppermute | solution.py:262
  30.5 13.8 %collective-permute-start.11 = (bf16[16,4096]{1,0:T(8,128)(2,1)S(1)}, bf16[16,4096]{1,0:T(8,128)(2,1)S(1)}, u32[]{:S(2)}, u32[]{:S(2)}) collective-permute-start(bf16[16,4096]{1,0:T(8,128)(2,1)S(1)} %get-tuple-element.53), channel_id=1, source_target_pairs={{0,2},{1,3},{2,0},{3,1},{4,6},{5,7},{6,4},{7,5},{8,10},{9,11},{10,... | collective-permute-start | bytes 393224 | tf_op jit(solution)/shard_map/ppermute | solution.py:262
  37.3 14.4 %collective-permute-start.12 = (bf16[16,4096]{1,0:T(8,128)(2,1)S(1)}, bf16[16,4096]{1,0:T(8,128)(2,1)S(1)}, u32[]{:S(2)}, u32[]{:S(2)}) collective-permute-start(bf16[16,4096]{1,0:T(8,128)(2,1)S(1)} %get-tuple-element.54), channel_id=1, source_target_pairs={{0,3},{1,2},{2,1},{3,0},{4,7},{5,6},{6,5},{7,4},{8,11},{9,10},{10,... | collective-permute-start | bytes 393224 | tf_op jit(solution)/shard_map/ppermute | solution.py:262
  38.4 13.3 %collective-permute-start.13 = (bf16[16,4096]{1,0:T(8,128)(2,1)S(1)}, bf16[16,4096]{1,0:T(8,128)(2,1)S(1)}, u32[]{:S(2)}, u32[]{:S(2)}) collective-permute-start(bf16[16,4096]{1,0:T(8,128)(2,1)S(1)} %get-tuple-element.55), channel_id=1, source_target_pairs={{0,16},{1,17},{2,18},{3,19},{4,20},{5,21},{6,22},{7,23},{8,24},{9,... | collective-permute-start | bytes 393224 | tf_op jit(solution)/shard_map/ppermute | solution.py:262
  40.0 11.8 %collective-permute-start.14 = (bf16[16,4096]{1,0:T(8,128)(2,1)S(1)}, bf16[16,4096]{1,0:T(8,128)(2,1)S(1)}, u32[]{:S(2)}, u32[]{:S(2)}) collective-permute-start(bf16[16,4096]{1,0:T(8,128)(2,1)S(1)} %get-tuple-element.56), channel_id=1, source_target_pairs={{0,17},{1,16},{2,19},{3,18},{4,21},{5,20},{6,23},{7,22},{8,25},{9,... | collective-permute-start | bytes 393224 | tf_op jit(solution)/shard_map/ppermute | solution.py:262
  41.4 10.3 %collective-permute-start.15 = (bf16[16,4096]{1,0:T(8,128)(2,1)S(1)}, bf16[16,4096]{1,0:T(8,128)(2,1)S(1)}, u32[]{:S(2)}, u32[]{:S(2)}) collective-permute-start(bf16[16,4096]{1,0:T(8,128)(2,1)S(1)} %get-tuple-element.57), channel_id=1, source_target_pairs={{0,18},{1,19},{2,16},{3,17},{4,22},{5,23},{6,20},{7,21},{8,26},{9,... | collective-permute-start | bytes 393224 | tf_op jit(solution)/shard_map/ppermute | solution.py:262
  44.4 7.4 %collective-permute-start.16 = (bf16[16,4096]{1,0:T(8,128)(2,1)S(1)}, bf16[16,4096]{1,0:T(8,128)(2,1)S(1)}, u32[]{:S(2)}, u32[]{:S(2)}) collective-permute-start(bf16[16,4096]{1,0:T(8,128)(2,1)S(1)} %get-tuple-element.58), channel_id=1, source_target_pairs={{0,19},{1,18},{2,17},{3,16},{4,23},{5,22},{6,21},{7,20},{8,27},{9,... | collective-permute-start | bytes 393224 | tf_op jit(solution)/shard_map/ppermute | solution.py:262
  59.2 28.6 %all-to-all-start = ((bf16[8,16,2560]{2,1,0:T(8,128)(2,1)}), bf16[8,16,2560]{2,1,0:T(8,128)(2,1)S(1)}, u32[]{:S(2)}, u32[]{:S(2)}) async-start(bf16[8,16,2560]{2,1,0:T(8,128)(2,1)} %get-tuple-element.65), calls=%async_computation | async-start | bytes 1310720 | tf_op jit(solution)/shard_map/all_to_all | solution.py:325
  64.3 10.3 %collective-permute-start.18 = (bf16[16,2560]{1,0:T(8,128)(2,1)S(1)}, bf16[16,2560]{1,0:T(8,128)(2,1)S(1)}, u32[]{:S(2)}, u32[]{:S(2)}) collective-permute-start(bf16[16,2560]{1,0:T(8,128)(2,1)S(1)} %get-tuple-element.71), channel_id=1, source_target_pairs={{0,1},{1,0},{2,3},{3,2},{4,5},{5,4},{6,7},{7,6},{8,9},{9,8},{10,11... | collective-permute-start | bytes 245768 | tf_op jit(solution)/shard_map/ppermute | solution.py:262
  66.3 10.9 %collective-permute-start.19 = (bf16[16,2560]{1,0:T(8,128)(2,1)S(1)}, bf16[16,2560]{1,0:T(8,128)(2,1)S(1)}, u32[]{:S(2)}, u32[]{:S(2)}) collective-permute-start(bf16[16,2560]{1,0:T(8,128)(2,1)S(1)} %get-tuple-element.72), channel_id=1, source_target_pairs={{0,2},{1,3},{2,0},{3,1},{4,6},{5,7},{6,4},{7,5},{8,10},{9,11},{10,... | collective-permute-start | bytes 245768 | tf_op jit(solution)/shard_map/ppermute | solution.py:262
  67.8 9.6 %collective-permute-start.20 = (bf16[16,2560]{1,0:T(8,128)(2,1)S(1)}, bf16[16,2560]{1,0:T(8,128)(2,1)S(1)}, u32[]{:S(2)}, u32[]{:S(2)}) collective-permute-start(bf16[16,2560]{1,0:T(8,128)(2,1)S(1)} %get-tuple-element.73), channel_id=1, source_target_pairs={{0,3},{1,2},{2,1},{3,0},{4,7},{5,6},{6,5},{7,4},{8,11},{9,10},{10,... | collective-permute-start | bytes 245768 | tf_op jit(solution)/shard_map/ppermute | solution.py:262
  67.8 9.6 %collective-permute-start.21 = (bf16[16,2560]{1,0:T(8,128)(2,1)S(1)}, bf16[16,2560]{1,0:T(8,128)(2,1)S(1)}, u32[]{:S(2)}, u32[]{:S(2)}) collective-permute-start(bf16[16,2560]{1,0:T(8,128)(2,1)S(1)} %get-tuple-element.74), channel_id=1, source_target_pairs={{0,16},{1,17},{2,18},{3,19},{4,20},{5,21},{6,22},{7,23},{8,24},{9,... | collective-permute-start | bytes 245768 | tf_op jit(solution)/shard_map/ppermute | solution.py:262
  69.8 7.6 %collective-permute-start.22 = (bf16[16,2560]{1,0:T(8,128)(2,1)S(1)}, bf16[16,2560]{1,0:T(8,128)(2,1)S(1)}, u32[]{:S(2)}, u32[]{:S(2)}) collective-permute-start(bf16[16,2560]{1,0:T(8,128)(2,1)S(1)} %get-tuple-element.75), channel_id=1, source_target_pairs={{0,17},{1,16},{2,19},{3,18},{4,21},{5,20},{6,23},{7,22},{8,25},{9,... | collective-permute-start | bytes 245768 | tf_op jit(solution)/shard_map/ppermute | solution.py:262
  74.6 5.3 %collective-permute-start.23 = (bf16[16,2560]{1,0:T(8,128)(2,1)S(1)}, bf16[16,2560]{1,0:T(8,128)(2,1)S(1)}, u32[]{:S(2)}, u32[]{:S(2)}) collective-permute-start(bf16[16,2560]{1,0:T(8,128)(2,1)S(1)} %get-tuple-element.76), channel_id=1, source_target_pairs={{0,18},{1,19},{2,16},{3,17},{4,22},{5,23},{6,20},{7,21},{8,26},{9,... | collective-permute-start | bytes 245768 | tf_op jit(solution)/shard_map/ppermute | solution.py:262
  77.2 6.2 %collective-permute-start.24 = (bf16[16,2560]{1,0:T(8,128)(2,1)S(1)}, bf16[16,2560]{1,0:T(8,128)(2,1)S(1)}, u32[]{:S(2)}, u32[]{:S(2)}) collective-permute-start(bf16[16,2560]{1,0:T(8,128)(2,1)S(1)} %get-tuple-element.77), channel_id=1, source_target_pairs={{0,19},{1,18},{2,17},{3,16},{4,23},{5,22},{6,21},{7,20},{8,27},{9,... | collective-permute-start | bytes 245768 | tf_op jit(solution)/shard_map/ppermute | solution.py:262
  83.7 1.4 %collective-permute-start.25 = (bf16[32,2176]{1,0:T(8,128)(2,1)S(1)}, bf16[32,2176]{1,0:T(8,128)(2,1)S(1)}, u32[]{:S(2)}, u32[]{:S(2)}) collective-permute-start(bf16[32,2176]{1,0:T(8,128)(2,1)S(1)} %get-tuple-element.79), channel_id=1, source_target_pairs={{0,8},{1,9},{2,10},{3,11},{4,12},{5,13},{6,14},{7,15},{8,0},{9,1},... | collective-permute-start | bytes 417800 | tf_op jit(solution)/shard_map/ppermute | solution.py:262
  85.1 9.5 %collective-permute-start.26 = (bf16[32,2176]{1,0:T(8,128)(2,1)S(1)}, bf16[32,2176]{1,0:T(8,128)(2,1)S(1)}, u32[]{:S(2)}, u32[]{:S(2)}) collective-permute-start(bf16[32,2176]{1,0:T(8,128)(2,1)S(1)} %shard_map.129), channel_id=1, source_target_pairs={{0,4},{1,5},{2,6},{3,7},{4,0},{5,1},{6,2},{7,3},{8,12},{9,13},{10,... | collective-permute-start | bytes 417800 | tf_op jit(solution)/shard_map/ppermute | solution.py:262
  88.1 6.6 %collective-permute-start.17 = (bf16[32,2176]{1,0:T(8,128)(2,1)S(1)}, bf16[32,2176]{1,0:T(8,128)(2,1)S(1)}, u32[]{:S(2)}, u32[]{:S(2)}) collective-permute-start(bf16[32,2176]{1,0:T(8,128)(2,1)S(1)} %get-tuple-element.67), channel_id=1, source_target_pairs={{0,8},{1,9},{2,10},{3,11},{4,12},{5,13},{6,14},{7,15},{8,0},{9,1},... | collective-permute-start | bytes 417800 | tf_op jit(solution)/shard_map/ppermute | solution.py:262
